TPU v7x, 32 devices: a whole 2x2x4 slice. The times are simulated.
32 devices in a mesh: groups: 2 (over y), chan: 4 (over z), blk: 2 (over x), dir: 2 (over core).
Axes of the slice: x: 2, y: 2, z: 4, core: 2. Of those that a mesh axis runs over, the one named last changes fastest.
Arguments:
- visibilities: float32 [16, 8, 2, 512], P('groups', 'chan', 'blk'), parts along dimension 0, may hold values from -6 to 6
- antenna_pairs: int32 [2, 2, 512], P(None, 'blk'), may hold values from 0 to 511, as said below
- valid_mask: int32 [2, 1024], P('blk', 'groups'), parts along dimension 1, may hold values 0 or 1
- station_positions: float32 [2, 512], replicated, may hold values from -20 to 20
- source_offsets: float32 [2, 256], replicated, may hold values from -0.3 to 0.3
- brightness: float32 [4, 256], replicated, may hold values from -0.375 to 0.375
- source_cluster: int32 [256], replicated, may hold values from 0 to 15
- jones_gains: float32 [16, 16, 512], P('dir', 'groups'), parts along dimension 1, may hold values from -3 to 3
Outputs:
- residuals: float32 [16, 8, 2, 512], P('groups', None, 'blk', 'chan'), parts along dimension 0
- solved_gains: float32 [16, 16, 512], P('dir', 'groups'), parts along dimension 1
There are 2 independent parts, one for each index of `groups`. A program takes and returns all parts, laid end to end along the dimension named above; an argument that names none is the same for every part. Nothing has to cross between parts.
Inputs may be any that keep to these rules, and one draw needn't show every extreme that they name: `antenna_pairs`: the two stations of a baseline differ.
All inputs are finite; a program needn't handle non-finite values. No bound on the sum of `valid_mask` on one device may be relied on, other than what follows from the above.
Results may differ from a plain program's by a relative error of at most 0.0003.
Values sent between devices are 32-bit elements; how exact they have to be, the bound alone decides.
No kernel may reach another device: no remote copies, remote signals or barrier semaphores. Data moves between devices by JAX's collectives and lax.ppermute only.
A program may use at most 64 MiB of HBM per device.

v0:
```python
import math

import jax
import jax.numpy as jnp
from jax import lax
from jax.sharding import PartitionSpec as P

ITERS = 2


TWO_PI = 2.0 * math.pi
STEP_SIZE = 0.3
EPSILON = 1e-06
HIGHEST = lax.Precision.HIGHEST


def jones_product(former, latter):
    real_list = []
    imag_list = []
    for row_number in (0, 1):
        for column in (0, 1):
            real_list.append(
                former[2 * row_number] * latter[column]
                - former[4 + 2 * row_number] * latter[4 + column]
                + former[2 * row_number + 1] * latter[2 + column]
                - former[5 + 2 * row_number] * latter[6 + column]
            )
            imag_list.append(
                former[2 * row_number] * latter[4 + column]
                + former[4 + 2 * row_number] * latter[column]
                + former[2 * row_number + 1] * latter[6 + column]
                + former[5 + 2 * row_number] * latter[2 + column]
            )
    return jnp.stack(real_list + imag_list)


def adjoint(matrix):
    return jnp.stack(
        [matrix[0], matrix[2], matrix[1], matrix[3], -matrix[4], -matrix[6], -matrix[5], -matrix[7]]
    )


def source_table(brightness, source_cluster, direction_ids):
    member = (source_cluster[None, :] == direction_ids[:, None]).astype(jnp.float32)
    return (brightness[:, None, :] * member[None, :, :]).reshape(
        4 * direction_ids.shape[0], brightness.shape[1]
    )


def coherency(bright_table, geometry, scales):
    phase_grid = (TWO_PI * scales)[None, :, None] * geometry[:, None, :]
    phases_flat = phase_grid.reshape(geometry.shape[0], -1)
    real_block = jnp.dot(bright_table, jnp.cos(phases_flat), precision=HIGHEST)
    imag_block = -jnp.dot(bright_table, jnp.sin(phases_flat), precision=HIGHEST)
    dir_count = bright_table.shape[0] // 4
    return jnp.concatenate([real_block, imag_block], axis=0).reshape(
        8, dir_count, scales.shape[0], geometry.shape[1]
    )


def per_device(
    visibilities,
    antenna_pairs,
    valid_mask,
    station_positions,
    source_offsets,
    brightness,
    source_cluster,
    jones_gains,
):
    relay_count = lax.axis_size("chan")
    base_count = antenna_pairs.shape[2] // relay_count
    station_count = station_positions.shape[1]
    offset = lax.axis_index("chan") * base_count
    own_pairs = lax.dynamic_slice_in_dim(antenna_pairs[:, 0], offset, base_count, 1)
    first_station = own_pairs[0]
    second_station = own_pairs[1]
    weight_row = lax.dynamic_slice_in_dim(valid_mask[0], offset, base_count, 0).astype(jnp.float32)
    regrouped = lax.all_to_all(visibilities, "chan", split_axis=3, concat_axis=1, tiled=True)[
        :, :, 0, :
    ]
    total_channels = regrouped.shape[1]
    own_directions = jones_gains.shape[0]
    channel_ids = jnp.arange(total_channels)
    gains_now = jones_gains
    direction_ids = lax.axis_index("dir") * own_directions + jnp.arange(own_directions)
    local_channels = regrouped.shape[1]
    scales = 1.0 + 0.5 * channel_ids.astype(jnp.float32) / total_channels
    u_coord = station_positions[0][first_station] - station_positions[0][second_station]
    v_coord = station_positions[1][first_station] - station_positions[1][second_station]
    geometry = (
        source_offsets[0][:, None] * u_coord[None, :]
        + source_offsets[1][:, None] * v_coord[None, :]
    )
    bright_table = source_table(brightness, source_cluster, direction_ids)
    group_size = math.gcd(local_channels, max(1, 2048 // base_count))
    group_count = local_channels // group_size
    scale_groups = scales.reshape(group_count, group_size)
    onehot_first = (first_station[:, None] == jnp.arange(station_count)[None, :]).astype(
        jnp.float32
    )
    onehot_second = (second_station[:, None] == jnp.arange(station_count)[None, :]).astype(
        jnp.float32
    )

    def station_gains(gains_current):
        gain_first = jnp.take(gains_current, first_station, axis=2).transpose(1, 0, 2)[
            :, :, None, :
        ]
        gain_second = jnp.take(gains_current, second_station, axis=2).transpose(1, 0, 2)[
            :, :, None, :
        ]
        return (gain_first, gain_second)

    def residual_of(gains_current):
        gain_first, gain_second = station_gains(gains_current)

        def residual_one_group(scale_group):
            coherent = coherency(bright_table, geometry, scale_group)
            return jnp.sum(
                jones_product(jones_product(gain_first, coherent), adjoint(gain_second)), axis=1
            )

        partial_model = jnp.moveaxis(lax.map(residual_one_group, scale_groups), 0, 1).reshape(
            8, local_channels, base_count
        )
        model_vis = lax.psum(partial_model, "dir")
        return weight_row * (regrouped - model_vis)

    for iteration in range(ITERS):
        residual_now = residual_of(gains_now)
        updated_gain_first, updated_gain_second = station_gains(gains_now)
        resid_groups = jnp.moveaxis(
            residual_now.reshape(8, group_count, group_size, base_count), 1, 0
        )
        dir_count = gains_now.shape[0]

        def updated_one_group(running, inputs):
            scale_group, resid_group = inputs
            coherent = coherency(bright_table, geometry, scale_group)
            toward_second = jones_product(updated_gain_second, adjoint(coherent))
            toward_first = jones_product(updated_gain_first, coherent)
            grad_first = jnp.sum(jones_product(resid_group[:, None], toward_second), axis=2)
            grad_second = jnp.sum(
                jones_product(adjoint(resid_group)[:, None], toward_first), axis=2
            )
            curv_first = jnp.sum(toward_second * toward_second, axis=(0, 2))
            curv_second = jnp.sum(toward_first * toward_first, axis=(0, 2))
            return (
                (
                    running[0] + grad_first,
                    running[1] + grad_second,
                    running[2] + curv_first,
                    running[3] + curv_second,
                ),
                None,
            )

        zero_sums = (
            jnp.zeros((8, dir_count, base_count), jnp.float32),
            jnp.zeros((8, dir_count, base_count), jnp.float32),
            jnp.zeros((dir_count, base_count), jnp.float32),
            jnp.zeros((dir_count, base_count), jnp.float32),
        )
        totals, ignored = lax.scan(updated_one_group, zero_sums, (scale_groups, resid_groups))
        grad_station = jnp.einsum(
            "cdb,bs->dcs", totals[0], onehot_first, precision=HIGHEST
        ) + jnp.einsum("cdb,bs->dcs", totals[1], onehot_second, precision=HIGHEST)
        curv_station = jnp.dot(weight_row * totals[2], onehot_first, precision=HIGHEST) + jnp.dot(
            weight_row * totals[3], onehot_second, precision=HIGHEST
        )
        grad_station, curv_station = lax.psum((grad_station, curv_station), ("chan", "blk"))
        gains_now = gains_now + STEP_SIZE * grad_station / (curv_station[:, None, :] + EPSILON)
    residual_now = residual_of(gains_now)
    return (residual_now[:, :, None, :], gains_now)


def solution(mesh):
    in_specs = (
        P("groups", "chan", "blk", None),
        P(None, "blk", None),
        P("blk", "groups"),
        P(),
        P(),
        P(),
        P(),
        P("dir", "groups", None),
    )
    out_specs = (P("groups", None, "blk", "chan"), P("dir", "groups", None))
    return jax.shard_map(
        per_device, mesh=mesh, in_specs=in_specs, out_specs=out_specs, check_vma=False
    )
```

profile of v0, /device:TPU:0, one launch (start us, length us, event | category | flops | bytes accessed | tf_op | source)
XLA Modules:
  0.0 311.1 jit_solution(10712981869981205140)
XLA Ops:
  8.2 1.4 reshape.6361
  9.6 6.3 %all-to-all-start = ((f32[4,1,2048]{2,1,0:T(1,128)}), f32[4,1,2048]{2,1,0:T(1,128)S(1)}, u32[]{:S(2)}, u32[]{:S(2)}) async-start(f32[4,1,2048]{2,1,0:T(1,128)} %reshape.6361), calls=%async_computation | async-start | bytes 65536 | tf_op jit(solution)/shard_map/all_to_all | solution.py:79
  18.0 1.3 gather_fusion.3
  19.3 1.3 gather_fusion.1
  20.6 1.3 gather_fusion
  21.9 1.4 gather_fusion.2
  24.4 3.7 %multiply_cosine_fusion = (f32[256,8,128]{2,1,0:T(8,128)S(1)}, f32[256,8,128]{2,1,0:T(8,128)S(1)}) fusion(f32[256,128]{1,0:T(8,128)S(1)} %multiply_add_fusion, f32[8]{0:T(128)S(1)} %add_multiply_fusion), kind=kLoop, calls=%fused_computation.11 | loop fusion | flops 262144 | bytes 2228256 | tf_op jit(solution)/shard_map/while/body/eval_jaxpr/cos | solution.py:53
  31.3 1.6 gather_fusion.4
  33.0 2.0 fusion.55
  35.0 1.2 copy.387
  36.2 1.2 copy.390
  39.1 2.0 fusion.54
  41.1 1.2 copy.391
  42.3 1.2 copy.394
  46.2 37.6 %psum.51 = f32[8,512]{1,0:T(8,128)S(1)} all-reduce(f32[8,512]{1,0:T(8,128)S(1)} %convolution_add_fusion.3), channel_id=1, replica_groups=mesh['groups'=2,'chan'=4,'blk'=2,'dir'=2] {'chan','blk'}, use_global_device_ids=true, to_apply=%region_7.9 | all-reduce | flops 4096 | bytes 32768 | tf_op jit(solution)/shard_map/psum | solution.py:172
  83.7 3.6 %psum.49 = f32[8,8,128]{2,1,0:T(8,128)S(1)} all-reduce(f32[8,8,128]{2,1,0:T(8,128)S(1)} %reduce_sum.110), channel_id=1, replica_groups=mesh['groups'=2,'chan'=4,'blk'=2,'dir'=2] {'dir'}, use_global_device_ids=true, to_apply=%region_1.3 | all-reduce | flops 8192 | bytes 65536 | tf_op jit(solution)/shard_map/psum | solution.py:127
  92.0 67.1 %all-reduce.3.cloned.1.call-done = f32[8,8,512]{2,0,1:T(8,128)} async-done(((f32[8,8,512]{2,0,1:T(8,128)}), f32[8,8,512]{2,0,1:T(8,128)}) %all-reduce.3.cloned.1.call-update) | async-done | bytes 131088 | tf_op jit(solution)/shard_map/psum | solution.py:172
  162.9 2.1 fusion.53
  165.0 1.2 copy.407
  166.3 1.2 copy.410
  168.1 1.2 copy.408
  172.3 2.2 fusion.52
  174.4 1.2 copy.411
  175.7 1.2 copy.414
  176.9 1.2 copy.413
  181.1 35.4 %psum.54 = f32[8,512]{1,0:T(8,128)S(1)} all-reduce(f32[8,512]{1,0:T(8,128)S(1)} %convolution_add_fusion.2), channel_id=1, replica_groups=mesh['groups'=2,'chan'=4,'blk'=2,'dir'=2] {'chan','blk'}, use_global_device_ids=true, to_apply=%region_15.17 | all-reduce | flops 4096 | bytes 32768 | tf_op jit(solution)/shard_map/psum | solution.py:172
  216.8 3.7 %psum.52 = f32[8,8,128]{2,1,0:T(8,128)S(1)} all-reduce(f32[8,8,128]{2,1,0:T(8,128)S(1)} %reduce_sum.115), channel_id=1, replica_groups=mesh['groups'=2,'chan'=4,'blk'=2,'dir'=2] {'dir'}, use_global_device_ids=true, to_apply=%region_9.11 | all-reduce | flops 8192 | bytes 65536 | tf_op jit(solution)/shard_map/psum | solution.py:127
  222.3 67.1 %all-reduce.5.cloned.1.call-done = f32[8,8,512]{2,0,1:T(8,128)} async-done(((f32[8,8,512]{2,0,1:T(8,128)}), f32[8,8,512]{2,0,1:T(8,128)}) %all-reduce.5.cloned.1.call-update) | async-done | bytes 131088 | tf_op jit(solution)/shard_map/psum | solution.py:172
  294.1 2.0 fusion.51
  296.1 1.2 copy.423
  297.3 1.2 copy.426
  300.2 3.4 %psum.55 = f32[8,8,128]{2,1,0:T(8,128)S(1)} all-reduce(f32[8,8,128]{2,1,0:T(8,128)S(1)} %reduce_sum.120), channel_id=1, replica_groups=mesh['groups'=2,'chan'=4,'blk'=2,'dir'=2] {'dir'}, use_global_device_ids=true, to_apply=%region_17.19 | all-reduce | flops 8192 | bytes 65536 | tf_op jit(solution)/shard_map/psum | solution.py:127
  (260 shorter events, 34.7 us)
Async XLA Ops:
  7.2 16.9 %copy-start.32 = (f32[2,256]{1,0:T(2,128)S(1)}, f32[2,256]{1,0:T(2,128)}, u32[]{:S(2)}) copy-start(f32[2,256]{1,0:T(2,128)} %param.14) | copy-start | bytes 6148
  7.2 17.0 %copy-start.37 = (s32[256]{0:T(256)S(1)}, s32[256]{0:T(256)}, u32[]{:S(2)}) copy-start(s32[256]{0:T(256)} %param.16) | copy-start | bytes 3076
  9.6 77.8 %all-to-all-start = ((f32[4,1,2048]{2,1,0:T(1,128)}), f32[4,1,2048]{2,1,0:T(1,128)S(1)}, u32[]{:S(2)}, u32[]{:S(2)}) async-start(f32[4,1,2048]{2,1,0:T(1,128)} %reshape.6361), calls=%async_computation | async-start | bytes 65536 | tf_op jit(solution)/shard_map/all_to_all | solution.py:79
  15.9 143.2 %all-reduce.3.cloned.1.call-start = ((), (), s32[]{:S(2)}) async-start(), calls=%async_computation.1 | async-start | bytes 262144 | tf_op jit(solution)/shard_map/psum | solution.py:172
  16.6 74.1 %copy-start.35 = (s32[128]{0:T(128)}, s32[128]{0:T(128)S(1)}, u32[]{:S(2)}) copy-start(s32[128]{0:T(128)S(1)} %get-tuple-element.223) | copy-start | bytes 1540
  16.6 145.9 %copy-start.23 = (pred[128]{0:T(512)(128)(4,1)}, pred[128]{0:T(512)(128)(4,1)S(1)}, u32[]{:S(2)}) copy-start(pred[128]{0:T(512)(128)(4,1)S(1)} %get-tuple-element.222) | copy-start | bytes 388
  17.3 73.7 %copy-start.33 = (s32[1,1,128]{2,1,0:T(1,128)}, s32[1,1,128]{2,1,0:T(1,128)S(1)}, u32[]{:S(2)}) copy-start(s32[1,1,128]{2,1,0:T(1,128)S(1)} %get-tuple-element.225) | copy-start | bytes 1540
  19.3 8.7 %copy-start.22 = (f32[4,256]{1,0:T(4,128)S(1)}, f32[4,256]{1,0:T(4,128)}, u32[]{:S(2)}) copy-start(f32[4,256]{1,0:T(4,128)} %param.15) | copy-start | bytes 12292
  24.0 65.6 %copy-start.27 = (f32[128]{0:T(128)}, f32[128]{0:T(128)S(1)}, u32[]{:S(2)}) copy-start(f32[128]{0:T(128)S(1)} %fusion.46) | copy-start | bytes 1540
  24.0 138.7 %copy-start.30 = (pred[128]{0:T(512)(128)(4,1)}, pred[128]{0:T(512)(128)(4,1)S(1)}, u32[]{:S(2)}) copy-start(pred[128]{0:T(512)(128)(4,1)S(1)} %compare_and_fusion.1) | copy-start | bytes 388
  24.1 137.6 %copy-start.25 = (s32[1024]{0:T(1024)}, s32[1024]{0:T(1024)S(1)}, u32[]{:S(2)}) copy-start(s32[1024]{0:T(1024)S(1)} %pad_clamp_fusion.3) | copy-start | bytes 12292
  24.1 136.8 %copy-start.26 = (s32[1024]{0:T(1024)}, s32[1024]{0:T(1024)S(1)}, u32[]{:S(2)}) copy-start(s32[1024]{0:T(1024)S(1)} %pad_clamp_fusion) | copy-start | bytes 12292
  24.4 5.4 %copy-start.1 = (f32[8,8,512]{2,1,0:T(8,128)S(1)}, f32[8,8,512]{2,1,0:T(8,128)}, u32[]{:S(2)}) copy-start(f32[8,8,512]{2,1,0:T(8,128)} %param.17) | copy-start | bytes 393220
  90.3 68.9 %copy-start.2 = (f32[8,8,512]{2,1,0:T(8,128)S(1)}, f32[8,8,512]{2,1,0:T(8,128)}, u32[]{:S(2)}) copy-start(f32[8,8,512]{2,1,0:T(8,128)} %param.17) | copy-start | bytes 393220
  91.9 197.5 %all-reduce.5.cloned.1.call-start = ((), (), s32[]{:S(2)}) async-start(), calls=%async_computation.2 | async-start | bytes 262144 | tf_op jit(solution)/shard_map/psum | solution.py:172
  167.5 4.1 %copy-start.6 = (f32[1,8,128]{2,1,0:T(8,128)}, f32[1,8,128]{2,1,0:T(8,128)S(1)}, u32[]{:S(2)}) copy-start(f32[1,8,128]{2,1,0:T(8,128)S(1)} %copy.410) | copy-start | bytes 12292
  169.3 2.5 copy-start.8
  174.4 4.9 %copy-start.11 = (f32[1,8,128]{2,1,0:T(8,128)S(1)}, f32[1,8,128]{2,1,0:T(8,128)}, u32[]{:S(2)}) copy-start(f32[1,8,128]{2,1,0:T(8,128)} %copy-done.10) | copy-start | bytes 12292
  174.4 4.9 %copy-start.13 = (f32[1,8,128]{2,1,0:T(8,128)S(1)}, f32[1,8,128]{2,1,0:T(8,128)}, u32[]{:S(2)}) copy-start(f32[1,8,128]{2,1,0:T(8,128)} %copy-done.12) | copy-start | bytes 12292
  175.7 4.4 %copy-start.14 = (f32[1,8,128]{2,1,0:T(8,128)}, f32[1,8,128]{2,1,0:T(8,128)S(1)}, u32[]{:S(2)}) copy-start(f32[1,8,128]{2,1,0:T(8,128)S(1)} %copy.411) | copy-start | bytes 12292
  176.9 3.1 %copy-start.15 = (f32[1,8,128]{2,1,0:T(8,128)}, f32[1,8,128]{2,1,0:T(8,128)S(1)}, u32[]{:S(2)}) copy-start(f32[1,8,128]{2,1,0:T(8,128)S(1)} %copy.414) | copy-start | bytes 12292
  176.9 2.5 copy-start.7
  176.9 2.5 copy-start.9
  179.3 37.3 %copy-start.20 = (f32[8,128]{1,0:T(8,128)S(1)}, f32[8,128]{1,0:T(8,128)}, u32[]{:S(2)}) copy-start(f32[8,128]{1,0:T(8,128)} %bitcast_negate_fusion.2) | copy-start | bytes 12292
  179.3 37.3 %copy-start.21 = (f32[8,128]{1,0:T(8,128)S(1)}, f32[8,128]{1,0:T(8,128)}, u32[]{:S(2)}) copy-start(f32[8,128]{1,0:T(8,128)} %bitcast_negate_fusion.3) | copy-start | bytes 12292
  179.3 37.3 %copy-start.18 = (f32[8,128]{1,0:T(8,128)S(1)}, f32[8,128]{1,0:T(8,128)}, u32[]{:S(2)}) copy-start(f32[8,128]{1,0:T(8,128)} %bitcast_negate_fusion) | copy-start | bytes 12292
  179.3 37.3 %copy-start.19 = (f32[8,128]{1,0:T(8,128)S(1)}, f32[8,128]{1,0:T(8,128)}, u32[]{:S(2)}) copy-start(f32[8,128]{1,0:T(8,128)} %bitcast_negate_fusion.1) | copy-start | bytes 12292
  179.5 41.0 %copy-start.4 = (f32[8,4,2,1,128]{4,0,2,1,3:T(8,128)S(1)}, f32[8,4,2,1,128]{4,0,2,1,3:T(8,128)}, u32[]{:S(2)}) copy-start(f32[8,4,2,1,128]{4,0,2,1,3:T(8,128)} %copy-done.3) | copy-start | bytes 98308
  221.3 72.5 %copy-start.31 = (pred[128]{0:T(512)(128)(4,1)S(1)}, pred[128]{0:T(512)(128)(4,1)}, u32[]{:S(2)}) copy-start(pred[128]{0:T(512)(128)(4,1)} %copy-done.30) | copy-start | bytes 388
  221.3 72.6 %copy-start.24 = (pred[128]{0:T(512)(128)(4,1)S(1)}, pred[128]{0:T(512)(128)(4,1)}, u32[]{:S(2)}) copy-start(pred[128]{0:T(512)(128)(4,1)} %copy-done.23) | copy-start | bytes 388
  299.2 4.5 %copy-start.5 = (f32[8,4,2,1,128]{4,0,2,1,3:T(8,128)S(1)}, f32[8,4,2,1,128]{4,0,2,1,3:T(8,128)}, u32[]{:S(2)}) copy-start(f32[8,4,2,1,128]{4,0,2,1,3:T(8,128)} %copy-done.3) | copy-start | bytes 98308
  299.2 4.5 %copy-start.29 = (f32[128]{0:T(128)S(1)}, f32[128]{0:T(128)}, u32[]{:S(2)}) copy-start(f32[128]{0:T(128)} %copy-done.27) | copy-start | bytes 1540
  (9 other events, 12.3 us)
Sparse Core Ops, SparseCore 0:
  92.1 67.0 all-reduce.2
  222.4 66.9 all-reduce.4
where the time goes:
time: 312 us; the launch traced here: 311 us
  waiting for transfers between devices  134 us (43%)
  blocking collectives  83.7 us (27%)
  local copies, waits for them, and re-layouts  50.7 us (16%)
  other arithmetic  15.7 us (5%)
  between operations  15.3 us (5%)
  starting transfers between devices  6.36 us (2%)
  matrix products  5.15 us (2%)
    psum x2, waiting for transfers between devices, per_device(): lax.psum((grad_station, curv_station), ('chan', 'blk'))  134 us
    psum x2, blocking collectives, per_device(): lax.psum((grad_station, curv_station), ('chan', 'blk'))  73 us
    psum x3, blocking collectives, residual_of(): model_vis = lax.psum(partial_model, 'dir')  10.7 us
    slice x9, local copies, waits for them, and re-layouts, jones_product(): former[2 * row_number] * latter[column]  10.5 us
    slice x4, local copies, waits for them, and re-layouts, adjoint(): matrix[2]  6.6 us
    all_to_all x1, starting transfers between devices, per_device(): lax.all_to_all(visibilities, 'chan', split_axis=3, concat_axis=1, tiled=T...  6.32 us
  transfers between devices with their start and end apart: 3, of which 2 were waited for; matrix products, arithmetic and copies ran while one was open for 10% of the time, Pallas kernels for 0%

commit v1 on v0

--- a/solution.py
+++ b/solution.py
@@ -1,8 +1,11 @@
+import functools
 import math
 
 import jax
 import jax.numpy as jnp
 from jax import lax
+from jax.experimental import pallas as pl
+from jax.experimental.pallas import tpu as pltpu
 from jax.sharding import PartitionSpec as P
 
 ITERS = 2
@@ -175,6 +178,475 @@
     return (residual_now[:, :, None, :], gains_now)
 
 
+COS_TERMS = (
+    0.9999999890590228,
+    -19.739204499454,
+    64.93911745989914,
+    -85.45013953093448,
+    60.16763095128989,
+    -25.96759924954187,
+    6.528658162606979,
+)
+SIN_TERMS = (
+    6.283185302511502,
+    -41.34170040531754,
+    81.6051313857969,
+    -76.70301535383193,
+    42.02592698564183,
+    -14.899846667160109,
+    3.2381375090822355,
+)
+RUN = 128
+BLOCK = 64
+BLOCKS = 8
+
+
+def pieces(value, count):
+    result = []
+    for index in range(count):
+        piece = value.astype(jnp.bfloat16)
+        result.append(piece)
+        if index < count - 1:
+            value = value - piece.astype(jnp.float32)
+    return result
+
+
+def dot_f32(left, right, contract_right=0):
+    return lax.dot_general(
+        left,
+        right,
+        (((1,), (contract_right,)), ((), ())),
+        preferred_element_type=jnp.float32,
+    )
+
+
+def horner(terms, x):
+    total = jnp.full_like(x, terms[-1])
+    for term in terms[-2::-1]:
+        total = total * x + term
+    return total
+
+
+def turn_pair(turns):
+    rest = turns - jnp.round(turns)
+    square = rest * rest
+    return horner(COS_TERMS, square), horner([-term for term in SIN_TERMS], square) * rest
+
+
+def product(a, b):
+    real = []
+    imag = []
+    for row in (0, 1):
+        for col in (0, 1):
+            ar, br, cr, dr = a[2 * row], b[col], a[2 * row + 1], b[2 + col]
+            ai, bi, ci, di = a[4 + 2 * row], b[4 + col], a[5 + 2 * row], b[6 + col]
+            real.append(ar * br - ai * bi + cr * dr - ci * di)
+            imag.append(ar * bi + ai * br + cr * di + ci * dr)
+    return real + imag
+
+
+def dagger(a):
+    return [a[0], a[2], a[1], a[3], -a[4], -a[6], -a[5], -a[7]]
+
+
+class Place:
+    def __init__(self, runs):
+        self.chan = lax.axis_index("chan")
+        self.core = lax.axis_index("dir")
+        self.window = lax.axis_index("blk") * lax.axis_size("dir") + self.core
+        self.runs = runs
+        self.lanes = runs * RUN
+        self.first_lane = pl.multiple_of(self.core * self.lanes, self.lanes)
+        self.width = runs * BLOCK
+        self.first_station = pl.multiple_of(self.window * self.width, self.width)
+
+    def onehot(self, pairs_ref, side):
+        station = pairs_ref[side, :, pl.ds(self.first_lane, self.lanes)]
+        local = jnp.where(station < BLOCK, station, station - self.first_station + RUN)
+        rows = lax.broadcasted_iota(jnp.int32, (RUN + self.width, self.lanes), 0)
+        return jnp.where(rows == local, 1.0, 0.0).astype(jnp.bfloat16)
+
+    def slot(self, channel, per_shard):
+        return jnp.bitwise_xor(channel // per_shard, self.chan) * per_shard + channel % per_shard
+
+
+def coherency_kernel(
+    runs, channels, per_shard, pairs, positions, offsets, brightness, cluster, out, base, spin, parts
+):
+    place = Place(runs)
+    table = jnp.concatenate(
+        [positions[:, 0:RUN], positions[:, pl.ds(place.first_station, place.width)]], axis=1
+    )
+    table = jnp.concatenate([p.astype(jnp.float32) for p in pieces(table, 3)] + [jnp.zeros((2, table.shape[1]))])
+    table = table.astype(jnp.bfloat16)
+    there = []
+    for side in (0, 1):
+        found = dot_f32(table, place.onehot(pairs, side))
+        there.append(found[0:2] + found[2:4] + found[4:6])
+    span = there[0] - there[1]
+    sources = offsets.shape[1]
+    columns = jnp.transpose(jnp.concatenate([offsets[...], jnp.zeros((6, sources))]))
+    step = 16
+    for start in range(0, sources, step):
+        rows = slice(start, start + step)
+        geometry = columns[rows, 0:1] * span[0:1] + columns[rows, 1:2] * span[1:2]
+        base[0, rows], base[1, rows] = turn_pair(geometry)
+        spin[0, rows], spin[1, rows] = turn_pair(geometry * (0.5 / channels))
+
+    directions = out.shape[1] // 8
+    member = lax.broadcasted_iota(jnp.int32, (directions, sources), 0) == cluster[...]
+    bright = jnp.concatenate([jnp.where(member, brightness[n : n + 1], 0.0) for n in range(4)])
+    high, low = pieces(bright, 2)
+    both = jnp.concatenate([high, low])
+    half = 4 * directions
+    for channel in range(channels):
+        for start in range(0, sources, step):
+            rows = slice(start, start + step)
+            c, s = base[0, rows], base[1, rows]
+            for index, value in enumerate((c, s)):
+                first, second = pieces(value, 2)
+                parts[channel % 2, index, 0, rows] = first
+                parts[channel % 2, index, 1, rows] = second
+            if channel < channels - 1:
+                dc, ds = spin[0, rows], spin[1, rows]
+                base[0, rows] = c * dc - s * ds
+                base[1, rows] = s * dc + c * ds
+        slot = place.slot(channel, per_shard)
+        for index in (0, 1):
+            wide = dot_f32(both, parts[channel % 2, index, 0])
+            narrow = dot_f32(high, parts[channel % 2, index, 1])
+            out[slot, half * index : half * (index + 1)] = wide[:half] + wide[half:] + narrow
+
+
+def iterate(place, coherent, shards, mask, pairs, jones, near, far, error, gather, sums):
+    first_hot = place.onehot(pairs, 0)
+    second_hot = place.onehot(pairs, 1)
+    rows = jones.shape[0]
+    directions = rows // 8
+    split = jnp.concatenate([p for p in pieces(jones[...], 3)])
+    for side, hot in enumerate((first_hot, second_hot)):
+        found = dot_f32(split, hot)
+        found = found[:rows] + found[rows : 2 * rows] + found[2 * rows :]
+        for run in range(place.runs):
+            gather[side, run] = found[:, run * RUN : (run + 1) * RUN]
+    weight = mask[:, pl.ds(place.first_lane, place.lanes)].astype(jnp.float32)
+    channels = coherent.shape[0]
+    per_shard = shards[0].shape[1]
+    halves = directions // 8
+
+    for run in range(place.runs):
+        lanes = slice(run * RUN, (run + 1) * RUN)
+        w = weight[:, lanes]
+
+        def gains(side, h):
+            return [gather[side, run, pl.ds(64 * h + n, 8, stride=8), :] for n in range(8)]
+
+        for channel in range(channels):
+            shard = shards[channel // per_shard]
+            models = [None] * 8
+            for h in range(halves):
+                coh = [
+                    coherent[channel, n * directions + 8 * h : n * directions + 8 * h + 8, lanes]
+                    for n in range(8)
+                ]
+                toward_first = product(gains(0, h), coh)
+                toward_second = product(gains(1, h), dagger(coh))
+                for n in range(8):
+                    near[h, channel, n] = toward_first[n]
+                    far[h, channel, n] = toward_second[n]
+                part = product(toward_first, dagger(gains(1, h)))
+                models = part if h == 0 else [a + b for a, b in zip(models, part)]
+            at = pl.multiple_of(place.first_lane + run * RUN, RUN)
+            for n in range(8):
+                model = jnp.sum(models[n], axis=0, keepdims=True)
+                seen = shard[n, channel % per_shard, :, pl.ds(at, RUN)]
+                error[channel, n : n + 1] = w * (seen - model)
+
+        for h in range(halves):
+            zero = jnp.zeros((8, RUN), jnp.float32)
+            first, second, curve_first, curve_second = [zero] * 8, [zero] * 8, zero, zero
+            for channel in range(channels):
+                err = [jnp.broadcast_to(error[channel, n : n + 1], (8, RUN)) for n in range(8)]
+                z = [near[h, channel, n] for n in range(8)]
+                y = [far[h, channel, n] for n in range(8)]
+                first = [a + b for a, b in zip(first, product(err, y))]
+                second = [a + b for a, b in zip(second, product(dagger(err), z))]
+                for n in range(8):
+                    curve_first = curve_first + y[n] * y[n]
+                    curve_second = curve_second + z[n] * z[n]
+            for n in range(8):
+                sums[0, run, pl.ds(64 * h + n, 8, stride=8), :] = first[n]
+                sums[1, run, pl.ds(64 * h + n, 8, stride=8), :] = second[n]
+            sums[0, run, rows + 8 * h : rows + 8 * h + 8] = w * curve_first
+            sums[1, run, rows + 8 * h : rows + 8 * h + 8] = w * curve_second
+
+    total = None
+    height = sums.shape[2]
+    for side, hot in enumerate((first_hot, second_hot)):
+        whole = jnp.concatenate([sums[side, run] for run in range(place.runs)], axis=1)
+        found = dot_f32(jnp.concatenate(pieces(whole, 2)), hot, 1)
+        found = found[:height] + found[height:]
+        total = found if total is None else total + found
+    return total
+
+
+def pack(total, rows):
+    half = rows // 2
+    low = jnp.concatenate([total[:half], total[rows : rows + half // 8]])
+    high = jnp.concatenate([total[half:rows], total[rows + half // 8 :]])
+    lane = lax.broadcasted_iota(jnp.int32, low.shape, 1)
+    return jnp.where(lane < BLOCK, low, pltpu.roll(high, BLOCK, 1))
+
+
+def unpack(packed):
+    half = packed.shape[0] * 8 // 9
+    turned = pltpu.roll(packed, BLOCK, 1)
+    return jnp.concatenate([packed[:half], turned[:half], packed[half:], turned[half:]])
+
+
+def update(jones, lanes, sums, keep=None):
+    rows = jones.shape[0]
+    for d in range(rows // 8):
+        now = jones[8 * d : 8 * d + 8, lanes]
+        curve = sums[rows + d : rows + d + 1] + EPSILON
+        new = now + STEP_SIZE * sums[8 * d : 8 * d + 8] / curve
+        if keep is not None:
+            new = jnp.where(keep, new, now)
+        jones[8 * d : 8 * d + 8, lanes] = new
+
+
+def block_zero():
+    return lax.broadcasted_iota(jnp.int32, (8, RUN), 1) < BLOCK
+
+
+def first_kernel(
+    runs, pairs, mask, coherent, own, other, s0, s1, s2, s3, packed, mine, jones, near, far, error, gather, sums
+):
+    place = Place(runs)
+    count = own.shape[0] * own.shape[1]
+    for ref, core in ((own, place.core), (other, 1 - place.core)):
+        at = pl.ds(pl.multiple_of(core * count, count), count)
+        value = ref[:, :, 0:RUN]
+        jones[at, 0:RUN] = value.reshape(count, RUN)
+        value = ref[:, :, pl.ds(place.first_station, place.width)]
+        jones[at, RUN:] = value.reshape(count, place.width)
+    total = iterate(place, coherent, (s0, s1, s2, s3), mask, pairs, jones, near, far, error, gather, sums)
+    packed[...] = pack(total[:, :RUN], jones.shape[0])
+    mine[...] = total[:, RUN:]
+
+
+def second_kernel(
+    runs, pairs, mask, coherent, before, mine, sum_here, sum_there, s0, s1, s2, s3,
+    packed, jones, near, far, error, gather, sums,
+):
+    place = Place(runs)
+    jones[...] = before[...]
+    update(jones, slice(0, RUN), unpack(sum_here[...] + sum_there[...]), block_zero())
+    update(jones, slice(RUN, None), mine[...])
+    total = iterate(place, coherent, (s0, s1, s2, s3), mask, pairs, jones, near, far, error, gather, sums)
+    rows = jones.shape[0]
+    held = packed.shape[0] - rows // 2
+    packed[:held] = pack(total[:, :RUN], rows)
+    update(jones, slice(RUN, None), total[:, RUN:])
+    packed[held:] = jones[pl.ds(pl.multiple_of((1 - place.core) * (rows // 2), rows // 2), rows // 2), RUN:]
+
+
+def join_kernel(here, there, jones, out):
+    held = out.shape[0] - 2 * (jones.shape[0] // 2)
+    half = jones.shape[0] // 2
+    core = lax.axis_index("dir")
+    out[:held] = here[:held] + there[:held]
+    out[held : held + half] = jones[pl.ds(pl.multiple_of(core * half, half), half), RUN:]
+    out[held + half :] = there[held:]
+
+
+def last_kernel(
+    runs, pairs, mask, coherent, before, here, there, s0, s1, s2, s3, residual, solved, jones, gather
+):
+    place = Place(runs)
+    jones[...] = before[...]
+    rows = jones.shape[0]
+    half = rows // 2
+    held = here.shape[0] - rows
+    update(jones, slice(0, RUN), unpack(here[:held] + there[:held]), block_zero())
+
+    blk = lax.axis_index("blk")
+    for ref, b in ((here, blk), (there, 1 - blk)):
+        for at, core in ((held, place.core), (held + half, 1 - place.core)):
+            lanes = pl.ds(pl.multiple_of((2 * b + core) * place.width, place.width), place.width)
+            solved[:, :, lanes] = ref[at : at + half].reshape(half // 8, 8, place.width)
+    zero = jones[pl.ds(pl.multiple_of(place.core * half, half), half), 0:RUN].reshape(half // 8, 8, RUN)
+    lane = lax.broadcasted_iota(jnp.int32, zero.shape, 2)
+    solved[:, :, 0:RUN] = jnp.where(lane < BLOCK, zero, solved[:, :, 0:RUN])
+
+    directions = rows // 8
+    run = lax.rem(place.chan, runs)
+    shift = pl.multiple_of(run * RUN, RUN)
+    split = jnp.concatenate([p for p in pieces(jones[...], 3)])
+    for side in (0, 1):
+        found = dot_f32(split, place.onehot(pairs, side))
+        found = found[:rows] + found[rows : 2 * rows] + found[2 * rows :]
+        for index in range(runs):
+            gather[side, index] = found[:, index * RUN : (index + 1) * RUN]
+    at = pl.multiple_of(place.first_lane + shift, RUN)
+    w = mask[:, pl.ds(at, RUN)].astype(jnp.float32)
+    shards = (s0, s1, s2, s3)
+    channels = coherent.shape[0]
+    per_shard = s0.shape[1]
+    here_lanes = pl.ds(shift, RUN)
+
+    def gains(side, h):
+        return [gather[side, run, pl.ds(64 * h + n, 8, stride=8), :] for n in range(8)]
+
+    for channel in range(channels):
+        models = None
+        for h in range(directions // 8):
+            coh = [
+                coherent[channel, n * directions + 8 * h : n * directions + 8 * h + 8, here_lanes]
+                for n in range(8)
+            ]
+            part = product(product(gains(0, h), coh), dagger(gains(1, h)))
+            models = part if models is None else [a + b for a, b in zip(models, part)]
+        shard = shards[channel // per_shard]
+        true_channel = place.slot(channel, per_shard)
+        for n in range(8):
+            model = jnp.sum(models[n], axis=0, keepdims=True)
+            seen = shard[n, channel % per_shard, :, pl.ds(at, RUN)]
+            residual[n, true_channel] = w * (seen - model)
+
+
+def call(kernel, out_shape, scratch, *operands):
+    return pl.pallas_call(
+        kernel,
+        out_shape=out_shape,
+        in_specs=[pl.BlockSpec(memory_space=pltpu.VMEM)] * len(operands),
+        out_specs=jax.tree.map(lambda _: pl.BlockSpec(memory_space=pltpu.VMEM), out_shape),
+        scratch_shapes=scratch,
+        compiler_params=pltpu.CompilerParams(vmem_limit_bytes=40 << 20),
+    )(*operands)
+
+
+def f32(*shape):
+    return jax.ShapeDtypeStruct(shape, jnp.float32)
+
+
+def swap(x, axis, bit=1):
+    return lax.ppermute(x, axis, [(i, i ^ bit) for i in range(lax.axis_size(axis))])
+
+
+def per_device_owned(
+    visibilities,
+    antenna_pairs,
+    valid_mask,
+    station_positions,
+    source_offsets,
+    brightness,
+    source_cluster,
+    jones_gains,
+):
+    relay_count = lax.axis_size("chan")
+    runs = relay_count // lax.axis_size("dir")
+    per_shard = visibilities.shape[1]
+    channels = per_shard * relay_count
+    half_directions = jones_gains.shape[0]
+    directions = 2 * half_directions
+    rows = 8 * directions
+    lanes = runs * RUN
+    width = runs * BLOCK
+    sources = source_offsets.shape[1]
+
+    other = swap(jones_gains, "dir")
+    shards = [visibilities] + [swap(visibilities, "chan", bit) for bit in range(1, relay_count)]
+    coherent = call(
+        functools.partial(coherency_kernel, runs, channels, per_shard),
+        f32(channels, rows, lanes),
+        [
+            pltpu.VMEM((2, sources, lanes), jnp.float32),
+            pltpu.VMEM((2, sources, lanes), jnp.float32),
+            pltpu.VMEM((2, 2, 2, sources, lanes), jnp.bfloat16),
+        ],
+        antenna_pairs,
+        station_positions,
+        source_offsets,
+        brightness,
+        source_cluster[None, :],
+    )
+    scratch = [
+        pltpu.VMEM((directions // 8, channels, 8, 8, RUN), jnp.float32),
+        pltpu.VMEM((directions // 8, channels, 8, 8, RUN), jnp.float32),
+        pltpu.VMEM((channels, 8, RUN), jnp.float32),
+        pltpu.VMEM((2, runs, rows, RUN), jnp.float32),
+        pltpu.VMEM((2, runs, rows + directions, RUN), jnp.float32),
+    ]
+    table = f32(rows, RUN + width)
+    held = (rows + directions) // 2
+    packed, mine, jones = call(
+        functools.partial(first_kernel, runs),
+        (f32(held, RUN), f32(rows + directions, width), table),
+        scratch,
+        antenna_pairs,
+        valid_mask,
+        coherent,
+        jones_gains,
+        other,
+        *shards,
+    )
+    packed = packed + swap(packed, "dir")
+    there = swap(packed, "blk")
+    packed, jones = call(
+        functools.partial(second_kernel, runs),
+        (f32(held + rows // 2, RUN), table),
+        scratch,
+        antenna_pairs,
+        valid_mask,
+        coherent,
+        jones,
+        mine,
+        packed,
+        there,
+        *shards,
+    )
+    joined = call(
+        join_kernel,
+        f32(held + rows, RUN),
+        [],
+        packed,
+        swap(packed, "dir"),
+        jones,
+    )
+    residual, solved = call(
+        functools.partial(last_kernel, runs),
+        (f32(8, channels, 1, RUN), f32(half_directions, 8, station_positions.shape[1])),
+        [pltpu.VMEM((rows, RUN + width), jnp.float32), pltpu.VMEM((2, runs, rows, RUN), jnp.float32)],
+        antenna_pairs,
+        valid_mask,
+        coherent,
+        jones,
+        joined,
+        swap(joined, "blk"),
+        *shards,
+    )
+    held_here = lax.axis_index("chan") // runs == lax.axis_index("dir")
+    residual = jnp.where(held_here, residual, swap(residual, "dir"))
+    return residual, solved
+
+
+def owned_layout(mesh, shapes):
+    sizes = mesh.shape
+    owners = sizes["chan"] * sizes["blk"]
+    visibilities, pairs, jones = shapes
+    return (
+        owners == BLOCKS
+        and sizes["blk"] == 2
+        and sizes["dir"] == 2
+        and sizes["chan"] == 4
+        and pairs[1] * pairs[2] == owners * RUN
+        and jones[0] == 16
+        and jones[2] == BLOCKS * BLOCK
+        and visibilities[1] % sizes["chan"] == 0
+    )
+
+
 def solution(mesh):
     in_specs = (
         P("groups", "chan", "blk", None),
@@ -187,6 +659,12 @@
         P("dir", "groups", None),
     )
     out_specs = (P("groups", None, "blk", "chan"), P("dir", "groups", None))
-    return jax.shard_map(
-        per_device, mesh=mesh, in_specs=in_specs, out_specs=out_specs, check_vma=False
-    )
+
+    def run(*arrays):
+        owned = owned_layout(mesh, (arrays[0].shape, arrays[1].shape, arrays[7].shape))
+        body = per_device_owned if owned else per_device
+        return jax.shard_map(
+            body, mesh=mesh, in_specs=in_specs, out_specs=out_specs, check_vma=False
+        )(*arrays)
+
+    return run

time: 312 us -> 31.4 us (0.10)
  waiting for transfers between devices: 134 us -> 10.7 us
  blocking collectives: 83.7 us -> 0 us
  local copies, waits for them, and re-layouts: 50.7 us -> 2.76 us
  other arithmetic: 15.7 us -> 0.63 us
  between operations: 15.3 us -> 0.71 us
  Pallas kernels: 0 us -> 7.38 us
  matrix products: 5.15 us -> 0 us
    psum x2 -> x0, waiting for transfers between devices: 134 us -> none  [per_device(): lax.psum((grad_station, curv_station), ('chan', 'blk'))]
    psum x5 -> x0, blocking collectives: 83.7 us -> none  [the longest x2 73 us: per_device(): lax.psum((grad_station, curv_station), ('chan', 'blk'))]
    slice x47 -> x0, local copies, waits for them, and re-layouts: 32.1 us -> none  [the longest x9 10.5 us: jones_product(): former[2 * row_number] * latter[column]]
    gather x11 -> x0, local copies, waits for them, and re-layouts: 11 us -> none  [the longest x3 3.19 us: station_gains(): jnp.take(gains_current, first_station, axis=2).transpose(1, 0, 2)]
    ppermute x0 -> x9, waiting for transfers between devices: none -> 10.7 us  [swap(): lax.ppermute(x, axis, [(i, i ^ bit) for i in range(lax.axis_size(axis))])]
    ppermute x0 -> x9, starting transfers between devices: none -> 8.95 us  [swap(): lax.ppermute(x, axis, [(i, i ^ bit) for i in range(lax.axis_size(axis))])]
    pallas_call x0 -> x5, Pallas kernels: none -> 7.38 us  [call(): pl.pallas_call(kernel, out_shape=out_shape, in_specs=[pl.BlockSpec(memory...]
    all_to_all x1 -> x0, starting transfers between devices: 6.32 us -> none  [per_device(): lax.all_to_all(visibilities, 'chan', split_axis=3, concat_axis=1, tiled=T...]
  transfers between devices with their start and end apart: 3 -> 9, of which waited for: 2 -> 6; matrix products, arithmetic and copies ran while one was open for 10% -> 0% of each run, Pallas kernels for 0% -> 6%
where the time goes in v1:
time: 31.4 us; the launch traced here: 31.2 us
  waiting for transfers between devices  10.7 us (34%)
  starting transfers between devices  8.95 us (29%)
  Pallas kernels  7.38 us (24%)
  local copies, waits for them, and re-layouts  2.76 us (9%)
  between operations  0.71 us (2%)
  other arithmetic  0.63 us (2%)
    ppermute x9, waiting for transfers between devices, swap(): lax.ppermute(x, axis, [(i, i ^ bit) for i in range(lax.axis_size(axis))])  10.7 us
    ppermute x9, starting transfers between devices, swap(): lax.ppermute(x, axis, [(i, i ^ bit) for i in range(lax.axis_size(axis))])  8.95 us
    pallas_call x5, Pallas kernels, call(): pl.pallas_call(kernel, out_shape=out_shape, in_specs=[pl.BlockSpec(memory...  7.38 us
    unnamed x18, local copies, waits for them, and re-layouts  2.76 us
  transfers between devices with their start and end apart: 9, of which 6 were waited for; matrix products, arithmetic and copies ran while one was open for 0% of the time, Pallas kernels for 6%

profile of v1, /device:TPU:0, one launch (start us, length us, event | category | flops | bytes accessed | tf_op | source)
XLA Modules:
  0.0 31.2 jit_solution(3968468363826889643)
XLA Ops:
  0.6 0.0 copy-start.8
  0.6 0.5 %collective-permute-start = (f32[8,8,512]{2,1,0:T(8,128)}, f32[8,8,512]{2,1,0:T(8,128)S(1)}, u32[]{:S(2)}, u32[]{:S(2)}) collective-permute-start(f32[8,8,512]{2,1,0:T(8,128)} %own.1), channel_id=1, source_target_pairs={{0,1},{1,0},{2,3},{3,2},{4,5},{5,4},{6,7},{7,6},{8,9},{9,8},{10,11... | collective-permute-start | bytes 393224 | tf_op jit(solution)/shard_map/ppermute | solution.py:534
  1.2 2.6 %collective-permute-start.1 = (f32[8,2,1,512]{3,2,1,0:T(1,128)}, f32[8,2,1,512]{3,2,1,0:T(1,128)S(1)}, u32[]{:S(2)}, u32[]{:S(2)}) collective-permute-start(f32[8,2,1,512]{3,2,1,0:T(1,128)} %s0.5), channel_id=1, source_target_pairs={{0,4},{4,0},{8,12},{12,8},{1,5},{5,1},{9,13},{13,9},{2,6},{6,2},{1... | collective-permute-start | bytes 98312 | tf_op jit(solution)/shard_map/ppermute | solution.py:534
  3.8 2.6 %collective-permute-start.2 = (f32[8,2,1,512]{3,2,1,0:T(1,128)}, f32[8,2,1,512]{3,2,1,0:T(1,128)S(1)}, u32[]{:S(2)}, u32[]{:S(2)}) collective-permute-start(f32[8,2,1,512]{3,2,1,0:T(1,128)} %s0.5), channel_id=1, source_target_pairs={{0,8},{4,12},{8,0},{12,4},{1,9},{5,13},{9,1},{13,5},{2,10},{6,14},... | collective-permute-start | bytes 98312 | tf_op jit(solution)/shard_map/ppermute | solution.py:534
  6.4 0.0 collective-permute-start.3
  6.4 0.0 copy-done.8
  6.4 0.7 %copy-done.2 = s32[2,1,512]{2,1,0:T(1,128)S(1)} copy-done((s32[2,1,512]{2,1,0:T(1,128)S(1)}, s32[2,1,512]{2,1,0:T(1,128)}, u32[]{:S(2)}) %copy-start.2) | copy-done | bytes 4120
  7.1 0.7 %copy-done.5 = f32[2,512]{1,0:T(2,128)S(1)} copy-done((f32[2,512]{1,0:T(2,128)S(1)}, f32[2,512]{1,0:T(2,128)}, u32[]{:S(2)}) %copy-start.5) | copy-done | bytes 4120
  7.8 0.7 %copy-done.6 = f32[4,256]{1,0:T(4,128)S(1)} copy-done((f32[4,256]{1,0:T(4,128)S(1)}, f32[4,256]{1,0:T(4,128)}, u32[]{:S(2)}) %copy-start.6) | copy-done | bytes 4120
  8.5 0.7 %copy-done.7 = f32[2,256]{1,0:T(2,128)S(1)} copy-done((f32[2,256]{1,0:T(2,128)S(1)}, f32[2,256]{1,0:T(2,128)}, u32[]{:S(2)}) %copy-start.7) | copy-done | bytes 2072
  9.2 2.0 %shard_map.95.coherent = f32[8,128,256]{2,1,0:T(8,128)S(1)} custom-call(s32[2,1,512]{2,1,0:T(1,128)S(1)} %copy-done.2, f32[2,512]{1,0:T(2,128)S(1)} %copy-done.5, f32[2,256]{1,0:T(2,128)S(1)} %copy-done.7, f32[4,256]{1,0:T(4,128)S(1)} %copy-done.6, s32[1,256]{1,0:T(1,128)S(1)} %bitcast.5), custom_call_target="tpu_custom_call" | custom-call | tf_op jit(solution)/shard_map/pallas_call | solution.py:519
  11.1 0.0 collective-permute-done.1.s1
  11.1 0.0 collective-permute-done.2.s2
  11.2 1.2 %collective-permute-done.3.s3 = f32[8,2,1,512]{3,2,1,0:T(1,128)S(1)} collective-permute-done((f32[8,2,1,512]{3,2,1,0:T(1,128)}, f32[8,2,1,512]{3,2,1,0:T(1,128)S(1)}, u32[]{:S(2)}, u32[]{:S(2)}) %collective-permute-start.3) | collective-permute-done | bytes 32800 | tf_op jit(solution)/shard_map/ppermute | solution.py:534
  12.3 0.0 collective-permute-done.other
  12.3 0.0 copy-done
  12.3 0.0 copy-done.1
  12.3 0.0 copy-done.4
  12.3 2.3 %shard_map.96 = (f32[72,128]{1,0:T(8,128)S(1)}, f32[144,128]{1,0:T(8,128)S(1)}, f32[128,256]{1,0:T(8,128)S(1)}) custom-call(s32[2,1,512]{2,1,0:T(1,128)S(1)} %copy-done.2, s32[1,512]{1,0:T(1,128)S(1)} %copy-done.4, f32[8,128,256]{2,1,0:T(8,128)S(1)} %shard_map.95.coherent, f32[8,8,512]{2,1,0:T(8,128)S(1)} %copy-done.1, ...), custom_call_target="tpu_custom_call" | custom-call | tf_op jit(solution)/shard_map/pallas_call | solution.py:519
  14.6 0.1 collective-permute-start.4
  14.7 1.2 %collective-permute-done.4 = f32[72,128]{1,0:T(8,128)S(1)} collective-permute-done((f32[72,128]{1,0:T(8,128)S(1)}, f32[72,128]{1,0:T(8,128)S(1)}, u32[]{:S(2)}, u32[]{:S(2)}) %collective-permute-start.4) | collective-permute-done | bytes 36896 | tf_op jit(solution)/shard_map/ppermute | solution.py:534
  15.9 1.5 %collective-permute-start.5 = (f32[72,128]{1,0:T(8,128)S(1)}, f32[72,128]{1,0:T(8,128)S(1)}, u32[]{:S(2)}, u32[]{:S(2)}) collective-permute-start(f32[72,128]{1,0:T(8,128)S(1)} %add.4.sum_here), channel_id=1, source_target_pairs={{0,2},{2,0},{1,3},{3,1},{4,6},{6,4},{5,7},{7,5},{8,10},{10,8},{9,1... | collective-permute-start | bytes 110600 | tf_op jit(solution)/shard_map/ppermute | solution.py:534
  17.4 2.5 %collective-permute-done.5.sum_there = f32[72,128]{1,0:T(8,128)S(1)} collective-permute-done((f32[72,128]{1,0:T(8,128)S(1)}, f32[72,128]{1,0:T(8,128)S(1)}, u32[]{:S(2)}, u32[]{:S(2)}) %collective-permute-start.5) | collective-permute-done | bytes 36896 | tf_op jit(solution)/shard_map/ppermute | solution.py:534
  19.9 2.3 %shard_map.97 = (f32[136,128]{1,0:T(8,128)S(1)}, f32[128,256]{1,0:T(8,128)S(1)}) custom-call(s32[2,1,512]{2,1,0:T(1,128)S(1)} %copy-done.2, s32[1,512]{1,0:T(1,128)S(1)} %copy-done.4, f32[8,128,256]{2,1,0:T(8,128)S(1)} %shard_map.95.coherent, f32[128,256]{1,0:T(8,128)S(1)} %get-tuple-element.9.before, f32[144,128]{1,0:T(8,128)S(1)} %get-tuple-element.10.mine, ...), custom_call_target="tpu_custom_call" | custom-call | tf_op jit(solution)/shard_map/pallas_call | solution.py:519
  22.2 0.1 collective-permute-start.6
  22.3 1.2 %collective-permute-done.6.there = f32[136,128]{1,0:T(8,128)S(1)} collective-permute-done((f32[136,128]{1,0:T(8,128)S(1)}, f32[136,128]{1,0:T(8,128)S(1)}, u32[]{:S(2)}, u32[]{:S(2)}) %collective-permute-start.6) | collective-permute-done | bytes 69664 | tf_op jit(solution)/shard_map/ppermute | solution.py:534
  23.6 1.6 %collective-permute-start.7 = (f32[200,128]{1,0:T(8,128)S(1)}, f32[200,128]{1,0:T(8,128)S(1)}, u32[]{:S(2)}, u32[]{:S(2)}) collective-permute-start(f32[200,128]{1,0:T(8,128)S(1)} %shard_map.98.here), channel_id=1, source_target_pairs={{0,2},{2,0},{1,3},{3,1},{4,6},{6,4},{5,7},{7,5},{8,10},{10,8},{9,1... | collective-permute-start | bytes 307208 | tf_op jit(solution)/shard_map/ppermute | solution.py:534
  25.1 3.5 %collective-permute-done.7.there = f32[200,128]{1,0:T(8,128)S(1)} collective-permute-done((f32[200,128]{1,0:T(8,128)S(1)}, f32[200,128]{1,0:T(8,128)S(1)}, u32[]{:S(2)}, u32[]{:S(2)}) %collective-permute-start.7) | collective-permute-done | bytes 102432 | tf_op jit(solution)/shard_map/ppermute | solution.py:534
  28.6 0.8 %shard_map.99 = (f32[8,8,1,128]{3,2,1,0:T(1,128)S(1)}, f32[8,8,512]{2,1,0:T(8,128)}) custom-call(s32[2,1,512]{2,1,0:T(1,128)S(1)} %copy-done.3, s32[1,512]{1,0:T(1,128)S(1)} %copy-done.4, f32[8,128,256]{2,1,0:T(8,128)S(1)} %shard_map.95.coherent, f32[128,256]{1,0:T(8,128)S(1)} %get-tuple-element.12.jones.before, f32[200,128]{1,0:T(8,128)S(1)} %shard_map.98.here, ...), custom_call_target="tpu_custom_call" | custom-call | tf_op jit(solution)/shard_map/pallas_call | solution.py:519
  29.3 0.0 collective-permute-start.8
  29.4 1.2 %collective-permute-done.8 = f32[8,8,1,128]{3,2,1,0:T(1,128)S(1)} collective-permute-done((f32[8,8,1,128]{3,2,1,0:T(1,128)S(1)}, f32[8,8,1,128]{3,2,1,0:T(1,128)S(1)}, u32[]{:S(2)}, u32[]{:S(2)}) %collective-permute-start.8) | collective-permute-done | bytes 32800 | tf_op jit(solution)/shard_map/ppermute | solution.py:534
  30.6 0.6 %broadcast_select_fusion = f32[8,1,8,128]{3,2,1,0:T(8,128)} fusion(f32[8,1,8,128]{3,2,1,0:T(8,128)S(1)} %bitcast.4, f32[8,1,8,128]{3,2,1,0:T(8,128)S(1)} %bitcast.6, pred[]{:T(512)S(6)} %eq.3), kind=kLoop, calls=%fused_computation | loop fusion | flops 8192 | bytes 98305 | tf_op jit(solution)/shard_map/jit(_where)/select_n | solution.py:630
  (11 shorter events, 0.0 us)
Async XLA Ops:
  0.6 5.8 %copy-start.8 = (s32[256]{0:T(256)S(1)}, s32[256]{0:T(256)}, u32[]{:S(2)}) copy-start(s32[256]{0:T(256)} %param.14) | copy-start | bytes 3076
  0.6 11.7 %collective-permute-start = (f32[8,8,512]{2,1,0:T(8,128)}, f32[8,8,512]{2,1,0:T(8,128)S(1)}, u32[]{:S(2)}, u32[]{:S(2)}) collective-permute-start(f32[8,8,512]{2,1,0:T(8,128)} %own.1), channel_id=1, source_target_pairs={{0,1},{1,0},{2,3},{3,2},{4,5},{5,4},{6,7},{7,6},{8,9},{9,8},{10,11... | collective-permute-start | bytes 393224 | tf_op jit(solution)/shard_map/ppermute | solution.py:534
  1.2 10.0 %collective-permute-start.1 = (f32[8,2,1,512]{3,2,1,0:T(1,128)}, f32[8,2,1,512]{3,2,1,0:T(1,128)S(1)}, u32[]{:S(2)}, u32[]{:S(2)}) collective-permute-start(f32[8,2,1,512]{3,2,1,0:T(1,128)} %s0.5), channel_id=1, source_target_pairs={{0,4},{4,0},{8,12},{12,8},{1,5},{5,1},{9,13},{13,9},{2,6},{6,2},{1... | collective-permute-start | bytes 98312 | tf_op jit(solution)/shard_map/ppermute | solution.py:534
  3.8 7.3 %collective-permute-start.2 = (f32[8,2,1,512]{3,2,1,0:T(1,128)}, f32[8,2,1,512]{3,2,1,0:T(1,128)S(1)}, u32[]{:S(2)}, u32[]{:S(2)}) collective-permute-start(f32[8,2,1,512]{3,2,1,0:T(1,128)} %s0.5), channel_id=1, source_target_pairs={{0,8},{4,12},{8,0},{12,4},{1,9},{5,13},{9,1},{13,5},{2,10},{6,14},... | collective-permute-start | bytes 98312 | tf_op jit(solution)/shard_map/ppermute | solution.py:534
  6.4 5.9 %collective-permute-start.3 = (f32[8,2,1,512]{3,2,1,0:T(1,128)}, f32[8,2,1,512]{3,2,1,0:T(1,128)S(1)}, u32[]{:S(2)}, u32[]{:S(2)}) collective-permute-start(f32[8,2,1,512]{3,2,1,0:T(1,128)} %s0.5), channel_id=1, source_target_pairs={{0,12},{4,8},{8,4},{12,0},{1,13},{5,9},{9,5},{13,1},{2,14},{6,10},... | collective-permute-start | bytes 98312 | tf_op jit(solution)/shard_map/ppermute | solution.py:534
  6.4 0.7 %copy-start.2 = (s32[2,1,512]{2,1,0:T(1,128)S(1)}, s32[2,1,512]{2,1,0:T(1,128)}, u32[]{:S(2)}) copy-start(s32[2,1,512]{2,1,0:T(1,128)} %pairs.7) | copy-start | bytes 12292
  7.1 0.7 %copy-start.5 = (f32[2,512]{1,0:T(2,128)S(1)}, f32[2,512]{1,0:T(2,128)}, u32[]{:S(2)}) copy-start(f32[2,512]{1,0:T(2,128)} %positions.1) | copy-start | bytes 12292
  7.8 0.7 %copy-start.6 = (f32[4,256]{1,0:T(4,128)S(1)}, f32[4,256]{1,0:T(4,128)}, u32[]{:S(2)}) copy-start(f32[4,256]{1,0:T(4,128)} %brightness.1) | copy-start | bytes 12292
  8.5 0.7 %copy-start.7 = (f32[2,256]{1,0:T(2,128)S(1)}, f32[2,256]{1,0:T(2,128)}, u32[]{:S(2)}) copy-start(f32[2,256]{1,0:T(2,128)} %offsets.1) | copy-start | bytes 6148
  9.2 3.2 %copy-start = (f32[8,2,1,512]{3,2,1,0:T(1,128)S(1)}, f32[8,2,1,512]{3,2,1,0:T(1,128)}, u32[]{:S(2)}) copy-start(f32[8,2,1,512]{3,2,1,0:T(1,128)} %s0.5) | copy-start | bytes 98308
  9.2 3.2 %copy-start.1 = (f32[8,8,512]{2,1,0:T(8,128)S(1)}, f32[8,8,512]{2,1,0:T(8,128)}, u32[]{:S(2)}) copy-start(f32[8,8,512]{2,1,0:T(8,128)} %own.1) | copy-start | bytes 393220
  9.2 3.2 %copy-start.4 = (s32[1,512]{1,0:T(1,128)S(1)}, s32[1,512]{1,0:T(1,128)}, u32[]{:S(2)}) copy-start(s32[1,512]{1,0:T(1,128)} %mask.5) | copy-start | bytes 6148
  14.6 1.3 %collective-permute-start.4 = (f32[72,128]{1,0:T(8,128)S(1)}, f32[72,128]{1,0:T(8,128)S(1)}, u32[]{:S(2)}, u32[]{:S(2)}) collective-permute-start(f32[72,128]{1,0:T(8,128)S(1)} %get-tuple-element.11), channel_id=1, source_target_pairs={{0,1},{1,0},{2,3},{3,2},{4,5},{5,4},{6,7},{7,6},{8,9},{9,8},{10,11... | collective-permute-start | bytes 110600 | tf_op jit(solution)/shard_map/ppermute | solution.py:534
  15.9 4.0 %collective-permute-start.5 = (f32[72,128]{1,0:T(8,128)S(1)}, f32[72,128]{1,0:T(8,128)S(1)}, u32[]{:S(2)}, u32[]{:S(2)}) collective-permute-start(f32[72,128]{1,0:T(8,128)S(1)} %add.4.sum_here), channel_id=1, source_target_pairs={{0,2},{2,0},{1,3},{3,1},{4,6},{6,4},{5,7},{7,5},{8,10},{10,8},{9,1... | collective-permute-start | bytes 110600 | tf_op jit(solution)/shard_map/ppermute | solution.py:534
  22.2 1.3 %collective-permute-start.6 = (f32[136,128]{1,0:T(8,128)S(1)}, f32[136,128]{1,0:T(8,128)S(1)}, u32[]{:S(2)}, u32[]{:S(2)}) collective-permute-start(f32[136,128]{1,0:T(8,128)S(1)} %get-tuple-element.13.here), channel_id=1, source_target_pairs={{0,1},{1,0},{2,3},{3,2},{4,5},{5,4},{6,7},{7,6},{8,9},{9,8},{10,11... | collective-permute-start | bytes 208904 | tf_op jit(solution)/shard_map/ppermute | solution.py:534
  23.5 5.0 %copy-start.3 = (s32[2,1,512]{2,1,0:T(1,128)S(1)}, s32[2,1,512]{2,1,0:T(1,128)}, u32[]{:S(2)}) copy-start(s32[2,1,512]{2,1,0:T(1,128)} %pairs.7) | copy-start | bytes 12292
  23.6 5.0 %collective-permute-start.7 = (f32[200,128]{1,0:T(8,128)S(1)}, f32[200,128]{1,0:T(8,128)S(1)}, u32[]{:S(2)}, u32[]{:S(2)}) collective-permute-start(f32[200,128]{1,0:T(8,128)S(1)} %shard_map.98.here), channel_id=1, source_target_pairs={{0,2},{2,0},{1,3},{3,1},{4,6},{6,4},{5,7},{7,5},{8,10},{10,8},{9,1... | collective-permute-start | bytes 307208 | tf_op jit(solution)/shard_map/ppermute | solution.py:534
  29.3 1.2 %collective-permute-start.8 = (f32[8,8,1,128]{3,2,1,0:T(1,128)S(1)}, f32[8,8,1,128]{3,2,1,0:T(1,128)S(1)}, u32[]{:S(2)}, u32[]{:S(2)}) collective-permute-start(f32[8,8,1,128]{3,2,1,0:T(1,128)S(1)} %get-tuple-element.14), channel_id=1, source_target_pairs={{0,1},{1,0},{2,3},{3,2},{4,5},{5,4},{6,7},{7,6},{8,9},{9,8},{10,11... | collective-permute-start | bytes 98312 | tf_op jit(solution)/shard_map/ppermute | solution.py:534

commit v2 on v0

--- a/solution.py
+++ b/solution.py
@@ -1,8 +1,11 @@
+import functools
 import math
 
 import jax
 import jax.numpy as jnp
 from jax import lax
+from jax.experimental import pallas as pl
+from jax.experimental.pallas import tpu as pltpu
 from jax.sharding import PartitionSpec as P
 
 ITERS = 2
@@ -175,6 +178,623 @@
     return (residual_now[:, :, None, :], gains_now)
 
 
+COS_TERMS = (
+    0.9999999890590228,
+    -19.739204499454,
+    64.93911745989914,
+    -85.45013953093448,
+    60.16763095128989,
+    -25.96759924954187,
+    6.528658162606979,
+)
+SIN_TERMS = (
+    6.283185302511502,
+    -41.34170040531754,
+    81.6051313857969,
+    -76.70301535383193,
+    42.02592698564183,
+    -14.899846667160109,
+    3.2381375090822355,
+)
+RUN = 128
+BLOCK = 64
+BLOCKS = 8
+PAIR = 2 * RUN
+
+
+def pieces(value, count):
+    result = []
+    for index in range(count):
+        piece = value.astype(jnp.bfloat16)
+        result.append(piece)
+        if index < count - 1:
+            value = value - piece.astype(jnp.float32)
+    return result
+
+
+def dot_f32(left, right, contract_right=0):
+    return lax.dot_general(
+        left,
+        right,
+        (((1,), (contract_right,)), ((), ())),
+        preferred_element_type=jnp.float32,
+    )
+
+
+def horner(terms, x):
+    total = jnp.full_like(x, terms[-1])
+    for term in terms[-2::-1]:
+        total = total * x + term
+    return total
+
+
+def turn_pair(turns):
+    rest = turns - jnp.round(turns)
+    square = rest * rest
+    return horner(COS_TERMS, square), horner([-term for term in SIN_TERMS], square) * rest
+
+
+def product(a, b, dagger_a=False, dagger_b=False, total=None):
+    result = [None] * 8 if total is None else list(total)
+
+    def add(n, x, y, positive):
+        term = x * y
+        if result[n] is None:
+            result[n] = term if positive else -term
+        else:
+            result[n] = result[n] + term if positive else result[n] - term
+
+    for row in (0, 1):
+        for col in (0, 1):
+            n = 2 * row + col
+            for inner in (0, 1):
+                i = 2 * inner + row if dagger_a else 2 * row + inner
+                j = 2 * col + inner if dagger_b else 2 * inner + col
+                add(n, a[i], b[j], True)
+                add(n, a[4 + i], b[4 + j], dagger_a != dagger_b)
+                if dagger_a:
+                    add(4 + n, a[i], b[4 + j], not dagger_b)
+                    add(4 + n, a[4 + i], b[j], False)
+                else:
+                    add(4 + n, a[4 + i], b[j], True)
+                    add(4 + n, a[i], b[4 + j], not dagger_b)
+    return result
+
+
+def sum_rows(parts):
+    row = lax.broadcasted_iota(jnp.int32, parts[0].shape, 0)
+    low = row < 4
+    parts = [
+        jnp.where(low, a, b) + pltpu.roll(jnp.where(low, b, a), 4, 0)
+        for a, b in zip(parts[:4], parts[4:])
+    ]
+    for step in (2, 1):
+        low = jnp.bitwise_and(row, step) == 0
+        parts = [
+            jnp.where(low, a + pltpu.roll(a, 8 - step, 0), b + pltpu.roll(b, step, 0))
+            for a, b in zip(parts[:step], parts[step:])
+        ]
+    return parts[0]
+
+
+class Place:
+    def __init__(self):
+        self.chan = lax.axis_index("chan")
+        self.core = lax.axis_index("dir")
+        self.blk = lax.axis_index("blk")
+        self.first_lane = pl.multiple_of(self.core * PAIR, PAIR)
+        self.last_core = self.chan // 2
+        self.last_lane = pl.multiple_of(self.chan * RUN, RUN)
+
+    def first_station(self, core):
+        return pl.multiple_of((2 * self.blk + core) * RUN, RUN)
+
+    def slot(self, channel, per_shard):
+        return jnp.bitwise_xor(channel // per_shard, self.chan) * per_shard + channel % per_shard
+
+
+def onehot(station, first_station):
+    local = jnp.where(station < BLOCK, station, station - first_station + RUN)
+    rows = lax.broadcasted_iota(jnp.int32, (2 * RUN, station.shape[1]), 0)
+    return jnp.where(rows == local, 1.0, 0.0).astype(jnp.bfloat16)
+
+
+def split_rows(value, count):
+    split = [p.astype(jnp.float32) for p in pieces(value, count)]
+    missing = -count * value.shape[0] % 16
+    if missing:
+        split.append(jnp.zeros((missing, value.shape[1]), jnp.float32))
+    return jnp.concatenate(split).astype(jnp.bfloat16)
+
+
+def grams(coh):
+    re, im = coh[:4], coh[4:]
+    size = [a * a + b * b for a, b in zip(re, im)]
+
+    def cross(i, j, k, l):
+        real = re[i] * re[j] + im[i] * im[j] + re[k] * re[l] + im[k] * im[l]
+        imag = re[i] * im[j] - im[i] * re[j] + re[k] * im[l] - im[k] * re[l]
+        return [real + real, imag + imag]
+
+    inner = [size[0] + size[2], size[1] + size[3]] + cross(0, 1, 2, 3)
+    outer = [size[0] + size[1], size[2] + size[3]] + cross(2, 0, 3, 1)
+    return inner + outer
+
+
+def curvature_of(gain, gram):
+    re, im = gain[:4], gain[4:]
+    size = [a * a + b * b for a, b in zip(re, im)]
+    real = re[0] * re[1] + im[0] * im[1] + re[2] * re[3] + im[2] * im[3]
+    imag = im[0] * re[1] - re[0] * im[1] + im[2] * re[3] - re[2] * im[3]
+    total = (size[0] + size[2]) * gram[0] + (size[1] + size[3]) * gram[1] + real * gram[2] - imag * gram[3]
+    return jnp.maximum(total, 0.0)
+
+
+def coherency_kernel(
+    channels, per_shard, pairs_at, positions_at, offsets_at, brightness_at, cluster_at, mask_at, seen_at, jones_at,
+    out, last_out, gram, hots, last_hots, mask, seen, jones,
+    pairs, positions, offsets, brightness, cluster, base, spin, parts, last_parts, sems,
+):
+    copies = [
+        pltpu.make_async_copy(source, target, sems.at[index])
+        for index, (source, target) in enumerate(
+            (
+                (pairs_at, pairs),
+                (positions_at, positions),
+                (offsets_at, offsets),
+                (brightness_at, brightness),
+                (cluster_at, cluster),
+                (mask_at, mask),
+                (seen_at, seen),
+                (jones_at, jones),
+            )
+        )
+    ]
+    for copy in copies:
+        copy.start()
+    for copy in copies[:5]:
+        copy.wait()
+    place = Place()
+    spans = []
+    for hot_ref, lanes, core in (
+        (hots, pl.ds(place.first_lane, PAIR), place.core),
+        (last_hots, pl.ds(place.last_lane, RUN), place.last_core),
+    ):
+        first_station = place.first_station(core)
+        table = jnp.concatenate([positions[:, 0:RUN], positions[:, pl.ds(first_station, RUN)]], axis=1)
+        table = split_rows(table, 3)
+        there = []
+        for side in (0, 1):
+            hot_ref[side] = onehot(pairs[side, :, lanes], first_station)
+            found = dot_f32(table, hot_ref[side])
+            there.append(found[0:2] + found[2:4] + found[4:6])
+        spans.append(there[0] - there[1])
+    span = jnp.concatenate(spans, axis=1)
+    sources = offsets.shape[1]
+    columns = jnp.transpose(jnp.concatenate([offsets[...], jnp.zeros((6, sources))]))
+    step = 16
+    for start in range(0, sources, step):
+        rows = slice(start, start + step)
+        geometry = columns[rows, 0:1] * span[0:1] + columns[rows, 1:2] * span[1:2]
+        base[0, rows], base[1, rows] = turn_pair(geometry)
+        spin[0, rows], spin[1, rows] = turn_pair(geometry * (0.5 / channels))
+
+    directions = out.shape[1] // 12
+    member = lax.broadcasted_iota(jnp.int32, (directions, sources), 0) == cluster[...]
+    bright = jnp.concatenate([jnp.where(member, brightness[n : n + 1], 0.0) for n in range(4)])
+    high, low = pieces(bright, 2)
+    both = jnp.concatenate([high, low])
+    half = 4 * directions
+
+    def table_times(refs):
+        wide = dot_f32(both, refs[0])
+        return wide[:half] + wide[half:] + dot_f32(high, refs[1])
+
+    for channel in range(channels):
+        odd = channel % 2
+        for start in range(0, sources, step):
+            rows = slice(start, start + step)
+            c, s = base[0, rows], base[1, rows]
+            for index, value in enumerate((c, s)):
+                for size, piece in enumerate(pieces(value, 2)):
+                    parts[odd, index, size, rows] = piece[:, :PAIR]
+                    last_parts[index, size, rows, odd * RUN : (odd + 1) * RUN] = piece[:, PAIR:]
+            if channel < channels - 1:
+                dc, ds = spin[0, rows], spin[1, rows]
+                base[0, rows] = c * dc - s * ds
+                base[1, rows] = s * dc + c * ds
+        slot = place.slot(channel, per_shard)
+        found = [table_times((parts[odd, index, 0], parts[odd, index, 1])) for index in (0, 1)]
+        out[slot, :half] = found[0]
+        out[slot, half : 2 * half] = found[1]
+        out[slot, 2 * half :] = found[0] - found[1]
+        entries = [found[n // 4][n % 4 * directions : (n % 4 + 1) * directions] for n in range(8)]
+        for n, value in enumerate(grams(entries)):
+            rows = slice(n * directions, (n + 1) * directions)
+            gram[rows] = value if channel == 0 else gram[rows] + value
+        if odd:
+            for index in (0, 1):
+                found = table_times((last_parts[index, 0], last_parts[index, 1]))
+                for before in (0, 1):
+                    slot = place.slot(channel - 1 + before, per_shard)
+                    last_out[slot, half * index : half * (index + 1)] = found[:, before * RUN : (before + 1) * RUN]
+    for copy in copies[5:]:
+        copy.wait()
+
+
+def gather_gains(table, hots, gather):
+    rows = table.shape[0]
+    split = jnp.concatenate(pieces(table, 2))
+    for side in (0, 1):
+        found = dot_f32(split, hots[side])
+        found = found[:rows] + found[rows:]
+        for run in range(found.shape[1] // RUN):
+            gather[side, run] = found[:, run * RUN : (run + 1) * RUN]
+
+
+def gains_of(gather, side, run, h):
+    return [gather[side, run, pl.ds(64 * h + n, 8, stride=8), :] for n in range(8)]
+
+
+def coherent_of(coherent, channel, h, lanes, directions, count):
+    return [
+        coherent[channel, n * directions + 8 * h : n * directions + 8 * h + 8, lanes] for n in range(count)
+    ]
+
+
+def small_product(a, b, turned=False):
+    order = ((0, 1), (2, 3)) if turned else ((0, 2), (1, 3))
+    return [
+        a[2 * row] * b[order[col][0]] + a[2 * row + 1] * b[order[col][1]] for row in (0, 1) for col in (0, 1)
+    ]
+
+
+def less(a, b):
+    return [x - y for x, y in zip(a, b)]
+
+
+def plus(a, b):
+    return [x + y for x, y in zip(a, b)]
+
+
+def model_parts(first, second, coh):
+    re, im, mixed = coh[:4], coh[4:8], coh[8:]
+    p1 = small_product(first[:4], re)
+    p2 = small_product(first[4:8], im)
+    p3 = small_product(first[8:], mixed)
+    zr = less(p1, p2)
+    zi = less(plus(p1, p2), p3)
+    return (
+        small_product(zr, second[:4], True)
+        + small_product(zi, second[4:8], True)
+        + small_product(plus(zr, zi), second[8:], True)
+    )
+
+
+def model_of(parts):
+    a, b, d = parts[:4], parts[4:8], parts[8:]
+    return plus(a, b) + plus(less(d, a), b)
+
+
+def with_difference(matrix):
+    return matrix + less(matrix[:4], matrix[4:])
+
+
+def multiply_into(total, a, b, conj_b=False):
+    real = a[0] * b[0]
+    imag = a[1] * b[0]
+    if total is not None:
+        real, imag = total[0] + real, total[1] + imag
+    if conj_b:
+        return real + a[1] * b[1], imag - a[0] * b[1]
+    return real - a[1] * b[1], imag + a[0] * b[1]
+
+
+def iterate(place, coherent, gram, hots, shards, mask, jones, model, error, gather, sums):
+    rows = jones.shape[0]
+    directions = rows // 8
+    halves = rows // 64
+    gather_gains(jones[...], hots, gather)
+    weight = mask[:, pl.ds(place.first_lane, PAIR)].astype(jnp.float32)
+    channels = coherent.shape[0]
+    per_shard = shards[0].shape[1]
+    for run in range(2):
+        lanes = slice(run * RUN, (run + 1) * RUN)
+        w = weight[:, lanes]
+        at = pl.multiple_of(place.first_lane + run * RUN, RUN)
+        for h in range(halves):
+            first_gain = with_difference(gains_of(gather, 0, run, h))
+            second_gain = with_difference(gains_of(gather, 1, run, h))
+            for channel in range(channels):
+                coh = coherent_of(coherent, channel, h, lanes, directions, 12)
+                part = model_parts(first_gain, second_gain, coh)
+                if h > 0:
+                    part = [a + model[channel, n] for n, a in enumerate(part)]
+                if h < halves - 1:
+                    for n in range(12):
+                        model[channel, n] = part[n]
+                else:
+                    seen = shards[channel // per_shard][:, channel % per_shard, 0, pl.ds(at, RUN)]
+                    err = w * (seen - sum_rows(model_of(part)))
+                    error[channel, 0] = err
+                    error[channel, 1] = err + pltpu.roll(err, 4, 0)
+
+        for h in range(halves):
+            first_gain, second_gain = gains_of(gather, 0, run, h), gains_of(gather, 1, run, h)
+            second = [None] * 4
+            for i in (0, 1):
+                zero = jnp.zeros((8, RUN), jnp.float32)
+                p1, p2, p3 = [zero] * 8, [zero] * 8, [zero] * 8
+                for channel in range(channels):
+                    coh = coherent_of(coherent, channel, h, lanes, directions, 12)
+
+                    def err(tile, n):
+                        return jnp.broadcast_to(error[channel, tile, n : n + 1], (8, RUN))
+
+                    for j in (0, 1):
+                        er, ei, es = err(0, 2 * i + j), err(0, 4 + 2 * i + j), err(1, 2 * i + j)
+                        for kl in range(4):
+                            n = 4 * j + kl
+                            p1[n] = p1[n] + er * coh[kl]
+                            p2[n] = p2[n] + ei * coh[4 + kl]
+                            p3[n] = p3[n] + es * coh[8 + kl]
+                outer = list(zip(plus(p1, p2), plus(less(p3, p1), p2)))
+                for l in (0, 1):
+                    total = None
+                    for j in (0, 1):
+                        for k in (0, 1):
+                            g = (second_gain[2 * j + k], second_gain[4 + 2 * j + k])
+                            total = multiply_into(total, outer[4 * j + 2 * l + k], g)
+                    for imag in (0, 1):
+                        n = 4 * imag + 2 * i + l
+                        sums[0, run, pl.ds(64 * h + n, 8, stride=8), :] = total[imag]
+                for a in (0, 1):
+                    for l in (0, 1):
+                        for k in (0, 1):
+                            g = (first_gain[2 * i + k], first_gain[4 + 2 * i + k])
+                            second[2 * a + l] = multiply_into(
+                                second[2 * a + l], g, outer[4 * a + 2 * k + l], conj_b=True
+                            )
+            for n in range(8):
+                sums[1, run, pl.ds(64 * h + n, 8, stride=8), :] = second[n % 4][n // 4]
+            form = [gram[n * directions + 8 * h : n * directions + 8 * h + 8, lanes] for n in range(8)]
+            sums[0, run, rows + 8 * h : rows + 8 * h + 8] = w * curvature_of(second_gain, form[:4])
+            sums[1, run, rows + 8 * h : rows + 8 * h + 8] = w * curvature_of(first_gain, form[4:])
+
+    total = None
+    height = sums.shape[2]
+    for side in (0, 1):
+        whole = jnp.concatenate([sums[side, run] for run in range(2)], axis=1)
+        found = dot_f32(jnp.concatenate(pieces(whole, 2)), hots[side], 1)
+        found = found[:height] + found[height:]
+        total = found if total is None else total + found
+    return total
+
+
+def pack(total, rows):
+    half = rows // 2
+    low = jnp.concatenate([total[:half], total[rows : rows + half // 8]])
+    high = jnp.concatenate([total[half:rows], total[rows + half // 8 :]])
+    lane = lax.broadcasted_iota(jnp.int32, low.shape, 1)
+    return jnp.where(lane < BLOCK, low, pltpu.roll(high, BLOCK, 1))
+
+
+def unpack(packed):
+    half = packed.shape[0] * 8 // 9
+    turned = pltpu.roll(packed, BLOCK, 1)
+    return jnp.concatenate([packed[:half], turned[:half], packed[half:], turned[half:]])
+
+
+def update(jones, lanes, sums, keep=None):
+    rows = jones.shape[0]
+    for d in range(rows // 8):
+        now = jones[8 * d : 8 * d + 8, lanes]
+        ratio = STEP_SIZE / (sums[rows + d : rows + d + 1] + EPSILON)
+        new = now + ratio * sums[8 * d : 8 * d + 8]
+        if keep is not None:
+            new = jnp.where(keep, new, now)
+        jones[8 * d : 8 * d + 8, lanes] = new
+
+
+def block_zero():
+    return lax.broadcasted_iota(jnp.int32, (8, RUN), 1) < BLOCK
+
+
+def first_kernel(
+    mask, coherent, gram, hots, own, other, s0, s1, s2, s3, packed, mine, jones, model, error, gather, sums
+):
+    place = Place()
+    count = own.shape[0] * own.shape[1]
+    for ref, core in ((own, place.core), (other, 1 - place.core)):
+        at = pl.ds(pl.multiple_of(core * count, count), count)
+        jones[at, 0:RUN] = ref[:, :, 0:RUN].reshape(count, RUN)
+        window = ref[:, :, pl.ds(place.first_station(place.core), RUN)]
+        jones[at, RUN:] = window.reshape(count, RUN)
+    total = iterate(
+        place, coherent, gram, hots, (s0, s1, s2, s3), mask, jones, model, error, gather, sums
+    )
+    packed[...] = pack(total[:, :RUN], jones.shape[0])
+    mine[...] = total[:, RUN:]
+
+
+def second_kernel(
+    mask, coherent, gram, hots, before, mine, sum_here, sum_there, s0, s1, s2, s3,
+    packed, jones, model, error, gather, sums,
+):
+    place = Place()
+    jones[...] = before[...]
+    update(jones, slice(0, RUN), unpack(sum_here[...] + sum_there[...]), block_zero())
+    update(jones, slice(RUN, None), mine[...])
+    total = iterate(
+        place, coherent, gram, hots, (s0, s1, s2, s3), mask, jones, model, error, gather, sums
+    )
+    rows = jones.shape[0]
+    held = packed.shape[0] - rows
+    packed[:held] = pack(total[:, :RUN], rows)
+    update(jones, slice(RUN, None), total[:, RUN:])
+    packed[held:] = jones[:, RUN:]
+
+
+def join_kernel(here, there, out):
+    half = here.shape[0] * 8 // 25
+    held = here.shape[0] - 2 * half
+    at = pl.ds(pl.multiple_of(held + lax.axis_index("dir") * half, 8), half)
+    out[:held] = here[:held] + there[:held]
+    out[held : held + half] = here[at]
+    out[held + half :] = there[at]
+
+
+def last_kernel(
+    mask, coherent, hots, before, mine, other, here, there, s0, s1, s2, s3, residual, solved, jones, gather
+):
+    place = Place()
+    rows = before.shape[0]
+    half = rows // 2
+    held = here.shape[0] - rows
+    own_core_last = place.last_core == place.core
+    jones[:, 0:RUN] = before[:, 0:RUN]
+    jones[:, RUN:] = jnp.where(own_core_last, mine[held:], other[held:])
+    update(jones, slice(0, RUN), unpack(here[:held] + there[:held]), block_zero())
+
+    for ref, blk in ((here, place.blk), (there, 1 - place.blk)):
+        for at, core in ((held, place.core), (held + half, 1 - place.core)):
+            lanes = pl.ds(pl.multiple_of((2 * blk + core) * RUN, RUN), RUN)
+            solved[:, :, lanes] = ref[at : at + half].reshape(half // 8, 8, RUN)
+    zero = jones[pl.ds(pl.multiple_of(place.core * half, half), half), 0:RUN].reshape(half // 8, 8, RUN)
+    lane = lax.broadcasted_iota(jnp.int32, zero.shape, 2)
+    solved[:, :, 0:RUN] = jnp.where(lane < BLOCK, zero, solved[:, :, 0:RUN])
+
+    gather_gains(jones[...], hots, gather)
+    w = mask[:, pl.ds(place.last_lane, RUN)].astype(jnp.float32)
+    shards = (s0, s1, s2, s3)
+    channels = coherent.shape[0]
+    per_shard = s0.shape[1]
+    gains = [[gains_of(gather, side, 0, h) for h in range(rows // 64)] for side in (0, 1)]
+    for channel in range(channels):
+        part = None
+        for h in range(rows // 64):
+            coh = coherent_of(coherent, channel, h, slice(0, RUN), rows // 8, 8)
+            z = product(gains[0][h], coh)
+            part = product(z, gains[1][h], dagger_b=True, total=part)
+        seen = shards[channel // per_shard][:, channel % per_shard, 0, pl.ds(place.last_lane, RUN)]
+        residual[:, place.slot(channel, per_shard), 0] = w * (seen - sum_rows(part))
+
+
+def call(kernel, out_shape, scratch, operands, space=pltpu.VMEM):
+    return pl.pallas_call(
+        kernel,
+        out_shape=out_shape,
+        in_specs=[pl.BlockSpec(memory_space=space)] * len(operands),
+        out_specs=jax.tree.map(lambda _: pl.BlockSpec(memory_space=pltpu.VMEM), out_shape),
+        scratch_shapes=scratch,
+        compiler_params=pltpu.CompilerParams(vmem_limit_bytes=40 << 20),
+    )(*[pltpu.with_memory_space_constraint(x, space) for x in operands])
+
+
+def f32(*shape):
+    return jax.ShapeDtypeStruct(shape, jnp.float32)
+
+
+def bf16(*shape):
+    return jax.ShapeDtypeStruct(shape, jnp.bfloat16)
+
+
+def swap(x, axis, bit=1):
+    return lax.ppermute(x, axis, [(i, i ^ bit) for i in range(lax.axis_size(axis))])
+
+
+def per_device_owned(
+    visibilities,
+    antenna_pairs,
+    valid_mask,
+    station_positions,
+    source_offsets,
+    brightness,
+    source_cluster,
+    jones_gains,
+):
+    relay_count = lax.axis_size("chan")
+    per_shard = visibilities.shape[1]
+    channels = per_shard * relay_count
+    half_directions = jones_gains.shape[0]
+    directions = 2 * half_directions
+    rows = 8 * directions
+    sources = source_offsets.shape[1]
+
+    other = swap(jones_gains, "dir")
+    shards = [swap(visibilities, "chan", bit) for bit in range(1, relay_count)]
+    kept = (valid_mask, visibilities, jones_gains)
+    inputs = (antenna_pairs, station_positions, source_offsets, brightness, source_cluster[None, :])
+    coherent, last_coherent, gram, hots, last_hots, mask, seen, own = call(
+        functools.partial(coherency_kernel, channels, per_shard),
+        (
+            f32(channels, 12 * directions, PAIR),
+            f32(channels, 8 * directions, RUN),
+            f32(8 * directions, PAIR),
+            bf16(2, 2 * RUN, PAIR),
+            bf16(2, 2 * RUN, RUN),
+            *[jax.ShapeDtypeStruct(x.shape, x.dtype) for x in kept],
+        ),
+        [pltpu.VMEM(x.shape, x.dtype) for x in inputs]
+        + [
+            pltpu.VMEM((2, sources, PAIR + RUN), jnp.float32),
+            pltpu.VMEM((2, sources, PAIR + RUN), jnp.float32),
+            pltpu.VMEM((2, 2, 2, sources, PAIR), jnp.bfloat16),
+            pltpu.VMEM((2, 2, sources, 2 * RUN), jnp.bfloat16),
+            pltpu.SemaphoreType.DMA((len(inputs + kept),)),
+        ],
+        inputs + kept,
+        pltpu.HBM,
+    )
+    shards = [seen] + shards
+    scratch = [
+        pltpu.VMEM((channels, 12, 8, RUN), jnp.float32),
+        pltpu.VMEM((channels, 2, 8, RUN), jnp.float32),
+        pltpu.VMEM((2, 2, rows, RUN), jnp.float32),
+        pltpu.VMEM((2, 2, rows + directions, RUN), jnp.float32),
+    ]
+    table = f32(rows, 2 * RUN)
+    held = (rows + directions) // 2
+    packed, mine, jones = call(
+        first_kernel,
+        (f32(held, RUN), f32(rows + directions, RUN), table),
+        scratch,
+        (mask, coherent, gram, hots, own, other, *shards),
+    )
+    packed = packed + swap(packed, "dir")
+    there = swap(packed, "blk")
+    mine, jones = call(
+        second_kernel,
+        (f32(held + rows, RUN), table),
+        scratch,
+        (mask, coherent, gram, hots, jones, mine, packed, there, *shards),
+    )
+    other = swap(mine, "dir")
+    joined = call(join_kernel, f32(held + rows, RUN), [], (mine, other))
+    return call(
+        last_kernel,
+        (f32(8, channels, 1, RUN), f32(half_directions, 8, station_positions.shape[1])),
+        [pltpu.VMEM((rows, 2 * RUN), jnp.float32), pltpu.VMEM((2, 1, rows, RUN), jnp.float32)],
+        (mask, last_coherent, last_hots, jones, mine, other, joined, swap(joined, "blk"), *shards),
+    )
+
+
+def owned_layout(mesh, shapes):
+    sizes = mesh.shape
+    owners = sizes["chan"] * sizes["blk"]
+    visibilities, pairs, jones = shapes
+    return (
+        owners == BLOCKS
+        and sizes["blk"] == 2
+        and sizes["dir"] == 2
+        and sizes["chan"] == 4
+        and pairs[1] * pairs[2] == owners * RUN
+        and jones[0] == 16
+        and jones[2] == BLOCKS * BLOCK
+        and visibilities[1] % sizes["chan"] == 0
+    )
+
+
 def solution(mesh):
     in_specs = (
         P("groups", "chan", "blk", None),
@@ -187,6 +807,12 @@
         P("dir", "groups", None),
     )
     out_specs = (P("groups", None, "blk", "chan"), P("dir", "groups", None))
-    return jax.shard_map(
-        per_device, mesh=mesh, in_specs=in_specs, out_specs=out_specs, check_vma=False
-    )
+
+    def run(*arrays):
+        owned = owned_layout(mesh, (arrays[0].shape, arrays[1].shape, arrays[7].shape))
+        body = per_device_owned if owned else per_device
+        return jax.shard_map(
+            body, mesh=mesh, in_specs=in_specs, out_specs=out_specs, check_vma=False
+        )(*arrays)
+
+    return run

time: 312 us -> 28.3 us (0.09)
  waiting for transfers between devices: 134 us -> 9.47 us
  blocking collectives: 83.7 us -> 0 us
  local copies, waits for them, and re-layouts: 50.7 us -> 0 us
  other arithmetic: 15.7 us -> 0.01 us
  between operations: 15.3 us -> 0.68 us
  Pallas kernels: 0 us -> 9.06 us
  matrix products: 5.15 us -> 0 us
    psum x2 -> x0, waiting for transfers between devices: 134 us -> none  [per_device(): lax.psum((grad_station, curv_station), ('chan', 'blk'))]
    psum x5 -> x0, blocking collectives: 83.7 us -> none  [the longest x2 73 us: per_device(): lax.psum((grad_station, curv_station), ('chan', 'blk'))]
    slice x47 -> x0, local copies, waits for them, and re-layouts: 32.1 us -> none  [the longest x9 10.5 us: jones_product(): former[2 * row_number] * latter[column]]
    gather x11 -> x0, local copies, waits for them, and re-layouts: 11 us -> none  [the longest x3 3.19 us: station_gains(): jnp.take(gains_current, first_station, axis=2).transpose(1, 0, 2)]
    ppermute x0 -> x8, waiting for transfers between devices: none -> 9.47 us  [swap(): lax.ppermute(x, axis, [(i, i ^ bit) for i in range(lax.axis_size(axis))])]
    pallas_call x0 -> x5, Pallas kernels: none -> 9.06 us  [call(): pl.pallas_call(kernel, out_shape=out_shape, in_specs=[pl.BlockSpec(memory...]
    ppermute x0 -> x8, starting transfers between devices: none -> 8.94 us  [swap(): lax.ppermute(x, axis, [(i, i ^ bit) for i in range(lax.axis_size(axis))])]
    all_to_all x1 -> x0, starting transfers between devices: 6.32 us -> none  [per_device(): lax.all_to_all(visibilities, 'chan', split_axis=3, concat_axis=1, tiled=T...]
  transfers between devices with their start and end apart: 3 -> 8, of which waited for: 2 -> 5; matrix products, arithmetic and copies ran while one was open for 10% -> 0% of each run, Pallas kernels for 0% -> 15%
where the time goes in v2:
time: 28.3 us; the launch traced here: 28.2 us
  waiting for transfers between devices  9.47 us (33%)
  Pallas kernels  9.06 us (32%)
  starting transfers between devices  8.94 us (32%)
  between operations  0.68 us (2%)
    ppermute x8, waiting for transfers between devices, swap(): lax.ppermute(x, axis, [(i, i ^ bit) for i in range(lax.axis_size(axis))])  9.47 us
    pallas_call x5, Pallas kernels, call(): pl.pallas_call(kernel, out_shape=out_shape, in_specs=[pl.BlockSpec(memory...  9.06 us
    ppermute x8, starting transfers between devices, swap(): lax.ppermute(x, axis, [(i, i ^ bit) for i in range(lax.axis_size(axis))])  8.94 us
  transfers between devices with their start and end apart: 8, of which 5 were waited for; matrix products, arithmetic and copies ran while one was open for 0% of the time, Pallas kernels for 15%

profile of v2, /device:TPU:0, one launch (start us, length us, event | category | flops | bytes accessed | tf_op | source)
XLA Modules:
  0.0 28.2 jit_solution(7544702104638336429)
XLA Ops:
  0.6 0.5 %collective-permute-start = (f32[8,8,512]{2,1,0:T(8,128)}, f32[8,8,512]{2,1,0:T(8,128)S(1)}, u32[]{:S(2)}, u32[]{:S(2)}) collective-permute-start(f32[8,8,512]{2,1,0:T(8,128)} %jones_at.1), channel_id=1, source_target_pairs={{0,1},{1,0},{2,3},{3,2},{4,5},{5,4},{6,7},{7,6},{8,9},{9,8},{10,11... | collective-permute-start | bytes 393224 | tf_op jit(solution)/shard_map/ppermute | solution.py:703
  1.2 2.6 %collective-permute-start.1 = (f32[8,2,1,512]{3,2,1,0:T(1,128)}, f32[8,2,1,512]{3,2,1,0:T(1,128)S(1)}, u32[]{:S(2)}, u32[]{:S(2)}) collective-permute-start(f32[8,2,1,512]{3,2,1,0:T(1,128)} %seen_at.1), channel_id=1, source_target_pairs={{0,4},{4,0},{8,12},{12,8},{1,5},{5,1},{9,13},{13,9},{2,6},{6,2},{1... | collective-permute-start | bytes 98312 | tf_op jit(solution)/shard_map/ppermute | solution.py:703
  3.8 2.5 %collective-permute-start.3 = (f32[8,2,1,512]{3,2,1,0:T(1,128)}, f32[8,2,1,512]{3,2,1,0:T(1,128)S(1)}, u32[]{:S(2)}, u32[]{:S(2)}) collective-permute-start(f32[8,2,1,512]{3,2,1,0:T(1,128)} %seen_at.1), channel_id=1, source_target_pairs={{0,12},{4,8},{8,4},{12,0},{1,13},{5,9},{9,5},{13,1},{2,14},{6,10},... | collective-permute-start | bytes 98312 | tf_op jit(solution)/shard_map/ppermute | solution.py:703
  6.3 0.1 collective-permute-start.2
  6.4 4.2 %shard_map.95 = (f32[8,192,256]{2,1,0:T(8,128)S(1)}, f32[8,128,128]{2,1,0:T(8,128)S(1)}, f32[128,256]{1,0:T(8,128)S(1)}, bf16[2,256,256]{2,1,0:T(8,128)(2,1)S(1)...) custom-call(s32[2,1,512]{2,1,0:T(1,128)} %pairs_at.1, ...), custom_call_target="tpu_custom_call" | custom-call | tf_op jit(solution)/shard_map/pallas_call | solution.py:684
  10.6 0.0 collective-permute-done.1.s1
  10.6 0.0 collective-permute-done.3.s3
  10.6 1.1 %collective-permute-done.2.s2 = f32[8,2,1,512]{3,2,1,0:T(1,128)S(1)} collective-permute-done((f32[8,2,1,512]{3,2,1,0:T(1,128)}, f32[8,2,1,512]{3,2,1,0:T(1,128)S(1)}, u32[]{:S(2)}, u32[]{:S(2)}) %collective-permute-start.2) | collective-permute-done | bytes 32800 | tf_op jit(solution)/shard_map/ppermute | solution.py:703
  11.7 0.0 collective-permute-done.other
  11.7 1.8 %shard_map.96 = (f32[72,128]{1,0:T(8,128)S(1)}, f32[144,128]{1,0:T(8,128)S(1)}, f32[128,256]{1,0:T(8,128)S(1)}) custom-call(s32[1,512]{1,0:T(1,128)S(1)} %get-tuple-element.15.mask, f32[8,192,256]{2,1,0:T(8,128)S(1)} %get-tuple-element.18.coherent, f32[128,256]{1,0:T(8,128)S(1)} %get-tuple-element.19.gram, bf16[2,256,256]{2,1,0:T(8,128)(2,1)S(1)} %get-tuple-element.20.hots, ...), custom_call_target="tpu_custom_call" | custom-call | tf_op jit(solution)/shard_map/pallas_call | solution.py:684
  13.4 0.1 collective-permute-start.4
  13.5 1.2 %collective-permute-done.4 = f32[72,128]{1,0:T(8,128)S(1)} collective-permute-done((f32[72,128]{1,0:T(8,128)S(1)}, f32[72,128]{1,0:T(8,128)S(1)}, u32[]{:S(2)}, u32[]{:S(2)}) %collective-permute-start.4) | collective-permute-done | bytes 36896 | tf_op jit(solution)/shard_map/ppermute | solution.py:703
  14.7 1.5 %collective-permute-start.5 = (f32[72,128]{1,0:T(8,128)S(1)}, f32[72,128]{1,0:T(8,128)S(1)}, u32[]{:S(2)}, u32[]{:S(2)}) collective-permute-start(f32[72,128]{1,0:T(8,128)S(1)} %add.3.sum_here), channel_id=1, source_target_pairs={{0,2},{2,0},{1,3},{3,1},{4,6},{6,4},{5,7},{7,5},{8,10},{10,8},{9,1... | collective-permute-start | bytes 110600 | tf_op jit(solution)/shard_map/ppermute | solution.py:703
  16.2 2.5 %collective-permute-done.5.sum_there = f32[72,128]{1,0:T(8,128)S(1)} collective-permute-done((f32[72,128]{1,0:T(8,128)S(1)}, f32[72,128]{1,0:T(8,128)S(1)}, u32[]{:S(2)}, u32[]{:S(2)}) %collective-permute-start.5) | collective-permute-done | bytes 36896 | tf_op jit(solution)/shard_map/ppermute | solution.py:703
  18.7 1.8 %shard_map.97 = (f32[200,128]{1,0:T(8,128)S(1)}, f32[128,256]{1,0:T(8,128)S(1)}) custom-call(s32[1,512]{1,0:T(1,128)S(1)} %get-tuple-element.15.mask, f32[8,192,256]{2,1,0:T(8,128)S(1)} %get-tuple-element.18.coherent, f32[128,256]{1,0:T(8,128)S(1)} %get-tuple-element.19.gram, bf16[2,256,256]{2,1,0:T(8,128)(2,1)S(1)} %get-tuple-element.20.hots, ...), custom_call_target="tpu_custom_call" | custom-call | tf_op jit(solution)/shard_map/pallas_call | solution.py:684
  20.5 0.1 collective-permute-start.6
  20.5 1.3 %collective-permute-done.6.there.other = f32[200,128]{1,0:T(8,128)S(1)} collective-permute-done((f32[200,128]{1,0:T(8,128)S(1)}, f32[200,128]{1,0:T(8,128)S(1)}, u32[]{:S(2)}, u32[]{:S(2)}) %collective-permute-start.6) | collective-permute-done | bytes 102432 | tf_op jit(solution)/shard_map/ppermute | solution.py:703
  21.8 1.6 %collective-permute-start.7 = (f32[200,128]{1,0:T(8,128)S(1)}, f32[200,128]{1,0:T(8,128)S(1)}, u32[]{:S(2)}, u32[]{:S(2)}) collective-permute-start(f32[200,128]{1,0:T(8,128)S(1)} %shard_map.98.here), channel_id=1, source_target_pairs={{0,2},{2,0},{1,3},{3,1},{4,6},{6,4},{5,7},{7,5},{8,10},{10,8},{9,1... | collective-permute-start | bytes 307208 | tf_op jit(solution)/shard_map/ppermute | solution.py:703
  23.4 3.4 %collective-permute-done.7.there = f32[200,128]{1,0:T(8,128)S(1)} collective-permute-done((f32[200,128]{1,0:T(8,128)S(1)}, f32[200,128]{1,0:T(8,128)S(1)}, u32[]{:S(2)}, u32[]{:S(2)}) %collective-permute-start.7) | collective-permute-done | bytes 102432 | tf_op jit(solution)/shard_map/ppermute | solution.py:703
  26.8 1.3 %shard_map.99 = (f32[8,8,1,128]{3,2,1,0:T(1,128)}, f32[8,8,512]{2,1,0:T(8,128)}) custom-call(s32[1,512]{1,0:T(1,128)S(1)} %get-tuple-element.15.mask, f32[8,128,128]{2,1,0:T(8,128)S(1)} %get-tuple-element.16.coherent, bf16[2,256,128]{2,1,0:T(8,128)(2,1)S(1)} %get-tuple-element.17.hots, f32[128,256]{1,0:T(8,128)S(1)} %get-tuple-element.26.before, ...), custom_call_target="tpu_custom_call" | custom-call | tf_op jit(solution)/shard_map/pallas_call | solution.py:684
  (2 shorter events, 0.0 us)
Async XLA Ops:
  0.6 11.0 %collective-permute-start = (f32[8,8,512]{2,1,0:T(8,128)}, f32[8,8,512]{2,1,0:T(8,128)S(1)}, u32[]{:S(2)}, u32[]{:S(2)}) collective-permute-start(f32[8,8,512]{2,1,0:T(8,128)} %jones_at.1), channel_id=1, source_target_pairs={{0,1},{1,0},{2,3},{3,2},{4,5},{5,4},{6,7},{7,6},{8,9},{9,8},{10,11... | collective-permute-start | bytes 393224 | tf_op jit(solution)/shard_map/ppermute | solution.py:703
  1.2 9.4 %collective-permute-start.1 = (f32[8,2,1,512]{3,2,1,0:T(1,128)}, f32[8,2,1,512]{3,2,1,0:T(1,128)S(1)}, u32[]{:S(2)}, u32[]{:S(2)}) collective-permute-start(f32[8,2,1,512]{3,2,1,0:T(1,128)} %seen_at.1), channel_id=1, source_target_pairs={{0,4},{4,0},{8,12},{12,8},{1,5},{5,1},{9,13},{13,9},{2,6},{6,2},{1... | collective-permute-start | bytes 98312 | tf_op jit(solution)/shard_map/ppermute | solution.py:703
  3.8 6.8 %collective-permute-start.3 = (f32[8,2,1,512]{3,2,1,0:T(1,128)}, f32[8,2,1,512]{3,2,1,0:T(1,128)S(1)}, u32[]{:S(2)}, u32[]{:S(2)}) collective-permute-start(f32[8,2,1,512]{3,2,1,0:T(1,128)} %seen_at.1), channel_id=1, source_target_pairs={{0,12},{4,8},{8,4},{12,0},{1,13},{5,9},{9,5},{13,1},{2,14},{6,10},... | collective-permute-start | bytes 98312 | tf_op jit(solution)/shard_map/ppermute | solution.py:703
  6.3 5.4 %collective-permute-start.2 = (f32[8,2,1,512]{3,2,1,0:T(1,128)}, f32[8,2,1,512]{3,2,1,0:T(1,128)S(1)}, u32[]{:S(2)}, u32[]{:S(2)}) collective-permute-start(f32[8,2,1,512]{3,2,1,0:T(1,128)} %seen_at.1), channel_id=1, source_target_pairs={{0,8},{4,12},{8,0},{12,4},{1,9},{5,13},{9,1},{13,5},{2,10},{6,14},... | collective-permute-start | bytes 98312 | tf_op jit(solution)/shard_map/ppermute | solution.py:703
  13.4 1.3 %collective-permute-start.4 = (f32[72,128]{1,0:T(8,128)S(1)}, f32[72,128]{1,0:T(8,128)S(1)}, u32[]{:S(2)}, u32[]{:S(2)}) collective-permute-start(f32[72,128]{1,0:T(8,128)S(1)} %get-tuple-element.25), channel_id=1, source_target_pairs={{0,1},{1,0},{2,3},{3,2},{4,5},{5,4},{6,7},{7,6},{8,9},{9,8},{10,11... | collective-permute-start | bytes 110600 | tf_op jit(solution)/shard_map/ppermute | solution.py:703
  14.7 4.0 %collective-permute-start.5 = (f32[72,128]{1,0:T(8,128)S(1)}, f32[72,128]{1,0:T(8,128)S(1)}, u32[]{:S(2)}, u32[]{:S(2)}) collective-permute-start(f32[72,128]{1,0:T(8,128)S(1)} %add.3.sum_here), channel_id=1, source_target_pairs={{0,2},{2,0},{1,3},{3,1},{4,6},{6,4},{5,7},{7,5},{8,10},{10,8},{9,1... | collective-permute-start | bytes 110600 | tf_op jit(solution)/shard_map/ppermute | solution.py:703
  20.5 1.4 %collective-permute-start.6 = (f32[200,128]{1,0:T(8,128)S(1)}, f32[200,128]{1,0:T(8,128)S(1)}, u32[]{:S(2)}, u32[]{:S(2)}) collective-permute-start(f32[200,128]{1,0:T(8,128)S(1)} %get-tuple-element.27.here.mine), channel_id=1, source_target_pairs={{0,1},{1,0},{2,3},{3,2},{4,5},{5,4},{6,7},{7,6},{8,9},{9,8},{10,11... | collective-permute-start | bytes 307208 | tf_op jit(solution)/shard_map/ppermute | solution.py:703
  21.8 5.0 %collective-permute-start.7 = (f32[200,128]{1,0:T(8,128)S(1)}, f32[200,128]{1,0:T(8,128)S(1)}, u32[]{:S(2)}, u32[]{:S(2)}) collective-permute-start(f32[200,128]{1,0:T(8,128)S(1)} %shard_map.98.here), channel_id=1, source_target_pairs={{0,2},{2,0},{1,3},{3,1},{4,6},{6,4},{5,7},{7,5},{8,10},{10,8},{9,1... | collective-permute-start | bytes 307208 | tf_op jit(solution)/shard_map/ppermute | solution.py:703

commit v3 on v2

--- a/solution.py
+++ b/solution.py
@@ -331,9 +331,9 @@
 
 
 def coherency_kernel(
-    channels, per_shard, pairs_at, positions_at, offsets_at, brightness_at, cluster_at, mask_at, seen_at, jones_at,
-    out, last_out, gram, hots, last_hots, mask, seen, jones,
-    pairs, positions, offsets, brightness, cluster, base, spin, parts, last_parts, sems,
+    channels, pairs_at, positions_at, offsets_at, brightness_at, cluster_at, mask_at, seen_at, own_at, other,
+    out, share, gram, hots, last_hots, mask, seen, jones, gather, predicted,
+    pairs, positions, offsets, brightness, cluster, own, base, spin, parts, model, sems,
 ):
     copies = [
         pltpu.make_async_copy(source, target, sems.at[index])
@@ -346,7 +346,7 @@
                 (cluster_at, cluster),
                 (mask_at, mask),
                 (seen_at, seen),
-                (jones_at, jones),
+                (own_at, own),
             )
         )
     ]
@@ -355,21 +355,17 @@
     for copy in copies[:5]:
         copy.wait()
     place = Place()
-    spans = []
-    for hot_ref, lanes, core in (
-        (hots, pl.ds(place.first_lane, PAIR), place.core),
-        (last_hots, pl.ds(place.last_lane, RUN), place.last_core),
-    ):
-        first_station = place.first_station(core)
-        table = jnp.concatenate([positions[:, 0:RUN], positions[:, pl.ds(first_station, RUN)]], axis=1)
-        table = split_rows(table, 3)
-        there = []
-        for side in (0, 1):
-            hot_ref[side] = onehot(pairs[side, :, lanes], first_station)
-            found = dot_f32(table, hot_ref[side])
-            there.append(found[0:2] + found[2:4] + found[4:6])
-        spans.append(there[0] - there[1])
-    span = jnp.concatenate(spans, axis=1)
+    window = place.first_station(place.core)
+    table = jnp.concatenate([positions[:, 0:RUN], positions[:, pl.ds(window, RUN)]], axis=1)
+    table = split_rows(table, 3)
+    there = []
+    for side in (0, 1):
+        hots[side] = onehot(pairs[side, :, pl.ds(place.first_lane, PAIR)], window)
+        last = pairs[side, :, pl.ds(place.last_lane, RUN)]
+        last_hots[side] = onehot(last, place.first_station(place.last_core))
+        found = dot_f32(table, hots[side])
+        there.append(found[0:2] + found[2:4] + found[4:6])
+    span = there[0] - there[1]
     sources = offsets.shape[1]
     columns = jnp.transpose(jnp.concatenate([offsets[...], jnp.zeros((6, sources))]))
     step = 16
@@ -380,6 +376,7 @@
         spin[0, rows], spin[1, rows] = turn_pair(geometry * (0.5 / channels))
 
     directions = out.shape[1] // 12
+    second_run = lax.rem(place.chan, 2) == 1
     member = lax.broadcasted_iota(jnp.int32, (directions, sources), 0) == cluster[...]
     bright = jnp.concatenate([jnp.where(member, brightness[n : n + 1], 0.0) for n in range(4)])
     high, low = pieces(bright, 2)
@@ -397,29 +394,28 @@
             c, s = base[0, rows], base[1, rows]
             for index, value in enumerate((c, s)):
                 for size, piece in enumerate(pieces(value, 2)):
-                    parts[odd, index, size, rows] = piece[:, :PAIR]
-                    last_parts[index, size, rows, odd * RUN : (odd + 1) * RUN] = piece[:, PAIR:]
+                    parts[odd, index, size, rows] = piece
             if channel < channels - 1:
                 dc, ds = spin[0, rows], spin[1, rows]
                 base[0, rows] = c * dc - s * ds
                 base[1, rows] = s * dc + c * ds
-        slot = place.slot(channel, per_shard)
         found = [table_times((parts[odd, index, 0], parts[odd, index, 1])) for index in (0, 1)]
-        out[slot, :half] = found[0]
-        out[slot, half : 2 * half] = found[1]
-        out[slot, 2 * half :] = found[0] - found[1]
+        out[channel, :half] = found[0]
+        out[channel, half : 2 * half] = found[1]
+        out[channel, 2 * half :] = found[0] - found[1]
+        for index in (0, 1):
+            mine = jnp.where(second_run, found[index][:, RUN:], found[index][:, :RUN])
+            share[channel, half * index : half * (index + 1)] = mine
         entries = [found[n // 4][n % 4 * directions : (n % 4 + 1) * directions] for n in range(8)]
         for n, value in enumerate(grams(entries)):
             rows = slice(n * directions, (n + 1) * directions)
             gram[rows] = value if channel == 0 else gram[rows] + value
-        if odd:
-            for index in (0, 1):
-                found = table_times((last_parts[index, 0], last_parts[index, 1]))
-                for before in (0, 1):
-                    slot = place.slot(channel - 1 + before, per_shard)
-                    last_out[slot, half * index : half * (index + 1)] = found[:, before * RUN : (before + 1) * RUN]
     for copy in copies[5:]:
         copy.wait()
+    fill_table(place, jones, own, other)
+    gather_gains(jones[...], hots, gather)
+    for run in range(2):
+        predict(out, gather, run, model, predicted)
 
 
 def gather_gains(table, hots, gather):
@@ -490,11 +486,39 @@
     return real - a[1] * b[1], imag + a[0] * b[1]
 
 
-def iterate(place, coherent, gram, hots, shards, mask, jones, model, error, gather, sums):
-    rows = jones.shape[0]
-    directions = rows // 8
+def fill_table(place, jones, own, other):
+    count = own.shape[0] * own.shape[1]
+    for ref, core in ((own, place.core), (other, 1 - place.core)):
+        at = pl.ds(pl.multiple_of(core * count, count), count)
+        jones[at, 0:RUN] = ref[:, :, 0:RUN].reshape(count, RUN)
+        window = ref[:, :, pl.ds(place.first_station(place.core), RUN)]
+        jones[at, RUN:] = window.reshape(count, RUN)
+
+
+def predict(coherent, gather, run, model, predicted):
+    channels = coherent.shape[0]
+    directions = coherent.shape[1] // 12
+    halves = directions // 8
+    lanes = slice(run * RUN, (run + 1) * RUN)
+    for h in range(halves):
+        first_gain = with_difference(gains_of(gather, 0, run, h))
+        second_gain = with_difference(gains_of(gather, 1, run, h))
+        for channel in range(channels):
+            coh = coherent_of(coherent, channel, h, lanes, directions, 12)
+            part = model_parts(first_gain, second_gain, coh)
+            if h > 0:
+                part = [a + model[channel, n] for n, a in enumerate(part)]
+            if h < halves - 1:
+                for n in range(12):
+                    model[channel, n] = part[n]
+            else:
+                predicted[run, channel] = sum_rows(model_of(part))
+
+
+def iterate(place, coherent, gram, hots, shards, mask, gather, predicted, error, sums):
+    directions = coherent.shape[1] // 12
+    rows = 8 * directions
     halves = rows // 64
-    gather_gains(jones[...], hots, gather)
     weight = mask[:, pl.ds(place.first_lane, PAIR)].astype(jnp.float32)
     channels = coherent.shape[0]
     per_shard = shards[0].shape[1]
@@ -502,22 +526,12 @@
         lanes = slice(run * RUN, (run + 1) * RUN)
         w = weight[:, lanes]
         at = pl.multiple_of(place.first_lane + run * RUN, RUN)
-        for h in range(halves):
-            first_gain = with_difference(gains_of(gather, 0, run, h))
-            second_gain = with_difference(gains_of(gather, 1, run, h))
-            for channel in range(channels):
-                coh = coherent_of(coherent, channel, h, lanes, directions, 12)
-                part = model_parts(first_gain, second_gain, coh)
-                if h > 0:
-                    part = [a + model[channel, n] for n, a in enumerate(part)]
-                if h < halves - 1:
-                    for n in range(12):
-                        model[channel, n] = part[n]
-                else:
-                    seen = shards[channel // per_shard][:, channel % per_shard, 0, pl.ds(at, RUN)]
-                    err = w * (seen - sum_rows(model_of(part)))
-                    error[channel, 0] = err
-                    error[channel, 1] = err + pltpu.roll(err, 4, 0)
+        for slot in range(channels):
+            channel = place.slot(slot, per_shard)
+            seen = shards[slot // per_shard][:, slot % per_shard, 0, pl.ds(at, RUN)]
+            err = w * (seen - predicted[run, channel])
+            error[channel, 0] = err
+            error[channel, 1] = err + pltpu.roll(err, 4, 0)
 
         for h in range(halves):
             first_gain, second_gain = gains_of(gather, 0, run, h), gains_of(gather, 1, run, h)
@@ -601,94 +615,112 @@
 
 
 def first_kernel(
-    mask, coherent, gram, hots, own, other, s0, s1, s2, s3, packed, mine, jones, model, error, gather, sums
+    mask, coherent, gram, hots, gather, predicted, s0, s1, s2, s3, packed, mine, error, sums
 ):
     place = Place()
-    count = own.shape[0] * own.shape[1]
-    for ref, core in ((own, place.core), (other, 1 - place.core)):
-        at = pl.ds(pl.multiple_of(core * count, count), count)
-        jones[at, 0:RUN] = ref[:, :, 0:RUN].reshape(count, RUN)
-        window = ref[:, :, pl.ds(place.first_station(place.core), RUN)]
-        jones[at, RUN:] = window.reshape(count, RUN)
-    total = iterate(
-        place, coherent, gram, hots, (s0, s1, s2, s3), mask, jones, model, error, gather, sums
-    )
-    packed[...] = pack(total[:, :RUN], jones.shape[0])
+    total = iterate(place, coherent, gram, hots, (s0, s1, s2, s3), mask, gather, predicted, error, sums)
+    packed[...] = pack(total[:, :RUN], 8 * (coherent.shape[1] // 12))
     mine[...] = total[:, RUN:]
 
 
+def block_sums(refs, held):
+    here, over_core, over_blk, over_both = [ref[:held] for ref in refs]
+    return unpack((here + over_core) + (over_blk + over_both))
+
+
 def second_kernel(
-    mask, coherent, gram, hots, before, mine, sum_here, sum_there, s0, s1, s2, s3,
-    packed, jones, model, error, gather, sums,
+    mask, coherent, gram, hots, before, mine, p0, p1, p2, p3, s0, s1, s2, s3,
+    to_core, to_blk, to_both, jones, model, error, gather, predicted, sums,
 ):
     place = Place()
+    held = p0.shape[0]
     jones[...] = before[...]
-    update(jones, slice(0, RUN), unpack(sum_here[...] + sum_there[...]), block_zero())
+    update(jones, slice(0, RUN), block_sums((p0, p1, p2, p3), held), block_zero())
     update(jones, slice(RUN, None), mine[...])
-    total = iterate(
-        place, coherent, gram, hots, (s0, s1, s2, s3), mask, jones, model, error, gather, sums
-    )
+    gather_gains(jones[...], hots, gather)
+    for run in range(2):
+        predict(coherent, gather, run, model, predicted)
+    total = iterate(place, coherent, gram, hots, (s0, s1, s2, s3), mask, gather, predicted, error, sums)
     rows = jones.shape[0]
-    held = packed.shape[0] - rows
-    packed[:held] = pack(total[:, :RUN], rows)
+    half = rows // 2
+    packed = pack(total[:, :RUN], rows)
     update(jones, slice(RUN, None), total[:, RUN:])
-    packed[held:] = jones[:, RUN:]
-
-
-def join_kernel(here, there, out):
-    half = here.shape[0] * 8 // 25
-    held = here.shape[0] - 2 * half
-    at = pl.ds(pl.multiple_of(held + lax.axis_index("dir") * half, 8), half)
-    out[:held] = here[:held] + there[:held]
-    out[held : held + half] = here[at]
-    out[held + half :] = there[at]
+    to_core[:held] = packed
+    to_blk[:held] = packed
+    to_both[:held] = packed
+    to_core[held:] = jones[:, RUN:]
+    to_blk[held:] = jones[pl.ds(pl.multiple_of(place.core * half, half), half), RUN:]
+    to_both[held:] = jones[pl.ds(pl.multiple_of((1 - place.core) * half, half), half), RUN:]
 
 
 def last_kernel(
-    mask, coherent, hots, before, mine, other, here, there, s0, s1, s2, s3, residual, solved, jones, gather
+    mask, share, other_share, hots, before, p0, p1, p2, p3, s0, s1, s2, s3,
+    residual, solved_at, jones, gather, solved, sem,
 ):
     place = Place()
     rows = before.shape[0]
     half = rows // 2
-    held = here.shape[0] - rows
-    own_core_last = place.last_core == place.core
+    held = p0.shape[0] - rows
+    owned = place.last_core == place.core
     jones[:, 0:RUN] = before[:, 0:RUN]
-    jones[:, RUN:] = jnp.where(own_core_last, mine[held:], other[held:])
-    update(jones, slice(0, RUN), unpack(here[:held] + there[:held]), block_zero())
-
-    for ref, blk in ((here, place.blk), (there, 1 - place.blk)):
-        for at, core in ((held, place.core), (held + half, 1 - place.core)):
-            lanes = pl.ds(pl.multiple_of((2 * blk + core) * RUN, RUN), RUN)
-            solved[:, :, lanes] = ref[at : at + half].reshape(half // 8, 8, RUN)
-    zero = jones[pl.ds(pl.multiple_of(place.core * half, half), half), 0:RUN].reshape(half // 8, 8, RUN)
+    jones[:, RUN:] = jnp.where(owned, p0[held:], p1[held:])
+    update(jones, slice(0, RUN), block_sums((p0, p1, p2, p3), held), block_zero())
+
+    own_rows = pl.multiple_of(place.core * half, half)
+    for ref, start, blk, core in (
+        (p0, held + own_rows, place.blk, place.core),
+        (p1, held + own_rows, place.blk, 1 - place.core),
+        (p2, held, 1 - place.blk, place.core),
+        (p3, held, 1 - place.blk, 1 - place.core),
+    ):
+        lanes = pl.ds(pl.multiple_of((2 * blk + core) * RUN, RUN), RUN)
+        solved[:, :, lanes] = ref[pl.ds(pl.multiple_of(start, 8), half)].reshape(half // 8, 8, RUN)
+    zero = jones[pl.ds(own_rows, half), 0:RUN].reshape(half // 8, 8, RUN)
     lane = lax.broadcasted_iota(jnp.int32, zero.shape, 2)
     solved[:, :, 0:RUN] = jnp.where(lane < BLOCK, zero, solved[:, :, 0:RUN])
+    copy = pltpu.make_async_copy(solved, solved_at, sem)
+    copy.start()
 
     gather_gains(jones[...], hots, gather)
     w = mask[:, pl.ds(place.last_lane, RUN)].astype(jnp.float32)
     shards = (s0, s1, s2, s3)
-    channels = coherent.shape[0]
+    channels = share.shape[0]
     per_shard = s0.shape[1]
     gains = [[gains_of(gather, side, 0, h) for h in range(rows // 64)] for side in (0, 1)]
-    for channel in range(channels):
+    for slot in range(channels):
+        channel = place.slot(slot, per_shard)
         part = None
         for h in range(rows // 64):
-            coh = coherent_of(coherent, channel, h, slice(0, RUN), rows // 8, 8)
-            z = product(gains[0][h], coh)
-            part = product(z, gains[1][h], dagger_b=True, total=part)
-        seen = shards[channel // per_shard][:, channel % per_shard, 0, pl.ds(place.last_lane, RUN)]
-        residual[:, place.slot(channel, per_shard), 0] = w * (seen - sum_rows(part))
-
-
-def call(kernel, out_shape, scratch, operands, space=pltpu.VMEM):
+            coh = [
+                jnp.where(owned, a, b)
+                for a, b in zip(
+                    coherent_of(share, channel, h, slice(0, RUN), rows // 8, 8),
+                    coherent_of(other_share, channel, h, slice(0, RUN), rows // 8, 8),
+                )
+            ]
+            part = product(product(gains[0][h], coh), gains[1][h], dagger_b=True, total=part)
+        seen = shards[slot // per_shard][:, slot % per_shard, 0, pl.ds(place.last_lane, RUN)]
+        residual[:, channel, 0] = w * (seen - sum_rows(part))
+    copy.wait()
+
+
+def call(kernel, out_shape, scratch, operands, flops, in_hbm=0, out_spaces=None):
+    spaces = [pltpu.HBM] * in_hbm + [pltpu.VMEM] * (len(operands) - in_hbm)
     return pl.pallas_call(
         kernel,
         out_shape=out_shape,
-        in_specs=[pl.BlockSpec(memory_space=space)] * len(operands),
-        out_specs=jax.tree.map(lambda _: pl.BlockSpec(memory_space=pltpu.VMEM), out_shape),
+        in_specs=[pl.BlockSpec(memory_space=space) for space in spaces],
+        out_specs=tuple(
+            pl.BlockSpec(memory_space=space) for space in out_spaces or [pltpu.VMEM] * len(out_shape)
+        ),
         scratch_shapes=scratch,
         compiler_params=pltpu.CompilerParams(vmem_limit_bytes=40 << 20),
-    )(*[pltpu.with_memory_space_constraint(x, space) for x in operands])
+        cost_estimate=pl.CostEstimate(
+            flops=flops,
+            transcendentals=0,
+            bytes_accessed=sum(x.size * x.dtype.itemsize for x in [*operands, *out_shape]),
+        ),
+    )(*[pltpu.with_memory_space_constraint(x, space) for x, space in zip(operands, spaces)])
 
 
 def f32(*shape):
@@ -701,6 +733,10 @@
 
 def swap(x, axis, bit=1):
     return lax.ppermute(x, axis, [(i, i ^ bit) for i in range(lax.axis_size(axis))])
+
+
+def from_three(core, blk, both):
+    return swap(core, "dir"), swap(blk, "blk"), swap(both, ("blk", "dir"), 3)
 
 
 def per_device_owned(
@@ -714,8 +750,7 @@
     jones_gains,
 ):
     relay_count = lax.axis_size("chan")
-    per_shard = visibilities.shape[1]
-    channels = per_shard * relay_count
+    channels = visibilities.shape[1] * relay_count
     half_directions = jones_gains.shape[0]
     directions = 2 * half_directions
     rows = 8 * directions
@@ -723,10 +758,19 @@
 
     other = swap(jones_gains, "dir")
     shards = [swap(visibilities, "chan", bit) for bit in range(1, relay_count)]
-    kept = (valid_mask, visibilities, jones_gains)
     inputs = (antenna_pairs, station_positions, source_offsets, brightness, source_cluster[None, :])
-    coherent, last_coherent, gram, hots, last_hots, mask, seen, own = call(
-        functools.partial(coherency_kernel, channels, per_shard),
+    kept = (valid_mask, visibilities)
+    held = (rows + directions) // 2
+    table = f32(rows, 2 * RUN)
+    gathered = f32(2, 2, rows, RUN)
+    predictions = f32(2, channels, 8, RUN)
+    model = pltpu.VMEM((channels, 12, 8, RUN), jnp.float32)
+    scratch = [
+        pltpu.VMEM((channels, 2, 8, RUN), jnp.float32),
+        pltpu.VMEM((2, 2, rows + directions, RUN), jnp.float32),
+    ]
+    coherent, share, gram, hots, last_hots, mask, seen, jones, gather, predicted = call(
+        functools.partial(coherency_kernel, channels),
         (
             f32(channels, 12 * directions, PAIR),
             f32(channels, 8 * directions, RUN),
@@ -734,48 +778,63 @@
             bf16(2, 2 * RUN, PAIR),
             bf16(2, 2 * RUN, RUN),
             *[jax.ShapeDtypeStruct(x.shape, x.dtype) for x in kept],
+            table,
+            gathered,
+            predictions,
         ),
-        [pltpu.VMEM(x.shape, x.dtype) for x in inputs]
+        [pltpu.VMEM(x.shape, x.dtype) for x in inputs + (jones_gains,)]
         + [
-            pltpu.VMEM((2, sources, PAIR + RUN), jnp.float32),
-            pltpu.VMEM((2, sources, PAIR + RUN), jnp.float32),
+            pltpu.VMEM((2, sources, PAIR), jnp.float32),
+            pltpu.VMEM((2, sources, PAIR), jnp.float32),
             pltpu.VMEM((2, 2, 2, sources, PAIR), jnp.bfloat16),
-            pltpu.VMEM((2, 2, sources, 2 * RUN), jnp.bfloat16),
-            pltpu.SemaphoreType.DMA((len(inputs + kept),)),
+            model,
+            pltpu.SemaphoreType.DMA((len(inputs + kept) + 1,)),
         ],
-        inputs + kept,
-        pltpu.HBM,
+        inputs + kept + (jones_gains, other),
+        4 * 10**9,
+        len(inputs + kept) + 1,
     )
     shards = [seen] + shards
-    scratch = [
-        pltpu.VMEM((channels, 12, 8, RUN), jnp.float32),
-        pltpu.VMEM((channels, 2, 8, RUN), jnp.float32),
-        pltpu.VMEM((2, 2, rows, RUN), jnp.float32),
-        pltpu.VMEM((2, 2, rows + directions, RUN), jnp.float32),
-    ]
-    table = f32(rows, 2 * RUN)
-    held = (rows + directions) // 2
-    packed, mine, jones = call(
+    packed, mine = call(
         first_kernel,
-        (f32(held, RUN), f32(rows + directions, RUN), table),
+        (f32(held, RUN), f32(rows + directions, RUN)),
         scratch,
-        (mask, coherent, gram, hots, own, other, *shards),
-    )
-    packed = packed + swap(packed, "dir")
-    there = swap(packed, "blk")
-    mine, jones = call(
+        (mask, coherent, gram, hots, gather, predicted, *shards),
+        10**9,
+    )
+    sums = from_three(packed, packed, packed)
+    *sums, share = lax.optimization_barrier((*sums, share))
+    other_share = swap(share, "dir")
+    to_core, to_blk, to_both, jones = call(
         second_kernel,
-        (f32(held + rows, RUN), table),
-        scratch,
-        (mask, coherent, gram, hots, jones, mine, packed, there, *shards),
-    )
-    other = swap(mine, "dir")
-    joined = call(join_kernel, f32(held + rows, RUN), [], (mine, other))
+        (f32(held + rows, RUN), f32(held + rows // 2, RUN), f32(held + rows // 2, RUN), table),
+        [
+            model,
+            scratch[0],
+            pltpu.VMEM(gathered.shape, jnp.float32),
+            pltpu.VMEM(predictions.shape, jnp.float32),
+            scratch[1],
+        ],
+        (mask, coherent, gram, hots, jones, mine, packed, *sums, *shards),
+        2 * 10**9,
+    )
+    solved = f32(half_directions, 8, station_positions.shape[1])
     return call(
         last_kernel,
-        (f32(8, channels, 1, RUN), f32(half_directions, 8, station_positions.shape[1])),
-        [pltpu.VMEM((rows, 2 * RUN), jnp.float32), pltpu.VMEM((2, 1, rows, RUN), jnp.float32)],
-        (mask, last_coherent, last_hots, jones, mine, other, joined, swap(joined, "blk"), *shards),
+        (f32(8, channels, 1, RUN), solved),
+        [
+            pltpu.VMEM((rows, 2 * RUN), jnp.float32),
+            pltpu.VMEM((2, 1, rows, RUN), jnp.float32),
+            pltpu.VMEM(solved.shape, jnp.float32),
+            pltpu.SemaphoreType.DMA,
+        ],
+        (
+            mask, share, other_share, last_hots, jones,
+            to_core, *from_three(to_core, to_blk, to_both), *shards,
+        ),
+        10**9,
+        0,
+        (pltpu.VMEM, pltpu.HBM),
     )
 
 

time: 28.3 us -> 26.9 us (0.951)
  waiting for transfers between devices: 9.47 us -> 8 us
  starting transfers between devices: 8.94 us -> 9.84 us
  Pallas kernels: 9.06 us -> 8.18 us
    ppermute x8 -> x11, waiting for transfers between devices: 9.47 us -> 8 us  [swap(): lax.ppermute(x, axis, [(i, i ^ bit) for i in range(lax.axis_size(axis))])]
    ppermute x8 -> x11, starting transfers between devices: 8.94 us -> 9.84 us  [swap(): lax.ppermute(x, axis, [(i, i ^ bit) for i in range(lax.axis_size(axis))])]
    pallas_call x5 -> x4, Pallas kernels: 9.06 us -> 8.18 us  [call(): pl.pallas_call(kernel, out_shape=out_shape, in_specs=[pl.BlockSpec(memory...]
  transfers between devices with their start and end apart: 8 -> 11, of which waited for: 5 -> 5; matrix products, arithmetic and copies ran while one was open for 0% -> 0% of each run, Pallas kernels for 15% -> 21%
where the time goes in v3:
time: 26.9 us; the launch traced here: 26.7 us
  starting transfers between devices  9.84 us (37%)
  Pallas kernels  8.18 us (30%)
  waiting for transfers between devices  8 us (30%)
  between operations  0.68 us (3%)
    ppermute x11, starting transfers between devices, swap(): lax.ppermute(x, axis, [(i, i ^ bit) for i in range(lax.axis_size(axis))])  9.84 us
    pallas_call x4, Pallas kernels, call(): pl.pallas_call(kernel, out_shape=out_shape, in_specs=[pl.BlockSpec(memory...  8.18 us
    ppermute x11, waiting for transfers between devices, swap(): lax.ppermute(x, axis, [(i, i ^ bit) for i in range(lax.axis_size(axis))])  8 us
  transfers between devices with their start and end apart: 11, of which 5 were waited for; matrix products, arithmetic and copies ran while one was open for 0% of the time, Pallas kernels for 21%

profile of v3, /device:TPU:0, one launch (start us, length us, event | category | flops | bytes accessed | tf_op | source)
XLA Modules:
  0.0 26.7 jit_solution(11721863361567022553)
XLA Ops:
  0.6 0.5 %collective-permute-start = (f32[8,8,512]{2,1,0:T(8,128)}, f32[8,8,512]{2,1,0:T(8,128)S(1)}, u32[]{:S(2)}, u32[]{:S(2)}) collective-permute-start(f32[8,8,512]{2,1,0:T(8,128)} %own_at.1), channel_id=1, source_target_pairs={{0,1},{1,0},{2,3},{3,2},{4,5},{5,4},{6,7},{7,6},{8,9},{9,8},{10,11... | collective-permute-start | bytes 393224 | tf_op jit(solution)/shard_map/ppermute | solution.py:735
  1.2 2.6 %collective-permute-start.1 = (f32[8,2,1,512]{3,2,1,0:T(1,128)}, f32[8,2,1,512]{3,2,1,0:T(1,128)S(1)}, u32[]{:S(2)}, u32[]{:S(2)}) collective-permute-start(f32[8,2,1,512]{3,2,1,0:T(1,128)} %seen_at.1), channel_id=1, source_target_pairs={{0,4},{4,0},{8,12},{12,8},{1,5},{5,1},{9,13},{13,9},{2,6},{6,2},{1... | collective-permute-start | bytes 98312 | tf_op jit(solution)/shard_map/ppermute | solution.py:735
  3.8 2.5 %collective-permute-start.3 = (f32[8,2,1,512]{3,2,1,0:T(1,128)}, f32[8,2,1,512]{3,2,1,0:T(1,128)S(1)}, u32[]{:S(2)}, u32[]{:S(2)}) collective-permute-start(f32[8,2,1,512]{3,2,1,0:T(1,128)} %seen_at.1), channel_id=1, source_target_pairs={{0,12},{4,8},{8,4},{12,0},{1,13},{5,9},{9,5},{13,1},{2,14},{6,10},... | collective-permute-start | bytes 98312 | tf_op jit(solution)/shard_map/ppermute | solution.py:735
  6.3 0.1 collective-permute-start.2
  6.4 0.0 collective-permute-done.other
  6.4 3.9 %shard_map.95 = (f32[8,192,256]{2,1,0:T(8,128)S(1)}, f32[8,128,128]{2,1,0:T(8,128)S(1)}, f32[128,256]{1,0:T(8,128)S(1)}, bf16[2,256,256]{2,1,0:T(8,128)(2,1)S(1)...) custom-call(s32[2,1,512]{2,1,0:T(1,128)} %pairs_at.1, ...), custom_call_target="tpu_custom_call" | custom-call | flops 4000000000 | bytes 3427328 | tf_op jit(solution)/shard_map/pallas_call | solution.py:709
  10.3 0.0 collective-permute-done.1.s1
  10.3 0.0 collective-permute-done.3.s3
  10.3 1.3 %collective-permute-done.2.s2 = f32[8,2,1,512]{3,2,1,0:T(1,128)S(1)} collective-permute-done((f32[8,2,1,512]{3,2,1,0:T(1,128)}, f32[8,2,1,512]{3,2,1,0:T(1,128)S(1)}, u32[]{:S(2)}, u32[]{:S(2)}) %collective-permute-start.2) | collective-permute-done | bytes 32800 | tf_op jit(solution)/shard_map/ppermute | solution.py:735
  11.7 1.1 %shard_map.96 = (f32[72,128]{1,0:T(8,128)S(1)}, f32[144,128]{1,0:T(8,128)S(1)}) custom-call(s32[1,512]{1,0:T(1,128)S(1)} %get-tuple-element.22.mask, f32[8,192,256]{2,1,0:T(8,128)S(1)} %get-tuple-element.23.coherent, f32[128,256]{1,0:T(8,128)S(1)} %get-tuple-element.24.gram, bf16[2,256,256]{2,1,0:T(8,128)(2,1)S(1)} %get-tuple-element.25.hots, ...), custom_call_target="tpu_custom_call" | custom-call | flops 1000000000 | bytes 2537472 | tf_op jit(solution)/shard_map/pallas_call | solution.py:709
  12.7 0.1 collective-permute-start.6
  12.8 1.6 %collective-permute-start.5 = (f32[72,128]{1,0:T(8,128)S(1)}, f32[72,128]{1,0:T(8,128)S(1)}, u32[]{:S(2)}, u32[]{:S(2)}) collective-permute-start(f32[72,128]{1,0:T(8,128)S(1)} %get-tuple-element.29.p0), channel_id=1, source_target_pairs={{0,2},{2,0},{1,3},{3,1},{4,6},{6,4},{5,7},{7,5},{8,10},{10,8},{9,1... | collective-permute-start | bytes 110600 | tf_op jit(solution)/shard_map/ppermute | solution.py:735
  14.4 0.3 %collective-permute-start.4 = (f32[72,128]{1,0:T(8,128)S(1)}, f32[72,128]{1,0:T(8,128)S(1)}, u32[]{:S(2)}, u32[]{:S(2)}) collective-permute-start(f32[72,128]{1,0:T(8,128)S(1)} %get-tuple-element.29.p0), channel_id=1, source_target_pairs={{0,1},{1,0},{2,3},{3,2},{4,5},{5,4},{6,7},{7,6},{8,9},{9,8},{10,11... | collective-permute-start | bytes 110600 | tf_op jit(solution)/shard_map/ppermute | solution.py:735
  14.7 1.9 %collective-permute-done.6.p3 = f32[72,128]{1,0:T(8,128)S(1)} collective-permute-done((f32[72,128]{1,0:T(8,128)S(1)}, f32[72,128]{1,0:T(8,128)S(1)}, u32[]{:S(2)}, u32[]{:S(2)}) %collective-permute-start.6) | collective-permute-done | bytes 36896 | tf_op jit(solution)/shard_map/ppermute | solution.py:735
  16.5 0.4 %collective-permute-done.5.p2 = f32[72,128]{1,0:T(8,128)S(1)} collective-permute-done((f32[72,128]{1,0:T(8,128)S(1)}, f32[72,128]{1,0:T(8,128)S(1)}, u32[]{:S(2)}, u32[]{:S(2)}) %collective-permute-start.5) | collective-permute-done | bytes 36896 | tf_op jit(solution)/shard_map/ppermute | solution.py:735
  17.0 0.0 collective-permute-done.4.p1
  17.0 0.2 collective-permute-start.7
  17.2 1.8 %shard_map.97 = (f32[200,128]{1,0:T(8,128)S(1)}, f32[136,128]{1,0:T(8,128)S(1)}, f32[136,128]{1,0:T(8,128)S(1)}, f32[128,256]{1,0:T(8,128)S(1)}) custom-call(s32[1,512]{1,0:T(1,128)S(1)} %get-tuple-element.22.mask, f32[8,192,256]{2,1,0:T(8,128)S(1)} %get-tuple-element.23.coherent, f32[128,256]{1,0:T(8,128)S(1)} %get-tuple-element.24.gram, ...), custom_call_target="tpu_custom_call" | custom-call | flops 2000000000 | bytes 2824192 | tf_op jit(solution)/shard_map/pallas_call | solution.py:709
  19.0 0.3 %collective-permute-start.8 = (f32[200,128]{1,0:T(8,128)S(1)}, f32[200,128]{1,0:T(8,128)S(1)}, u32[]{:S(2)}, u32[]{:S(2)}) collective-permute-start(f32[200,128]{1,0:T(8,128)S(1)} %get-tuple-element.39.p0), channel_id=1, source_target_pairs={{0,1},{1,0},{2,3},{3,2},{4,5},{5,4},{6,7},{7,6},{8,9},{9,8},{10,11... | collective-permute-start | bytes 307208 | tf_op jit(solution)/shard_map/ppermute | solution.py:735
  19.4 1.5 %collective-permute-start.9 = (f32[136,128]{1,0:T(8,128)S(1)}, f32[136,128]{1,0:T(8,128)S(1)}, u32[]{:S(2)}, u32[]{:S(2)}) collective-permute-start(f32[136,128]{1,0:T(8,128)S(1)} %get-tuple-element.40), channel_id=1, source_target_pairs={{0,2},{2,0},{1,3},{3,1},{4,6},{6,4},{5,7},{7,5},{8,10},{10,8},{9,1... | collective-permute-start | bytes 208904 | tf_op jit(solution)/shard_map/ppermute | solution.py:735
  20.9 0.1 collective-permute-start.10
  21.0 2.7 %collective-permute-done.9.p2 = f32[136,128]{1,0:T(8,128)S(1)} collective-permute-done((f32[136,128]{1,0:T(8,128)S(1)}, f32[136,128]{1,0:T(8,128)S(1)}, u32[]{:S(2)}, u32[]{:S(2)}) %collective-permute-start.9) | collective-permute-done | bytes 69664 | tf_op jit(solution)/shard_map/ppermute | solution.py:735
  23.7 1.6 %collective-permute-done.10.p3 = f32[136,128]{1,0:T(8,128)S(1)} collective-permute-done((f32[136,128]{1,0:T(8,128)S(1)}, f32[136,128]{1,0:T(8,128)S(1)}, u32[]{:S(2)}, u32[]{:S(2)}) %collective-permute-start.10) | collective-permute-done | bytes 69664 | tf_op jit(solution)/shard_map/ppermute | solution.py:735
  25.3 0.0 collective-permute-done.8.p1
  25.3 0.0 collective-permute-done.7.other_share
  25.3 1.4 %shard_map.98 = (f32[8,8,1,128]{3,2,1,0:T(1,128)}, f32[8,8,512]{2,1,0:T(8,128)}) custom-call(s32[1,512]{1,0:T(1,128)S(1)} %get-tuple-element.22.mask, f32[8,128,128]{2,1,0:T(8,128)S(1)} %get-tuple-element.31.share, f32[8,128,128]{2,1,0:T(8,128)S(1)} %collective-permute-done.7.other_share, bf16[2,256,128]{2,1,0:T(8,128)(2,1)S(1)} %get-tuple-element.32.hots, ...), custom_call_target="tpu_custom_call" | custom-call | flops 1000000000 | bytes 1951744 | tf_op jit(solution)/shard_map/pallas_call | solution.py:709
Async XLA Ops:
  0.6 5.8 %collective-permute-start = (f32[8,8,512]{2,1,0:T(8,128)}, f32[8,8,512]{2,1,0:T(8,128)S(1)}, u32[]{:S(2)}, u32[]{:S(2)}) collective-permute-start(f32[8,8,512]{2,1,0:T(8,128)} %own_at.1), channel_id=1, source_target_pairs={{0,1},{1,0},{2,3},{3,2},{4,5},{5,4},{6,7},{7,6},{8,9},{9,8},{10,11... | collective-permute-start | bytes 393224 | tf_op jit(solution)/shard_map/ppermute | solution.py:735
  1.2 9.2 %collective-permute-start.1 = (f32[8,2,1,512]{3,2,1,0:T(1,128)}, f32[8,2,1,512]{3,2,1,0:T(1,128)S(1)}, u32[]{:S(2)}, u32[]{:S(2)}) collective-permute-start(f32[8,2,1,512]{3,2,1,0:T(1,128)} %seen_at.1), channel_id=1, source_target_pairs={{0,4},{4,0},{8,12},{12,8},{1,5},{5,1},{9,13},{13,9},{2,6},{6,2},{1... | collective-permute-start | bytes 98312 | tf_op jit(solution)/shard_map/ppermute | solution.py:735
  3.8 6.5 %collective-permute-start.3 = (f32[8,2,1,512]{3,2,1,0:T(1,128)}, f32[8,2,1,512]{3,2,1,0:T(1,128)S(1)}, u32[]{:S(2)}, u32[]{:S(2)}) collective-permute-start(f32[8,2,1,512]{3,2,1,0:T(1,128)} %seen_at.1), channel_id=1, source_target_pairs={{0,12},{4,8},{8,4},{12,0},{1,13},{5,9},{9,5},{13,1},{2,14},{6,10},... | collective-permute-start | bytes 98312 | tf_op jit(solution)/shard_map/ppermute | solution.py:735
  6.3 5.4 %collective-permute-start.2 = (f32[8,2,1,512]{3,2,1,0:T(1,128)}, f32[8,2,1,512]{3,2,1,0:T(1,128)S(1)}, u32[]{:S(2)}, u32[]{:S(2)}) collective-permute-start(f32[8,2,1,512]{3,2,1,0:T(1,128)} %seen_at.1), channel_id=1, source_target_pairs={{0,8},{4,12},{8,0},{12,4},{1,9},{5,13},{9,1},{13,5},{2,10},{6,14},... | collective-permute-start | bytes 98312 | tf_op jit(solution)/shard_map/ppermute | solution.py:735
  12.7 3.8 %collective-permute-start.6 = (f32[72,128]{1,0:T(8,128)S(1)}, f32[72,128]{1,0:T(8,128)S(1)}, u32[]{:S(2)}, u32[]{:S(2)}) collective-permute-start(f32[72,128]{1,0:T(8,128)S(1)} %get-tuple-element.29.p0), channel_id=1, source_target_pairs={{0,3},{1,2},{2,1},{3,0},{4,7},{5,6},{6,5},{7,4},{8,11},{9,10},{10,... | collective-permute-start | bytes 110600 | tf_op jit(solution)/shard_map/ppermute | solution.py:735
  12.8 4.2 %collective-permute-start.5 = (f32[72,128]{1,0:T(8,128)S(1)}, f32[72,128]{1,0:T(8,128)S(1)}, u32[]{:S(2)}, u32[]{:S(2)}) collective-permute-start(f32[72,128]{1,0:T(8,128)S(1)} %get-tuple-element.29.p0), channel_id=1, source_target_pairs={{0,2},{2,0},{1,3},{3,1},{4,6},{6,4},{5,7},{7,5},{8,10},{10,8},{9,1... | collective-permute-start | bytes 110600 | tf_op jit(solution)/shard_map/ppermute | solution.py:735
  14.4 2.6 %collective-permute-start.4 = (f32[72,128]{1,0:T(8,128)S(1)}, f32[72,128]{1,0:T(8,128)S(1)}, u32[]{:S(2)}, u32[]{:S(2)}) collective-permute-start(f32[72,128]{1,0:T(8,128)S(1)} %get-tuple-element.29.p0), channel_id=1, source_target_pairs={{0,1},{1,0},{2,3},{3,2},{4,5},{5,4},{6,7},{7,6},{8,9},{9,8},{10,11... | collective-permute-start | bytes 110600 | tf_op jit(solution)/shard_map/ppermute | solution.py:735
  17.0 8.3 %collective-permute-start.7 = (f32[8,128,128]{2,1,0:T(8,128)S(1)}, f32[8,128,128]{2,1,0:T(8,128)S(1)}, u32[]{:S(2)}, u32[]{:S(2)}) collective-permute-start(f32[8,128,128]{2,1,0:T(8,128)S(1)} %get-tuple-element.31.share), channel_id=1, source_target_pairs={{0,1},{1,0},{2,3},{3,2},{4,5},{5,4},{6,7},{7,6},{8,9},{9,8},{10,11... | collective-permute-start | bytes 1572872 | tf_op jit(solution)/shard_map/ppermute | solution.py:735
  19.0 6.3 %collective-permute-start.8 = (f32[200,128]{1,0:T(8,128)S(1)}, f32[200,128]{1,0:T(8,128)S(1)}, u32[]{:S(2)}, u32[]{:S(2)}) collective-permute-start(f32[200,128]{1,0:T(8,128)S(1)} %get-tuple-element.39.p0), channel_id=1, source_target_pairs={{0,1},{1,0},{2,3},{3,2},{4,5},{5,4},{6,7},{7,6},{8,9},{9,8},{10,11... | collective-permute-start | bytes 307208 | tf_op jit(solution)/shard_map/ppermute | solution.py:735
  19.4 4.3 %collective-permute-start.9 = (f32[136,128]{1,0:T(8,128)S(1)}, f32[136,128]{1,0:T(8,128)S(1)}, u32[]{:S(2)}, u32[]{:S(2)}) collective-permute-start(f32[136,128]{1,0:T(8,128)S(1)} %get-tuple-element.40), channel_id=1, source_target_pairs={{0,2},{2,0},{1,3},{3,1},{4,6},{6,4},{5,7},{7,5},{8,10},{10,8},{9,1... | collective-permute-start | bytes 208904 | tf_op jit(solution)/shard_map/ppermute | solution.py:735
  20.9 4.5 %collective-permute-start.10 = (f32[136,128]{1,0:T(8,128)S(1)}, f32[136,128]{1,0:T(8,128)S(1)}, u32[]{:S(2)}, u32[]{:S(2)}) collective-permute-start(f32[136,128]{1,0:T(8,128)S(1)} %get-tuple-element.41), channel_id=1, source_target_pairs={{0,3},{1,2},{2,1},{3,0},{4,7},{5,6},{6,5},{7,4},{8,11},{9,10},{10,... | collective-permute-start | bytes 208904 | tf_op jit(solution)/shard_map/ppermute | solution.py:735

commit v4 on v3

--- a/solution.py
+++ b/solution.py
@@ -289,8 +289,9 @@
     def first_station(self, core):
         return pl.multiple_of((2 * self.blk + core) * RUN, RUN)
 
-    def slot(self, channel, per_shard):
-        return jnp.bitwise_xor(channel // per_shard, self.chan) * per_shard + channel % per_shard
+    def channel_of(self, slot, per_shard):
+        bits = (0, 1 + 2 * self.core, 2, 3 - 2 * self.core)[slot // per_shard]
+        return jnp.bitwise_xor(bits, self.chan) * per_shard + slot % per_shard
 
 
 def onehot(station, first_station):
@@ -331,9 +332,9 @@
 
 
 def coherency_kernel(
-    channels, pairs_at, positions_at, offsets_at, brightness_at, cluster_at, mask_at, seen_at, own_at, other,
-    out, share, gram, hots, last_hots, mask, seen, jones, gather, predicted,
-    pairs, positions, offsets, brightness, cluster, own, base, spin, parts, model, sems,
+    channels, pairs_at, positions_at, offsets_at, brightness_at, cluster_at, mask_at, seen_at, own_at,
+    out, gram, hots, last_hots, mask, seen, own,
+    pairs, positions, offsets, brightness, cluster, base, spin, parts, sems,
 ):
     copies = [
         pltpu.make_async_copy(source, target, sems.at[index])
@@ -372,11 +373,14 @@
     for start in range(0, sources, step):
         rows = slice(start, start + step)
         geometry = columns[rows, 0:1] * span[0:1] + columns[rows, 1:2] * span[1:2]
-        base[0, rows], base[1, rows] = turn_pair(geometry)
-        spin[0, rows], spin[1, rows] = turn_pair(geometry * (0.5 / channels))
+        c, s = turn_pair(geometry * (0.5 / channels))
+        spin[0, rows], spin[1, rows] = c, s
+        for _ in range((2 * channels).bit_length() - 1):
+            twice = s + s
+            c, s = 1.0 - twice * s, twice * c
+        base[0, rows], base[1, rows] = c, s
 
     directions = out.shape[1] // 12
-    second_run = lax.rem(place.chan, 2) == 1
     member = lax.broadcasted_iota(jnp.int32, (directions, sources), 0) == cluster[...]
     bright = jnp.concatenate([jnp.where(member, brightness[n : n + 1], 0.0) for n in range(4)])
     high, low = pieces(bright, 2)
@@ -403,19 +407,20 @@
         out[channel, :half] = found[0]
         out[channel, half : 2 * half] = found[1]
         out[channel, 2 * half :] = found[0] - found[1]
-        for index in (0, 1):
-            mine = jnp.where(second_run, found[index][:, RUN:], found[index][:, :RUN])
-            share[channel, half * index : half * (index + 1)] = mine
         entries = [found[n // 4][n % 4 * directions : (n % 4 + 1) * directions] for n in range(8)]
         for n, value in enumerate(grams(entries)):
             rows = slice(n * directions, (n + 1) * directions)
             gram[rows] = value if channel == 0 else gram[rows] + value
     for copy in copies[5:]:
         copy.wait()
+
+
+def model_kernel(coherent, hots, own, other, jones, gather, predicted, model):
+    place = Place()
     fill_table(place, jones, own, other)
     gather_gains(jones[...], hots, gather)
     for run in range(2):
-        predict(out, gather, run, model, predicted)
+        predict(coherent, gather, run, model, predicted)
 
 
 def gather_gains(table, hots, gather):
@@ -527,7 +532,7 @@
         w = weight[:, lanes]
         at = pl.multiple_of(place.first_lane + run * RUN, RUN)
         for slot in range(channels):
-            channel = place.slot(slot, per_shard)
+            channel = place.channel_of(slot, per_shard)
             seen = shards[slot // per_shard][:, slot % per_shard, 0, pl.ds(at, RUN)]
             err = w * (seen - predicted[run, channel])
             error[channel, 0] = err
@@ -615,11 +620,17 @@
 
 
 def first_kernel(
-    mask, coherent, gram, hots, gather, predicted, s0, s1, s2, s3, packed, mine, error, sums
+    mask, coherent, gram, hots, gather, predicted, s0, s1, s2, s3, packed, to_core, mine, error, sums
 ):
     place = Place()
+    held = packed.shape[0]
+    count = 8 * (coherent.shape[1] // 12)
+    run = pl.ds(pl.multiple_of(lax.rem(place.chan, 2) * RUN, RUN), RUN)
+    for channel in range(coherent.shape[0]):
+        to_core[held + count * channel : held + count * (channel + 1)] = coherent[channel, :count, run]
     total = iterate(place, coherent, gram, hots, (s0, s1, s2, s3), mask, gather, predicted, error, sums)
-    packed[...] = pack(total[:, :RUN], 8 * (coherent.shape[1] // 12))
+    packed[...] = pack(total[:, :RUN], count)
+    to_core[:held] = packed[...]
     mine[...] = total[:, RUN:]
 
 
@@ -653,6 +664,11 @@
     to_both[held:] = jones[pl.ds(pl.multiple_of((1 - place.core) * half, half), half), RUN:]
 
 
+def shared_of(share, channel, h, rows):
+    start = (rows + rows // 8) // 2 + channel * rows + 8 * h
+    return [share[pl.ds(pl.multiple_of(start + n * (rows // 8), 8), 8)] for n in range(8)]
+
+
 def last_kernel(
     mask, share, other_share, hots, before, p0, p1, p2, p3, s0, s1, s2, s3,
     residual, solved_at, jones, gather, solved, sem,
@@ -684,19 +700,16 @@
     gather_gains(jones[...], hots, gather)
     w = mask[:, pl.ds(place.last_lane, RUN)].astype(jnp.float32)
     shards = (s0, s1, s2, s3)
-    channels = share.shape[0]
     per_shard = s0.shape[1]
+    channels = 4 * per_shard
     gains = [[gains_of(gather, side, 0, h) for h in range(rows // 64)] for side in (0, 1)]
     for slot in range(channels):
-        channel = place.slot(slot, per_shard)
+        channel = place.channel_of(slot, per_shard)
         part = None
         for h in range(rows // 64):
             coh = [
                 jnp.where(owned, a, b)
-                for a, b in zip(
-                    coherent_of(share, channel, h, slice(0, RUN), rows // 8, 8),
-                    coherent_of(other_share, channel, h, slice(0, RUN), rows // 8, 8),
-                )
+                for a, b in zip(shared_of(share, channel, h, rows), shared_of(other_share, channel, h, rows))
             ]
             part = product(product(gains[0][h], coh), gains[1][h], dagger_b=True, total=part)
         seen = shards[slot // per_shard][:, slot % per_shard, 0, pl.ds(place.last_lane, RUN)]
@@ -757,9 +770,15 @@
     sources = source_offsets.shape[1]
 
     other = swap(jones_gains, "dir")
-    shards = [swap(visibilities, "chan", bit) for bit in range(1, relay_count)]
+    places = [(chan, core) for chan in range(relay_count) for core in range(2)]
+    odd = lax.ppermute(
+        visibilities,
+        ("chan", "dir"),
+        [(2 * chan + core, 2 * (chan ^ (1 + 2 * core)) + core) for chan, core in places],
+    )
+    even = swap(visibilities, "chan", 2)
     inputs = (antenna_pairs, station_positions, source_offsets, brightness, source_cluster[None, :])
-    kept = (valid_mask, visibilities)
+    kept = (valid_mask, visibilities, jones_gains)
     held = (rows + directions) // 2
     table = f32(rows, 2 * RUN)
     gathered = f32(2, 2, rows, RUN)
@@ -769,42 +788,43 @@
         pltpu.VMEM((channels, 2, 8, RUN), jnp.float32),
         pltpu.VMEM((2, 2, rows + directions, RUN), jnp.float32),
     ]
-    coherent, share, gram, hots, last_hots, mask, seen, jones, gather, predicted = call(
+    coherent, gram, hots, last_hots, mask, seen, own = call(
         functools.partial(coherency_kernel, channels),
         (
             f32(channels, 12 * directions, PAIR),
-            f32(channels, 8 * directions, RUN),
             f32(8 * directions, PAIR),
             bf16(2, 2 * RUN, PAIR),
             bf16(2, 2 * RUN, RUN),
             *[jax.ShapeDtypeStruct(x.shape, x.dtype) for x in kept],
-            table,
-            gathered,
-            predictions,
         ),
-        [pltpu.VMEM(x.shape, x.dtype) for x in inputs + (jones_gains,)]
+        [pltpu.VMEM(x.shape, x.dtype) for x in inputs]
         + [
             pltpu.VMEM((2, sources, PAIR), jnp.float32),
             pltpu.VMEM((2, sources, PAIR), jnp.float32),
             pltpu.VMEM((2, 2, 2, sources, PAIR), jnp.bfloat16),
-            model,
-            pltpu.SemaphoreType.DMA((len(inputs + kept) + 1,)),
+            pltpu.SemaphoreType.DMA((len(inputs + kept),)),
         ],
-        inputs + kept + (jones_gains, other),
+        inputs + kept,
         4 * 10**9,
-        len(inputs + kept) + 1,
-    )
-    shards = [seen] + shards
-    packed, mine = call(
+        len(inputs + kept),
+    )
+    odd, coherent, hots = lax.optimization_barrier((odd, coherent, hots))
+    shards = [seen, odd, even, swap(odd, "dir")]
+    jones, gather, predicted = call(
+        model_kernel,
+        (table, gathered, predictions),
+        [model],
+        (coherent, hots, own, other),
+        2 * 10**9,
+    )
+    packed, share, mine = call(
         first_kernel,
-        (f32(held, RUN), f32(rows + directions, RUN)),
+        (f32(held, RUN), f32(held + channels * rows, RUN), f32(rows + directions, RUN)),
         scratch,
         (mask, coherent, gram, hots, gather, predicted, *shards),
         10**9,
     )
-    sums = from_three(packed, packed, packed)
-    *sums, share = lax.optimization_barrier((*sums, share))
-    other_share = swap(share, "dir")
+    sums = from_three(share, packed, packed)
     to_core, to_blk, to_both, jones = call(
         second_kernel,
         (f32(held + rows, RUN), f32(held + rows // 2, RUN), f32(held + rows // 2, RUN), table),
@@ -829,7 +849,7 @@
             pltpu.SemaphoreType.DMA,
         ],
         (
-            mask, share, other_share, last_hots, jones,
+            mask, share, sums[0], last_hots, jones,
             to_core, *from_three(to_core, to_blk, to_both), *shards,
         ),
         10**9,
@@ -851,6 +871,7 @@
         and jones[0] == 16
         and jones[2] == BLOCKS * BLOCK
         and visibilities[1] % sizes["chan"] == 0
+        and visibilities[1] & (visibilities[1] - 1) == 0
     )
 
 

time: 26.9 us -> 26.4 us (0.981)
  waiting for transfers between devices: 8 us -> 7.27 us
  starting transfers between devices: 9.84 us -> 10.4 us
  Pallas kernels: 8.18 us -> 7.91 us
    ppermute x0 -> x1, starting transfers between devices: none -> 1.58 us  [per_device_owned(): lax.ppermute(visibilities, ('chan', 'dir'), [(2 * chan + core, 2 * (chan...]
    ppermute x11 -> x9, starting transfers between devices: 9.84 us -> 8.81 us  [swap(): lax.ppermute(x, axis, [(i, i ^ bit) for i in range(lax.axis_size(axis))])]
    ppermute x11 -> x9, waiting for transfers between devices: 8 us -> 7.27 us  [swap(): lax.ppermute(x, axis, [(i, i ^ bit) for i in range(lax.axis_size(axis))])]
    pallas_call x4 -> x5, Pallas kernels: 8.18 us -> 7.91 us  [call(): pl.pallas_call(kernel, out_shape=out_shape, in_specs=[pl.BlockSpec(memory...]
  transfers between devices with their start and end apart: 11 -> 10, of which waited for: 5 -> 5; matrix products, arithmetic and copies ran while one was open for 0% -> 0% of each run, Pallas kernels for 21% -> 14%
where the time goes in v4:
time: 26.4 us; the launch traced here: 26.2 us
  starting transfers between devices  10.4 us (39%)
  Pallas kernels  7.91 us (30%)
  waiting for transfers between devices  7.27 us (28%)
  between operations  0.68 us (3%)
    ppermute x9, starting transfers between devices, swap(): lax.ppermute(x, axis, [(i, i ^ bit) for i in range(lax.axis_size(axis))])  8.81 us
    pallas_call x5, Pallas kernels, call(): pl.pallas_call(kernel, out_shape=out_shape, in_specs=[pl.BlockSpec(memory...  7.91 us
    ppermute x9, waiting for transfers between devices, swap(): lax.ppermute(x, axis, [(i, i ^ bit) for i in range(lax.axis_size(axis))])  7.27 us
    ppermute x1, starting transfers between devices, per_device_owned(): lax.ppermute(visibilities, ('chan', 'dir'), [(2 * chan + core, 2 * (chan...  1.58 us
  transfers between devices with their start and end apart: 10, of which 5 were waited for; matrix products, arithmetic and copies ran while one was open for 0% of the time, Pallas kernels for 14%

profile of v4, /device:TPU:0, one launch (start us, length us, event | category | flops | bytes accessed | tf_op | source)
XLA Modules:
  0.0 26.2 jit_solution(3955381749160282632)
XLA Ops:
  0.6 4.1 %collective-permute-start.2 = (f32[8,2,1,512]{3,2,1,0:T(1,128)}, f32[8,2,1,512]{3,2,1,0:T(1,128)S(1)}, u32[]{:S(2)}, u32[]{:S(2)}) collective-permute-start(f32[8,2,1,512]{3,2,1,0:T(1,128)} %seen_at.1), channel_id=1, source_target_pairs={{0,8},{4,12},{8,0},{12,4},{1,9},{5,13},{9,1},{13,5},{2,10},{6,14},... | collective-permute-start | bytes 98312 | tf_op jit(solution)/shard_map/ppermute | solution.py:748
  4.7 1.6 %collective-permute-start = (f32[8,2,1,512]{3,2,1,0:T(1,128)}, f32[8,2,1,512]{3,2,1,0:T(1,128)S(1)}, u32[]{:S(2)}, u32[]{:S(2)}) collective-permute-start(f32[8,2,1,512]{3,2,1,0:T(1,128)} %seen_at.1), channel_id=1, source_target_pairs={{0,4},{1,13},{4,0},{5,9},{8,12},{9,5},{12,8},{13,1},{2,6},{3,15},{... | collective-permute-start | bytes 98312 | tf_op jit(solution)/shard_map/ppermute | solution.py:774
  6.3 0.0 collective-permute-start.1
  6.3 3.0 %shard_map.95 = (f32[8,192,256]{2,1,0:T(8,128)S(1)}, f32[128,256]{1,0:T(8,128)S(1)}, bf16[2,256,256]{2,1,0:T(8,128)(2,1)S(1)}, bf16[2,256,128]{2,1,0:T(8,128)(2,...) custom-call(s32[2,1,512]{2,1,0:T(1,128)} %pairs_at.1, ...), custom_call_target="tpu_custom_call" | custom-call | flops 4000000000 | bytes 2444288 | tf_op jit(solution)/shard_map/pallas_call | solution.py:722
  9.3 0.0 collective-permute-done.s1
  9.3 0.6 %collective-permute-start.3 = (f32[8,2,1,512]{3,2,1,0:T(1,128)S(1)}, f32[8,2,1,512]{3,2,1,0:T(1,128)S(1)}, u32[]{:S(2)}, u32[]{:S(2)}) collective-permute-start(f32[8,2,1,512]{3,2,1,0:T(1,128)S(1)} %collective-permute-done.s1), channel_id=1, source_target_pairs={{0,1},{1,0},{2,3},{3,2},{4,5},{5,4},{6,7},{7,6},{8,9},{9,8},{10,11... | collective-permute-start | bytes 98312 | tf_op jit(solution)/shard_map/ppermute | solution.py:748
  9.9 0.0 collective-permute-done.1.other
  9.9 0.8 %shard_map.96 = (f32[128,256]{1,0:T(8,128)S(1)}, f32[2,2,128,128]{3,2,1,0:T(8,128)S(1)}, f32[2,8,8,128]{3,2,1,0:T(8,128)S(1)}) custom-call(f32[8,192,256]{2,1,0:T(8,128)S(1)} %get-tuple-element.25.coherent, bf16[2,256,256]{2,1,0:T(8,128)(2,1)S(1)} %get-tuple-element.27.hots, f32[8,8,512]{2,1,0:T(8,128)S(1)} %get-tuple-element.28.own, ...), custom_call_target="tpu_custom_call" | custom-call | flops 2000000000 | bytes 2555904 | tf_op jit(solution)/shard_map/pallas_call | solution.py:722
  10.7 0.0 collective-permute-done.2.s2
  10.7 0.1 collective-permute-done.3.s3
  10.7 1.0 %shard_map.97 = (f32[72,128]{1,0:T(8,128)S(1)}, f32[1096,128]{1,0:T(8,128)S(1)}, f32[144,128]{1,0:T(8,128)S(1)}) custom-call(s32[1,512]{1,0:T(1,128)S(1)} %get-tuple-element.22.mask, f32[8,192,256]{2,1,0:T(8,128)S(1)} %get-tuple-element.25.coherent, f32[128,256]{1,0:T(8,128)S(1)} %get-tuple-element.26.gram, bf16[2,256,256]{2,1,0:T(8,128)(2,1)S(1)} %get-tuple-element.27.hots, ...), custom_call_target="tpu_custom_call" | custom-call | flops 1000000000 | bytes 3098624 | tf_op jit(solution)/shard_map/pallas_call | solution.py:722
  11.8 0.4 %collective-permute-start.4 = (f32[1096,128]{1,0:T(8,128)S(1)}, f32[1096,128]{1,0:T(8,128)S(1)}, u32[]{:S(2)}, u32[]{:S(2)}) collective-permute-start(f32[1096,128]{1,0:T(8,128)S(1)} %get-tuple-element.33.share), channel_id=1, source_target_pairs={{0,1},{1,0},{2,3},{3,2},{4,5},{5,4},{6,7},{7,6},{8,9},{9,8},{10,11... | collective-permute-start | bytes 1683464 | tf_op jit(solution)/shard_map/ppermute | solution.py:748
  12.2 1.3 %collective-permute-start.6 = (f32[72,128]{1,0:T(8,128)S(1)}, f32[72,128]{1,0:T(8,128)S(1)}, u32[]{:S(2)}, u32[]{:S(2)}) collective-permute-start(f32[72,128]{1,0:T(8,128)S(1)} %get-tuple-element.37.p0), channel_id=1, source_target_pairs={{0,3},{1,2},{2,1},{3,0},{4,7},{5,6},{6,5},{7,4},{8,11},{9,10},{10,... | collective-permute-start | bytes 110600 | tf_op jit(solution)/shard_map/ppermute | solution.py:748
  13.4 0.5 %collective-permute-start.5 = (f32[72,128]{1,0:T(8,128)S(1)}, f32[72,128]{1,0:T(8,128)S(1)}, u32[]{:S(2)}, u32[]{:S(2)}) collective-permute-start(f32[72,128]{1,0:T(8,128)S(1)} %get-tuple-element.37.p0), channel_id=1, source_target_pairs={{0,2},{2,0},{1,3},{3,1},{4,6},{6,4},{5,7},{7,5},{8,10},{10,8},{9,1... | collective-permute-start | bytes 110600 | tf_op jit(solution)/shard_map/ppermute | solution.py:748
  14.0 1.6 %collective-permute-done.6.p3 = f32[72,128]{1,0:T(8,128)S(1)} collective-permute-done((f32[72,128]{1,0:T(8,128)S(1)}, f32[72,128]{1,0:T(8,128)S(1)}, u32[]{:S(2)}, u32[]{:S(2)}) %collective-permute-start.6) | collective-permute-done | bytes 36896 | tf_op jit(solution)/shard_map/ppermute | solution.py:748
  15.6 1.8 %collective-permute-done.5.p2 = f32[72,128]{1,0:T(8,128)S(1)} collective-permute-done((f32[72,128]{1,0:T(8,128)S(1)}, f32[72,128]{1,0:T(8,128)S(1)}, u32[]{:S(2)}, u32[]{:S(2)}) %collective-permute-start.5) | collective-permute-done | bytes 36896 | tf_op jit(solution)/shard_map/ppermute | solution.py:748
  17.4 0.0 collective-permute-done.4.p1.other_share
  17.4 1.8 %shard_map.98 = (f32[200,128]{1,0:T(8,128)S(1)}, f32[136,128]{1,0:T(8,128)S(1)}, f32[136,128]{1,0:T(8,128)S(1)}, f32[128,256]{1,0:T(8,128)S(1)}) custom-call(s32[1,512]{1,0:T(1,128)S(1)} %get-tuple-element.22.mask, f32[8,192,256]{2,1,0:T(8,128)S(1)} %get-tuple-element.25.coherent, f32[128,256]{1,0:T(8,128)S(1)} %get-tuple-element.26.gram, ...), custom_call_target="tpu_custom_call" | custom-call | flops 2000000000 | bytes 3348480 | tf_op jit(solution)/shard_map/pallas_call | solution.py:722
  19.2 0.1 collective-permute-start.7
  19.2 0.9 %collective-permute-start.8 = (f32[136,128]{1,0:T(8,128)S(1)}, f32[136,128]{1,0:T(8,128)S(1)}, u32[]{:S(2)}, u32[]{:S(2)}) collective-permute-start(f32[136,128]{1,0:T(8,128)S(1)} %get-tuple-element.40), channel_id=1, source_target_pairs={{0,2},{2,0},{1,3},{3,1},{4,6},{6,4},{5,7},{7,5},{8,10},{10,8},{9,1... | collective-permute-start | bytes 208904 | tf_op jit(solution)/shard_map/ppermute | solution.py:748
  20.1 1.0 %collective-permute-start.9 = (f32[136,128]{1,0:T(8,128)S(1)}, f32[136,128]{1,0:T(8,128)S(1)}, u32[]{:S(2)}, u32[]{:S(2)}) collective-permute-start(f32[136,128]{1,0:T(8,128)S(1)} %get-tuple-element.41), channel_id=1, source_target_pairs={{0,3},{1,2},{2,1},{3,0},{4,7},{5,6},{6,5},{7,4},{8,11},{9,10},{10,... | collective-permute-start | bytes 208904 | tf_op jit(solution)/shard_map/ppermute | solution.py:748
  21.1 3.2 %collective-permute-done.8.p2 = f32[136,128]{1,0:T(8,128)S(1)} collective-permute-done((f32[136,128]{1,0:T(8,128)S(1)}, f32[136,128]{1,0:T(8,128)S(1)}, u32[]{:S(2)}, u32[]{:S(2)}) %collective-permute-start.8) | collective-permute-done | bytes 69664 | tf_op jit(solution)/shard_map/ppermute | solution.py:748
  24.3 0.6 %collective-permute-done.9.p3 = f32[136,128]{1,0:T(8,128)S(1)} collective-permute-done((f32[136,128]{1,0:T(8,128)S(1)}, f32[136,128]{1,0:T(8,128)S(1)}, u32[]{:S(2)}, u32[]{:S(2)}) %collective-permute-start.9) | collective-permute-done | bytes 69664 | tf_op jit(solution)/shard_map/ppermute | solution.py:748
  24.9 0.0 collective-permute-done.7.p1
  24.9 1.4 %shard_map.99 = (f32[8,8,1,128]{3,2,1,0:T(1,128)}, f32[8,8,512]{2,1,0:T(8,128)}) custom-call(s32[1,512]{1,0:T(1,128)S(1)} %get-tuple-element.22.mask, f32[1096,128]{1,0:T(8,128)S(1)} %get-tuple-element.33.share, f32[1096,128]{1,0:T(8,128)S(1)} %collective-permute-done.4.p1.other_share, bf16[2,256,128]{2,1,0:T(8,128)(2,1)S(1)} %get-tuple-element.34.hots, ...), custom_call_target="tpu_custom_call" | custom-call | flops 1000000000 | bytes 2025472 | tf_op jit(solution)/shard_map/pallas_call | solution.py:722
Async XLA Ops:
  0.6 10.0 %collective-permute-start.2 = (f32[8,2,1,512]{3,2,1,0:T(1,128)}, f32[8,2,1,512]{3,2,1,0:T(1,128)S(1)}, u32[]{:S(2)}, u32[]{:S(2)}) collective-permute-start(f32[8,2,1,512]{3,2,1,0:T(1,128)} %seen_at.1), channel_id=1, source_target_pairs={{0,8},{4,12},{8,0},{12,4},{1,9},{5,13},{9,1},{13,5},{2,10},{6,14},... | collective-permute-start | bytes 98312 | tf_op jit(solution)/shard_map/ppermute | solution.py:748
  4.7 4.6 %collective-permute-start = (f32[8,2,1,512]{3,2,1,0:T(1,128)}, f32[8,2,1,512]{3,2,1,0:T(1,128)S(1)}, u32[]{:S(2)}, u32[]{:S(2)}) collective-permute-start(f32[8,2,1,512]{3,2,1,0:T(1,128)} %seen_at.1), channel_id=1, source_target_pairs={{0,4},{1,13},{4,0},{5,9},{8,12},{9,5},{12,8},{13,1},{2,6},{3,15},{... | collective-permute-start | bytes 98312 | tf_op jit(solution)/shard_map/ppermute | solution.py:774
  6.3 3.6 %collective-permute-start.1 = (f32[8,8,512]{2,1,0:T(8,128)}, f32[8,8,512]{2,1,0:T(8,128)S(1)}, u32[]{:S(2)}, u32[]{:S(2)}) collective-permute-start(f32[8,8,512]{2,1,0:T(8,128)} %own_at.1), channel_id=1, source_target_pairs={{0,1},{1,0},{2,3},{3,2},{4,5},{5,4},{6,7},{7,6},{8,9},{9,8},{10,11... | collective-permute-start | bytes 393224 | tf_op jit(solution)/shard_map/ppermute | solution.py:748
  9.3 1.4 %collective-permute-start.3 = (f32[8,2,1,512]{3,2,1,0:T(1,128)S(1)}, f32[8,2,1,512]{3,2,1,0:T(1,128)S(1)}, u32[]{:S(2)}, u32[]{:S(2)}) collective-permute-start(f32[8,2,1,512]{3,2,1,0:T(1,128)S(1)} %collective-permute-done.s1), channel_id=1, source_target_pairs={{0,1},{1,0},{2,3},{3,2},{4,5},{5,4},{6,7},{7,6},{8,9},{9,8},{10,11... | collective-permute-start | bytes 98312 | tf_op jit(solution)/shard_map/ppermute | solution.py:748
  11.8 5.6 %collective-permute-start.4 = (f32[1096,128]{1,0:T(8,128)S(1)}, f32[1096,128]{1,0:T(8,128)S(1)}, u32[]{:S(2)}, u32[]{:S(2)}) collective-permute-start(f32[1096,128]{1,0:T(8,128)S(1)} %get-tuple-element.33.share), channel_id=1, source_target_pairs={{0,1},{1,0},{2,3},{3,2},{4,5},{5,4},{6,7},{7,6},{8,9},{9,8},{10,11... | collective-permute-start | bytes 1683464 | tf_op jit(solution)/shard_map/ppermute | solution.py:748
  12.2 3.4 %collective-permute-start.6 = (f32[72,128]{1,0:T(8,128)S(1)}, f32[72,128]{1,0:T(8,128)S(1)}, u32[]{:S(2)}, u32[]{:S(2)}) collective-permute-start(f32[72,128]{1,0:T(8,128)S(1)} %get-tuple-element.37.p0), channel_id=1, source_target_pairs={{0,3},{1,2},{2,1},{3,0},{4,7},{5,6},{6,5},{7,4},{8,11},{9,10},{10,... | collective-permute-start | bytes 110600 | tf_op jit(solution)/shard_map/ppermute | solution.py:748
  13.4 4.0 %collective-permute-start.5 = (f32[72,128]{1,0:T(8,128)S(1)}, f32[72,128]{1,0:T(8,128)S(1)}, u32[]{:S(2)}, u32[]{:S(2)}) collective-permute-start(f32[72,128]{1,0:T(8,128)S(1)} %get-tuple-element.37.p0), channel_id=1, source_target_pairs={{0,2},{2,0},{1,3},{3,1},{4,6},{6,4},{5,7},{7,5},{8,10},{10,8},{9,1... | collective-permute-start | bytes 110600 | tf_op jit(solution)/shard_map/ppermute | solution.py:748
  19.2 5.7 %collective-permute-start.7 = (f32[200,128]{1,0:T(8,128)S(1)}, f32[200,128]{1,0:T(8,128)S(1)}, u32[]{:S(2)}, u32[]{:S(2)}) collective-permute-start(f32[200,128]{1,0:T(8,128)S(1)} %get-tuple-element.39.p0), channel_id=1, source_target_pairs={{0,1},{1,0},{2,3},{3,2},{4,5},{5,4},{6,7},{7,6},{8,9},{9,8},{10,11... | collective-permute-start | bytes 307208 | tf_op jit(solution)/shard_map/ppermute | solution.py:748
  19.2 5.0 %collective-permute-start.8 = (f32[136,128]{1,0:T(8,128)S(1)}, f32[136,128]{1,0:T(8,128)S(1)}, u32[]{:S(2)}, u32[]{:S(2)}) collective-permute-start(f32[136,128]{1,0:T(8,128)S(1)} %get-tuple-element.40), channel_id=1, source_target_pairs={{0,2},{2,0},{1,3},{3,1},{4,6},{6,4},{5,7},{7,5},{8,10},{10,8},{9,1... | collective-permute-start | bytes 208904 | tf_op jit(solution)/shard_map/ppermute | solution.py:748
  20.1 4.7 %collective-permute-start.9 = (f32[136,128]{1,0:T(8,128)S(1)}, f32[136,128]{1,0:T(8,128)S(1)}, u32[]{:S(2)}, u32[]{:S(2)}) collective-permute-start(f32[136,128]{1,0:T(8,128)S(1)} %get-tuple-element.41), channel_id=1, source_target_pairs={{0,3},{1,2},{2,1},{3,0},{4,7},{5,6},{6,5},{7,4},{8,11},{9,10},{10,... | collective-permute-start | bytes 208904 | tf_op jit(solution)/shard_map/ppermute | solution.py:748

commit v5 on v4

--- a/solution.py
+++ b/solution.py
@@ -333,7 +333,7 @@
 
 def coherency_kernel(
     channels, pairs_at, positions_at, offsets_at, brightness_at, cluster_at, mask_at, seen_at, own_at,
-    out, gram, hots, last_hots, mask, seen, own,
+    out, share, gram, hots, last_hots, mask, seen, own,
     pairs, positions, offsets, brightness, cluster, base, spin, parts, sems,
 ):
     copies = [
@@ -381,6 +381,7 @@
         base[0, rows], base[1, rows] = c, s
 
     directions = out.shape[1] // 12
+    second_run = lax.rem(place.chan, 2) == 1
     member = lax.broadcasted_iota(jnp.int32, (directions, sources), 0) == cluster[...]
     bright = jnp.concatenate([jnp.where(member, brightness[n : n + 1], 0.0) for n in range(4)])
     high, low = pieces(bright, 2)
@@ -407,6 +408,9 @@
         out[channel, :half] = found[0]
         out[channel, half : 2 * half] = found[1]
         out[channel, 2 * half :] = found[0] - found[1]
+        for index in (0, 1):
+            mine = jnp.where(second_run, found[index][:, RUN:], found[index][:, :RUN])
+            share[channel, half * index : half * (index + 1)] = mine
         entries = [found[n // 4][n % 4 * directions : (n % 4 + 1) * directions] for n in range(8)]
         for n, value in enumerate(grams(entries)):
             rows = slice(n * directions, (n + 1) * directions)
@@ -620,17 +624,11 @@
 
 
 def first_kernel(
-    mask, coherent, gram, hots, gather, predicted, s0, s1, s2, s3, packed, to_core, mine, error, sums
+    mask, coherent, gram, hots, gather, predicted, s0, s1, s2, s3, packed, mine, error, sums
 ):
     place = Place()
-    held = packed.shape[0]
-    count = 8 * (coherent.shape[1] // 12)
-    run = pl.ds(pl.multiple_of(lax.rem(place.chan, 2) * RUN, RUN), RUN)
-    for channel in range(coherent.shape[0]):
-        to_core[held + count * channel : held + count * (channel + 1)] = coherent[channel, :count, run]
     total = iterate(place, coherent, gram, hots, (s0, s1, s2, s3), mask, gather, predicted, error, sums)
-    packed[...] = pack(total[:, :RUN], count)
-    to_core[:held] = packed[...]
+    packed[...] = pack(total[:, :RUN], 8 * (coherent.shape[1] // 12))
     mine[...] = total[:, RUN:]
 
 
@@ -664,11 +662,6 @@
     to_both[held:] = jones[pl.ds(pl.multiple_of((1 - place.core) * half, half), half), RUN:]
 
 
-def shared_of(share, channel, h, rows):
-    start = (rows + rows // 8) // 2 + channel * rows + 8 * h
-    return [share[pl.ds(pl.multiple_of(start + n * (rows // 8), 8), 8)] for n in range(8)]
-
-
 def last_kernel(
     mask, share, other_share, hots, before, p0, p1, p2, p3, s0, s1, s2, s3,
     residual, solved_at, jones, gather, solved, sem,
@@ -700,8 +693,8 @@
     gather_gains(jones[...], hots, gather)
     w = mask[:, pl.ds(place.last_lane, RUN)].astype(jnp.float32)
     shards = (s0, s1, s2, s3)
+    channels = share.shape[0]
     per_shard = s0.shape[1]
-    channels = 4 * per_shard
     gains = [[gains_of(gather, side, 0, h) for h in range(rows // 64)] for side in (0, 1)]
     for slot in range(channels):
         channel = place.channel_of(slot, per_shard)
@@ -709,7 +702,10 @@
         for h in range(rows // 64):
             coh = [
                 jnp.where(owned, a, b)
-                for a, b in zip(shared_of(share, channel, h, rows), shared_of(other_share, channel, h, rows))
+                for a, b in zip(
+                    coherent_of(share, channel, h, slice(0, RUN), rows // 8, 8),
+                    coherent_of(other_share, channel, h, slice(0, RUN), rows // 8, 8),
+                )
             ]
             part = product(product(gains[0][h], coh), gains[1][h], dagger_b=True, total=part)
         seen = shards[slot // per_shard][:, slot % per_shard, 0, pl.ds(place.last_lane, RUN)]
@@ -788,10 +784,11 @@
         pltpu.VMEM((channels, 2, 8, RUN), jnp.float32),
         pltpu.VMEM((2, 2, rows + directions, RUN), jnp.float32),
     ]
-    coherent, gram, hots, last_hots, mask, seen, own = call(
+    coherent, share, gram, hots, last_hots, mask, seen, own = call(
         functools.partial(coherency_kernel, channels),
         (
             f32(channels, 12 * directions, PAIR),
+            f32(channels, 8 * directions, RUN),
             f32(8 * directions, PAIR),
             bf16(2, 2 * RUN, PAIR),
             bf16(2, 2 * RUN, RUN),
@@ -808,8 +805,9 @@
         4 * 10**9,
         len(inputs + kept),
     )
-    odd, coherent, hots = lax.optimization_barrier((odd, coherent, hots))
+    odd, coherent, hots, share = lax.optimization_barrier((odd, coherent, hots, share))
     shards = [seen, odd, even, swap(odd, "dir")]
+    other_share = swap(share, "dir")
     jones, gather, predicted = call(
         model_kernel,
         (table, gathered, predictions),
@@ -817,14 +815,14 @@
         (coherent, hots, own, other),
         2 * 10**9,
     )
-    packed, share, mine = call(
+    packed, mine = call(
         first_kernel,
-        (f32(held, RUN), f32(held + channels * rows, RUN), f32(rows + directions, RUN)),
+        (f32(held, RUN), f32(rows + directions, RUN)),
         scratch,
         (mask, coherent, gram, hots, gather, predicted, *shards),
         10**9,
     )
-    sums = from_three(share, packed, packed)
+    sums = from_three(packed, packed, packed)
     to_core, to_blk, to_both, jones = call(
         second_kernel,
         (f32(held + rows, RUN), f32(held + rows // 2, RUN), f32(held + rows // 2, RUN), table),
@@ -849,7 +847,7 @@
             pltpu.SemaphoreType.DMA,
         ],
         (
-            mask, share, sums[0], last_hots, jones,
+            mask, share, other_share, last_hots, jones,
             to_core, *from_three(to_core, to_blk, to_both), *shards,
         ),
         10**9,

time: 26.4 us -> 26.4 us (level)
    ppermute x9 -> x10, waiting for transfers between devices: 7.27 us -> 7.2 us  [swap(): lax.ppermute(x, axis, [(i, i ^ bit) for i in range(lax.axis_size(axis))])]
    ppermute x9 -> x10, starting transfers between devices: 8.81 us -> 8.83 us  [swap(): lax.ppermute(x, axis, [(i, i ^ bit) for i in range(lax.axis_size(axis))])]
  transfers between devices with their start and end apart: 10 -> 11, of which waited for: 5 -> 4; matrix products, arithmetic and copies ran while one was open for 0% -> 0% of each run, Pallas kernels for 14% -> 25%
where the time goes in v5:
time: 26.4 us; the launch traced here: 26.2 us
  starting transfers between devices  10.4 us (39%)
  Pallas kernels  7.9 us (30%)
  waiting for transfers between devices  7.21 us (27%)
  between operations  0.69 us (3%)
    ppermute x10, starting transfers between devices, swap(): lax.ppermute(x, axis, [(i, i ^ bit) for i in range(lax.axis_size(axis))])  8.83 us
    pallas_call x5, Pallas kernels, call(): pl.pallas_call(kernel, out_shape=out_shape, in_specs=[pl.BlockSpec(memory...  7.9 us
    ppermute x10, waiting for transfers between devices, swap(): lax.ppermute(x, axis, [(i, i ^ bit) for i in range(lax.axis_size(axis))])  7.2 us
    ppermute x1, starting transfers between devices, per_device_owned(): lax.ppermute(visibilities, ('chan', 'dir'), [(2 * chan + core, 2 * (chan...  1.58 us
  transfers between devices with their start and end apart: 11, of which 4 were waited for; matrix products, arithmetic and copies ran while one was open for 0% of the time, Pallas kernels for 25%

profile of v5, /device:TPU:0, one launch (start us, length us, event | category | flops | bytes accessed | tf_op | source)
XLA Modules:
  0.0 26.2 jit_solution(4154572327442528259)
XLA Ops:
  0.6 4.1 %collective-permute-start.3 = (f32[8,2,1,512]{3,2,1,0:T(1,128)}, f32[8,2,1,512]{3,2,1,0:T(1,128)S(1)}, u32[]{:S(2)}, u32[]{:S(2)}) collective-permute-start(f32[8,2,1,512]{3,2,1,0:T(1,128)} %seen_at.1), channel_id=1, source_target_pairs={{0,8},{4,12},{8,0},{12,4},{1,9},{5,13},{9,1},{13,5},{2,10},{6,14},... | collective-permute-start | bytes 98312 | tf_op jit(solution)/shard_map/ppermute | solution.py:744
  4.7 1.6 %collective-permute-start = (f32[8,2,1,512]{3,2,1,0:T(1,128)}, f32[8,2,1,512]{3,2,1,0:T(1,128)S(1)}, u32[]{:S(2)}, u32[]{:S(2)}) collective-permute-start(f32[8,2,1,512]{3,2,1,0:T(1,128)} %seen_at.1), channel_id=1, source_target_pairs={{0,4},{1,13},{4,0},{5,9},{8,12},{9,5},{12,8},{13,1},{2,6},{3,15},{... | collective-permute-start | bytes 98312 | tf_op jit(solution)/shard_map/ppermute | solution.py:770
  6.3 0.0 collective-permute-start.2
  6.3 3.0 %shard_map.95 = (f32[8,192,256]{2,1,0:T(8,128)S(1)}, f32[8,128,128]{2,1,0:T(8,128)S(1)}, f32[128,256]{1,0:T(8,128)S(1)}, bf16[2,256,256]{2,1,0:T(8,128)(2,1)S(1)...) custom-call(s32[2,1,512]{2,1,0:T(1,128)} %pairs_at.1, ...), custom_call_target="tpu_custom_call" | custom-call | flops 4000000000 | bytes 2968576 | tf_op jit(solution)/shard_map/pallas_call | solution.py:718
  9.3 0.0 collective-permute-done.s1
  9.3 0.6 %collective-permute-start.4 = (f32[8,2,1,512]{3,2,1,0:T(1,128)S(1)}, f32[8,2,1,512]{3,2,1,0:T(1,128)S(1)}, u32[]{:S(2)}, u32[]{:S(2)}) collective-permute-start(f32[8,2,1,512]{3,2,1,0:T(1,128)S(1)} %collective-permute-done.s1), channel_id=1, source_target_pairs={{0,1},{1,0},{2,3},{3,2},{4,5},{5,4},{6,7},{7,6},{8,9},{9,8},{10,11... | collective-permute-start | bytes 98312 | tf_op jit(solution)/shard_map/ppermute | solution.py:744
  9.9 0.1 collective-permute-start.1
  10.0 0.0 collective-permute-done.2.other
  10.0 0.8 %shard_map.96 = (f32[128,256]{1,0:T(8,128)S(1)}, f32[2,2,128,128]{3,2,1,0:T(8,128)S(1)}, f32[2,8,8,128]{3,2,1,0:T(8,128)S(1)}) custom-call(f32[8,192,256]{2,1,0:T(8,128)S(1)} %get-tuple-element.29.coherent, bf16[2,256,256]{2,1,0:T(8,128)(2,1)S(1)} %get-tuple-element.31.hots, f32[8,8,512]{2,1,0:T(8,128)S(1)} %get-tuple-element.32.own, ...), custom_call_target="tpu_custom_call" | custom-call | flops 2000000000 | bytes 2555904 | tf_op jit(solution)/shard_map/pallas_call | solution.py:718
  10.7 0.0 collective-permute-done.3.s2
  10.8 0.0 collective-permute-done.4.s3
  10.8 1.0 %shard_map.97 = (f32[72,128]{1,0:T(8,128)S(1)}, f32[144,128]{1,0:T(8,128)S(1)}) custom-call(s32[1,512]{1,0:T(1,128)S(1)} %get-tuple-element.23.mask, f32[8,192,256]{2,1,0:T(8,128)S(1)} %get-tuple-element.29.coherent, f32[128,256]{1,0:T(8,128)S(1)} %get-tuple-element.30.gram, bf16[2,256,256]{2,1,0:T(8,128)(2,1)S(1)} %get-tuple-element.31.hots, ...), custom_call_target="tpu_custom_call" | custom-call | flops 1000000000 | bytes 2537472 | tf_op jit(solution)/shard_map/pallas_call | solution.py:718
  11.8 1.6 %collective-permute-start.7 = (f32[72,128]{1,0:T(8,128)S(1)}, f32[72,128]{1,0:T(8,128)S(1)}, u32[]{:S(2)}, u32[]{:S(2)}) collective-permute-start(f32[72,128]{1,0:T(8,128)S(1)} %get-tuple-element.39.p0), channel_id=1, source_target_pairs={{0,3},{1,2},{2,1},{3,0},{4,7},{5,6},{6,5},{7,4},{8,11},{9,10},{10,... | collective-permute-start | bytes 110600 | tf_op jit(solution)/shard_map/ppermute | solution.py:744
  13.4 0.5 %collective-permute-start.6 = (f32[72,128]{1,0:T(8,128)S(1)}, f32[72,128]{1,0:T(8,128)S(1)}, u32[]{:S(2)}, u32[]{:S(2)}) collective-permute-start(f32[72,128]{1,0:T(8,128)S(1)} %get-tuple-element.39.p0), channel_id=1, source_target_pairs={{0,2},{2,0},{1,3},{3,1},{4,6},{6,4},{5,7},{7,5},{8,10},{10,8},{9,1... | collective-permute-start | bytes 110600 | tf_op jit(solution)/shard_map/ppermute | solution.py:744
  13.9 0.0 collective-permute-start.5
  13.9 1.3 %collective-permute-done.7.p3 = f32[72,128]{1,0:T(8,128)S(1)} collective-permute-done((f32[72,128]{1,0:T(8,128)S(1)}, f32[72,128]{1,0:T(8,128)S(1)}, u32[]{:S(2)}, u32[]{:S(2)}) %collective-permute-start.7) | collective-permute-done | bytes 36896 | tf_op jit(solution)/shard_map/ppermute | solution.py:744
  15.2 2.1 %collective-permute-done.6.p2 = f32[72,128]{1,0:T(8,128)S(1)} collective-permute-done((f32[72,128]{1,0:T(8,128)S(1)}, f32[72,128]{1,0:T(8,128)S(1)}, u32[]{:S(2)}, u32[]{:S(2)}) %collective-permute-start.6) | collective-permute-done | bytes 36896 | tf_op jit(solution)/shard_map/ppermute | solution.py:744
  17.4 0.0 collective-permute-done.5.p1
  17.4 1.7 %shard_map.98 = (f32[200,128]{1,0:T(8,128)S(1)}, f32[136,128]{1,0:T(8,128)S(1)}, f32[136,128]{1,0:T(8,128)S(1)}, f32[128,256]{1,0:T(8,128)S(1)}) custom-call(s32[1,512]{1,0:T(1,128)S(1)} %get-tuple-element.23.mask, f32[8,192,256]{2,1,0:T(8,128)S(1)} %get-tuple-element.29.coherent, f32[128,256]{1,0:T(8,128)S(1)} %get-tuple-element.30.gram, ...), custom_call_target="tpu_custom_call" | custom-call | flops 2000000000 | bytes 2824192 | tf_op jit(solution)/shard_map/pallas_call | solution.py:718
  19.1 0.1 collective-permute-start.8
  19.2 0.6 %collective-permute-start.9 = (f32[136,128]{1,0:T(8,128)S(1)}, f32[136,128]{1,0:T(8,128)S(1)}, u32[]{:S(2)}, u32[]{:S(2)}) collective-permute-start(f32[136,128]{1,0:T(8,128)S(1)} %get-tuple-element.42), channel_id=1, source_target_pairs={{0,2},{2,0},{1,3},{3,1},{4,6},{6,4},{5,7},{7,5},{8,10},{10,8},{9,1... | collective-permute-start | bytes 208904 | tf_op jit(solution)/shard_map/ppermute | solution.py:744
  19.8 1.2 %collective-permute-start.10 = (f32[136,128]{1,0:T(8,128)S(1)}, f32[136,128]{1,0:T(8,128)S(1)}, u32[]{:S(2)}, u32[]{:S(2)}) collective-permute-start(f32[136,128]{1,0:T(8,128)S(1)} %get-tuple-element.43), channel_id=1, source_target_pairs={{0,3},{1,2},{2,1},{3,0},{4,7},{5,6},{6,5},{7,4},{8,11},{9,10},{10,... | collective-permute-start | bytes 208904 | tf_op jit(solution)/shard_map/ppermute | solution.py:744
  21.1 3.2 %collective-permute-done.9.p2 = f32[136,128]{1,0:T(8,128)S(1)} collective-permute-done((f32[136,128]{1,0:T(8,128)S(1)}, f32[136,128]{1,0:T(8,128)S(1)}, u32[]{:S(2)}, u32[]{:S(2)}) %collective-permute-start.9) | collective-permute-done | bytes 69664 | tf_op jit(solution)/shard_map/ppermute | solution.py:744
  24.2 0.6 %collective-permute-done.10.p3 = f32[136,128]{1,0:T(8,128)S(1)} collective-permute-done((f32[136,128]{1,0:T(8,128)S(1)}, f32[136,128]{1,0:T(8,128)S(1)}, u32[]{:S(2)}, u32[]{:S(2)}) %collective-permute-start.10) | collective-permute-done | bytes 69664 | tf_op jit(solution)/shard_map/ppermute | solution.py:744
  24.8 0.0 collective-permute-done.8.p1
  24.8 0.0 collective-permute-done.1.other_share
  24.8 1.4 %shard_map.99 = (f32[8,8,1,128]{3,2,1,0:T(1,128)}, f32[8,8,512]{2,1,0:T(8,128)}) custom-call(s32[1,512]{1,0:T(1,128)S(1)} %get-tuple-element.23.mask, f32[8,128,128]{2,1,0:T(8,128)S(1)} %get-tuple-element.27.share, f32[8,128,128]{2,1,0:T(8,128)S(1)} %collective-permute-done.1.other_share, bf16[2,256,128]{2,1,0:T(8,128)(2,1)S(1)} %get-tuple-element.28.hots, ...), custom_call_target="tpu_custom_call" | custom-call | flops 1000000000 | bytes 1951744 | tf_op jit(solution)/shard_map/pallas_call | solution.py:718
Async XLA Ops:
  0.6 10.1 %collective-permute-start.3 = (f32[8,2,1,512]{3,2,1,0:T(1,128)}, f32[8,2,1,512]{3,2,1,0:T(1,128)S(1)}, u32[]{:S(2)}, u32[]{:S(2)}) collective-permute-start(f32[8,2,1,512]{3,2,1,0:T(1,128)} %seen_at.1), channel_id=1, source_target_pairs={{0,8},{4,12},{8,0},{12,4},{1,9},{5,13},{9,1},{13,5},{2,10},{6,14},... | collective-permute-start | bytes 98312 | tf_op jit(solution)/shard_map/ppermute | solution.py:744
  4.7 4.6 %collective-permute-start = (f32[8,2,1,512]{3,2,1,0:T(1,128)}, f32[8,2,1,512]{3,2,1,0:T(1,128)S(1)}, u32[]{:S(2)}, u32[]{:S(2)}) collective-permute-start(f32[8,2,1,512]{3,2,1,0:T(1,128)} %seen_at.1), channel_id=1, source_target_pairs={{0,4},{1,13},{4,0},{5,9},{8,12},{9,5},{12,8},{13,1},{2,6},{3,15},{... | collective-permute-start | bytes 98312 | tf_op jit(solution)/shard_map/ppermute | solution.py:770
  6.3 3.7 %collective-permute-start.2 = (f32[8,8,512]{2,1,0:T(8,128)}, f32[8,8,512]{2,1,0:T(8,128)S(1)}, u32[]{:S(2)}, u32[]{:S(2)}) collective-permute-start(f32[8,8,512]{2,1,0:T(8,128)} %own_at.1), channel_id=1, source_target_pairs={{0,1},{1,0},{2,3},{3,2},{4,5},{5,4},{6,7},{7,6},{8,9},{9,8},{10,11... | collective-permute-start | bytes 393224 | tf_op jit(solution)/shard_map/ppermute | solution.py:744
  9.3 1.5 %collective-permute-start.4 = (f32[8,2,1,512]{3,2,1,0:T(1,128)S(1)}, f32[8,2,1,512]{3,2,1,0:T(1,128)S(1)}, u32[]{:S(2)}, u32[]{:S(2)}) collective-permute-start(f32[8,2,1,512]{3,2,1,0:T(1,128)S(1)} %collective-permute-done.s1), channel_id=1, source_target_pairs={{0,1},{1,0},{2,3},{3,2},{4,5},{5,4},{6,7},{7,6},{8,9},{9,8},{10,11... | collective-permute-start | bytes 98312 | tf_op jit(solution)/shard_map/ppermute | solution.py:744
  9.9 14.9 %collective-permute-start.1 = (f32[8,128,128]{2,1,0:T(8,128)S(1)}, f32[8,128,128]{2,1,0:T(8,128)S(1)}, u32[]{:S(2)}, u32[]{:S(2)}) collective-permute-start(f32[8,128,128]{2,1,0:T(8,128)S(1)} %get-tuple-element.27.share), channel_id=1, source_target_pairs={{0,1},{1,0},{2,3},{3,2},{4,5},{5,4},{6,7},{7,6},{8,9},{9,8},{10,11... | collective-permute-start | bytes 1572872 | tf_op jit(solution)/shard_map/ppermute | solution.py:744
  11.8 3.4 %collective-permute-start.7 = (f32[72,128]{1,0:T(8,128)S(1)}, f32[72,128]{1,0:T(8,128)S(1)}, u32[]{:S(2)}, u32[]{:S(2)}) collective-permute-start(f32[72,128]{1,0:T(8,128)S(1)} %get-tuple-element.39.p0), channel_id=1, source_target_pairs={{0,3},{1,2},{2,1},{3,0},{4,7},{5,6},{6,5},{7,4},{8,11},{9,10},{10,... | collective-permute-start | bytes 110600 | tf_op jit(solution)/shard_map/ppermute | solution.py:744
  13.4 4.0 %collective-permute-start.6 = (f32[72,128]{1,0:T(8,128)S(1)}, f32[72,128]{1,0:T(8,128)S(1)}, u32[]{:S(2)}, u32[]{:S(2)}) collective-permute-start(f32[72,128]{1,0:T(8,128)S(1)} %get-tuple-element.39.p0), channel_id=1, source_target_pairs={{0,2},{2,0},{1,3},{3,1},{4,6},{6,4},{5,7},{7,5},{8,10},{10,8},{9,1... | collective-permute-start | bytes 110600 | tf_op jit(solution)/shard_map/ppermute | solution.py:744
  13.9 3.4 %collective-permute-start.5 = (f32[72,128]{1,0:T(8,128)S(1)}, f32[72,128]{1,0:T(8,128)S(1)}, u32[]{:S(2)}, u32[]{:S(2)}) collective-permute-start(f32[72,128]{1,0:T(8,128)S(1)} %get-tuple-element.39.p0), channel_id=1, source_target_pairs={{0,1},{1,0},{2,3},{3,2},{4,5},{5,4},{6,7},{7,6},{8,9},{9,8},{10,11... | collective-permute-start | bytes 110600 | tf_op jit(solution)/shard_map/ppermute | solution.py:744
  19.1 5.7 %collective-permute-start.8 = (f32[200,128]{1,0:T(8,128)S(1)}, f32[200,128]{1,0:T(8,128)S(1)}, u32[]{:S(2)}, u32[]{:S(2)}) collective-permute-start(f32[200,128]{1,0:T(8,128)S(1)} %get-tuple-element.41.p0), channel_id=1, source_target_pairs={{0,1},{1,0},{2,3},{3,2},{4,5},{5,4},{6,7},{7,6},{8,9},{9,8},{10,11... | collective-permute-start | bytes 307208 | tf_op jit(solution)/shard_map/ppermute | solution.py:744
  19.2 5.0 %collective-permute-start.9 = (f32[136,128]{1,0:T(8,128)S(1)}, f32[136,128]{1,0:T(8,128)S(1)}, u32[]{:S(2)}, u32[]{:S(2)}) collective-permute-start(f32[136,128]{1,0:T(8,128)S(1)} %get-tuple-element.42), channel_id=1, source_target_pairs={{0,2},{2,0},{1,3},{3,1},{4,6},{6,4},{5,7},{7,5},{8,10},{10,8},{9,1... | collective-permute-start | bytes 208904 | tf_op jit(solution)/shard_map/ppermute | solution.py:744
  19.8 5.0 %collective-permute-start.10 = (f32[136,128]{1,0:T(8,128)S(1)}, f32[136,128]{1,0:T(8,128)S(1)}, u32[]{:S(2)}, u32[]{:S(2)}) collective-permute-start(f32[136,128]{1,0:T(8,128)S(1)} %get-tuple-element.43), channel_id=1, source_target_pairs={{0,3},{1,2},{2,1},{3,0},{4,7},{5,6},{6,5},{7,4},{8,11},{9,10},{10,... | collective-permute-start | bytes 208904 | tf_op jit(solution)/shard_map/ppermute | solution.py:744

commit v6 on v5

--- a/solution.py
+++ b/solution.py
@@ -802,7 +802,7 @@
             pltpu.SemaphoreType.DMA((len(inputs + kept),)),
         ],
         inputs + kept,
-        4 * 10**9,
+        8 * 10**10,
         len(inputs + kept),
     )
     odd, coherent, hots, share = lax.optimization_barrier((odd, coherent, hots, share))
@@ -813,14 +813,14 @@
         (table, gathered, predictions),
         [model],
         (coherent, hots, own, other),
-        2 * 10**9,
+        4 * 10**10,
     )
     packed, mine = call(
         first_kernel,
         (f32(held, RUN), f32(rows + directions, RUN)),
         scratch,
         (mask, coherent, gram, hots, gather, predicted, *shards),
-        10**9,
+        2 * 10**10,
     )
     sums = from_three(packed, packed, packed)
     to_core, to_blk, to_both, jones = call(
@@ -834,7 +834,7 @@
             scratch[1],
         ],
         (mask, coherent, gram, hots, jones, mine, packed, *sums, *shards),
-        2 * 10**9,
+        4 * 10**10,
     )
     solved = f32(half_directions, 8, station_positions.shape[1])
     return call(
@@ -850,7 +850,7 @@
             mask, share, other_share, last_hots, jones,
             to_core, *from_three(to_core, to_blk, to_both), *shards,
         ),
-        10**9,
+        2 * 10**10,
         0,
         (pltpu.VMEM, pltpu.HBM),
     )

time: 26.4 us -> 26.3 us (level)
  waiting for transfers between devices: 7.21 us -> 6.76 us
  starting transfers between devices: 10.4 us -> 10.7 us
    ppermute x10, waiting for transfers between devices: 7.2 us -> 6.76 us  [swap(): lax.ppermute(x, axis, [(i, i ^ bit) for i in range(lax.axis_size(axis))])]
    ppermute x10, starting transfers between devices: 8.83 us -> 9.16 us  [swap(): lax.ppermute(x, axis, [(i, i ^ bit) for i in range(lax.axis_size(axis))])]
  transfers between devices with their start and end apart: 11 -> 11, of which waited for: 4 -> 5; matrix products, arithmetic and copies ran while one was open for 0% -> 0% of each run, Pallas kernels for 25% -> 21%
where the time goes in v6:
time: 26.3 us; the launch traced here: 26.1 us
  starting transfers between devices  10.7 us (41%)
  Pallas kernels  7.9 us (30%)
  waiting for transfers between devices  6.76 us (26%)
  between operations  0.68 us (3%)
    ppermute x10, starting transfers between devices, swap(): lax.ppermute(x, axis, [(i, i ^ bit) for i in range(lax.axis_size(axis))])  9.16 us
    pallas_call x5, Pallas kernels, call(): pl.pallas_call(kernel, out_shape=out_shape, in_specs=[pl.BlockSpec(memory...  7.9 us
    ppermute x10, waiting for transfers between devices, swap(): lax.ppermute(x, axis, [(i, i ^ bit) for i in range(lax.axis_size(axis))])  6.76 us
    ppermute x1, starting transfers between devices, per_device_owned(): lax.ppermute(visibilities, ('chan', 'dir'), [(2 * chan + core, 2 * (chan...  1.58 us
  transfers between devices with their start and end apart: 11, of which 5 were waited for; matrix products, arithmetic and copies ran while one was open for 0% of the time, Pallas kernels for 21%

profile of v6, /device:TPU:0, one launch (start us, length us, event | category | flops | bytes accessed | tf_op | source)
XLA Modules:
  0.0 26.1 jit_solution(16337715775563318105)
XLA Ops:
  0.6 4.1 %collective-permute-start.3 = (f32[8,2,1,512]{3,2,1,0:T(1,128)}, f32[8,2,1,512]{3,2,1,0:T(1,128)S(1)}, u32[]{:S(2)}, u32[]{:S(2)}) collective-permute-start(f32[8,2,1,512]{3,2,1,0:T(1,128)} %seen_at.1), channel_id=1, source_target_pairs={{0,8},{4,12},{8,0},{12,4},{1,9},{5,13},{9,1},{13,5},{2,10},{6,14},... | collective-permute-start | bytes 98312 | tf_op jit(solution)/shard_map/ppermute | solution.py:744
  4.7 1.6 %collective-permute-start = (f32[8,2,1,512]{3,2,1,0:T(1,128)}, f32[8,2,1,512]{3,2,1,0:T(1,128)S(1)}, u32[]{:S(2)}, u32[]{:S(2)}) collective-permute-start(f32[8,2,1,512]{3,2,1,0:T(1,128)} %seen_at.1), channel_id=1, source_target_pairs={{0,4},{1,13},{4,0},{5,9},{8,12},{9,5},{12,8},{13,1},{2,6},{3,15},{... | collective-permute-start | bytes 98312 | tf_op jit(solution)/shard_map/ppermute | solution.py:770
  6.3 0.0 collective-permute-start.2
  6.3 3.0 %shard_map.95 = (f32[8,192,256]{2,1,0:T(8,128)S(1)}, f32[8,128,128]{2,1,0:T(8,128)S(1)}, f32[128,256]{1,0:T(8,128)S(1)}, bf16[2,256,256]{2,1,0:T(8,128)(2,1)S(1)...) custom-call(s32[2,1,512]{2,1,0:T(1,128)} %pairs_at.1, ...), custom_call_target="tpu_custom_call" | custom-call | flops 80000000000 | bytes 2968576 | tf_op jit(solution)/shard_map/pallas_call | solution.py:718
  9.3 0.0 collective-permute-done.s1
  9.3 0.6 %collective-permute-start.4 = (f32[8,2,1,512]{3,2,1,0:T(1,128)S(1)}, f32[8,2,1,512]{3,2,1,0:T(1,128)S(1)}, u32[]{:S(2)}, u32[]{:S(2)}) collective-permute-start(f32[8,2,1,512]{3,2,1,0:T(1,128)S(1)} %collective-permute-done.s1), channel_id=1, source_target_pairs={{0,1},{1,0},{2,3},{3,2},{4,5},{5,4},{6,7},{7,6},{8,9},{9,8},{10,11... | collective-permute-start | bytes 98312 | tf_op jit(solution)/shard_map/ppermute | solution.py:744
  9.9 0.0 collective-permute-done.2.other
  9.9 0.8 %shard_map.96 = (f32[128,256]{1,0:T(8,128)S(1)}, f32[2,2,128,128]{3,2,1,0:T(8,128)S(1)}, f32[2,8,8,128]{3,2,1,0:T(8,128)S(1)}) custom-call(f32[8,192,256]{2,1,0:T(8,128)S(1)} %get-tuple-element.29.coherent, bf16[2,256,256]{2,1,0:T(8,128)(2,1)S(1)} %get-tuple-element.31.hots, f32[8,8,512]{2,1,0:T(8,128)S(1)} %get-tuple-element.32.own, ...), custom_call_target="tpu_custom_call" | custom-call | flops 40000000000 | bytes 2555904 | tf_op jit(solution)/shard_map/pallas_call | solution.py:718
  10.7 0.0 collective-permute-done.3.s2
  10.7 0.1 collective-permute-done.4.s3
  10.7 1.0 %shard_map.97 = (f32[72,128]{1,0:T(8,128)S(1)}, f32[144,128]{1,0:T(8,128)S(1)}) custom-call(s32[1,512]{1,0:T(1,128)S(1)} %get-tuple-element.23.mask, f32[8,192,256]{2,1,0:T(8,128)S(1)} %get-tuple-element.29.coherent, f32[128,256]{1,0:T(8,128)S(1)} %get-tuple-element.30.gram, bf16[2,256,256]{2,1,0:T(8,128)(2,1)S(1)} %get-tuple-element.31.hots, ...), custom_call_target="tpu_custom_call" | custom-call | flops 20000000000 | bytes 2537472 | tf_op jit(solution)/shard_map/pallas_call | solution.py:718
  11.8 1.5 %collective-permute-start.7 = (f32[72,128]{1,0:T(8,128)S(1)}, f32[72,128]{1,0:T(8,128)S(1)}, u32[]{:S(2)}, u32[]{:S(2)}) collective-permute-start(f32[72,128]{1,0:T(8,128)S(1)} %get-tuple-element.39.p0), channel_id=1, source_target_pairs={{0,3},{1,2},{2,1},{3,0},{4,7},{5,6},{6,5},{7,4},{8,11},{9,10},{10,... | collective-permute-start | bytes 110600 | tf_op jit(solution)/shard_map/ppermute | solution.py:744
  13.3 0.5 %collective-permute-start.6 = (f32[72,128]{1,0:T(8,128)S(1)}, f32[72,128]{1,0:T(8,128)S(1)}, u32[]{:S(2)}, u32[]{:S(2)}) collective-permute-start(f32[72,128]{1,0:T(8,128)S(1)} %get-tuple-element.39.p0), channel_id=1, source_target_pairs={{0,2},{2,0},{1,3},{3,1},{4,6},{6,4},{5,7},{7,5},{8,10},{10,8},{9,1... | collective-permute-start | bytes 110600 | tf_op jit(solution)/shard_map/ppermute | solution.py:744
  13.8 0.0 collective-permute-start.5
  13.8 0.5 %collective-permute-start.1 = (f32[8,128,128]{2,1,0:T(8,128)S(1)}, f32[8,128,128]{2,1,0:T(8,128)S(1)}, u32[]{:S(2)}, u32[]{:S(2)}) collective-permute-start(f32[8,128,128]{2,1,0:T(8,128)S(1)} %get-tuple-element.27.share), channel_id=1, source_target_pairs={{0,1},{1,0},{2,3},{3,2},{4,5},{5,4},{6,7},{7,6},{8,9},{9,8},{10,11... | collective-permute-start | bytes 1572872 | tf_op jit(solution)/shard_map/ppermute | solution.py:744
  14.3 0.9 %collective-permute-done.7.p3 = f32[72,128]{1,0:T(8,128)S(1)} collective-permute-done((f32[72,128]{1,0:T(8,128)S(1)}, f32[72,128]{1,0:T(8,128)S(1)}, u32[]{:S(2)}, u32[]{:S(2)}) %collective-permute-start.7) | collective-permute-done | bytes 36896 | tf_op jit(solution)/shard_map/ppermute | solution.py:744
  15.2 2.0 %collective-permute-done.6.p2 = f32[72,128]{1,0:T(8,128)S(1)} collective-permute-done((f32[72,128]{1,0:T(8,128)S(1)}, f32[72,128]{1,0:T(8,128)S(1)}, u32[]{:S(2)}, u32[]{:S(2)}) %collective-permute-start.6) | collective-permute-done | bytes 36896 | tf_op jit(solution)/shard_map/ppermute | solution.py:744
  17.2 0.0 collective-permute-done.5.p1
  17.2 1.7 %shard_map.98 = (f32[200,128]{1,0:T(8,128)S(1)}, f32[136,128]{1,0:T(8,128)S(1)}, f32[136,128]{1,0:T(8,128)S(1)}, f32[128,256]{1,0:T(8,128)S(1)}) custom-call(s32[1,512]{1,0:T(1,128)S(1)} %get-tuple-element.23.mask, f32[8,192,256]{2,1,0:T(8,128)S(1)} %get-tuple-element.29.coherent, f32[128,256]{1,0:T(8,128)S(1)} %get-tuple-element.30.gram, ...), custom_call_target="tpu_custom_call" | custom-call | flops 40000000000 | bytes 2824192 | tf_op jit(solution)/shard_map/pallas_call | solution.py:718
  19.0 0.1 collective-permute-start.8
  19.1 0.7 %collective-permute-start.9 = (f32[136,128]{1,0:T(8,128)S(1)}, f32[136,128]{1,0:T(8,128)S(1)}, u32[]{:S(2)}, u32[]{:S(2)}) collective-permute-start(f32[136,128]{1,0:T(8,128)S(1)} %get-tuple-element.42), channel_id=1, source_target_pairs={{0,2},{2,0},{1,3},{3,1},{4,6},{6,4},{5,7},{7,5},{8,10},{10,8},{9,1... | collective-permute-start | bytes 208904 | tf_op jit(solution)/shard_map/ppermute | solution.py:744
  19.8 1.1 %collective-permute-start.10 = (f32[136,128]{1,0:T(8,128)S(1)}, f32[136,128]{1,0:T(8,128)S(1)}, u32[]{:S(2)}, u32[]{:S(2)}) collective-permute-start(f32[136,128]{1,0:T(8,128)S(1)} %get-tuple-element.43), channel_id=1, source_target_pairs={{0,3},{1,2},{2,1},{3,0},{4,7},{5,6},{6,5},{7,4},{8,11},{9,10},{10,... | collective-permute-start | bytes 208904 | tf_op jit(solution)/shard_map/ppermute | solution.py:744
  20.9 3.2 %collective-permute-done.9.p2 = f32[136,128]{1,0:T(8,128)S(1)} collective-permute-done((f32[136,128]{1,0:T(8,128)S(1)}, f32[136,128]{1,0:T(8,128)S(1)}, u32[]{:S(2)}, u32[]{:S(2)}) %collective-permute-start.9) | collective-permute-done | bytes 69664 | tf_op jit(solution)/shard_map/ppermute | solution.py:744
  24.1 0.6 %collective-permute-done.10.p3 = f32[136,128]{1,0:T(8,128)S(1)} collective-permute-done((f32[136,128]{1,0:T(8,128)S(1)}, f32[136,128]{1,0:T(8,128)S(1)}, u32[]{:S(2)}, u32[]{:S(2)}) %collective-permute-start.10) | collective-permute-done | bytes 69664 | tf_op jit(solution)/shard_map/ppermute | solution.py:744
  24.7 0.0 collective-permute-done.8.p1
  24.7 0.0 collective-permute-done.1.other_share
  24.7 1.4 %shard_map.99 = (f32[8,8,1,128]{3,2,1,0:T(1,128)}, f32[8,8,512]{2,1,0:T(8,128)}) custom-call(s32[1,512]{1,0:T(1,128)S(1)} %get-tuple-element.23.mask, f32[8,128,128]{2,1,0:T(8,128)S(1)} %get-tuple-element.27.share, f32[8,128,128]{2,1,0:T(8,128)S(1)} %collective-permute-done.1.other_share, bf16[2,256,128]{2,1,0:T(8,128)(2,1)S(1)} %get-tuple-element.28.hots, ...), custom_call_target="tpu_custom_call" | custom-call | flops 20000000000 | bytes 1951744 | tf_op jit(solution)/shard_map/pallas_call | solution.py:718
Async XLA Ops:
  0.6 10.0 %collective-permute-start.3 = (f32[8,2,1,512]{3,2,1,0:T(1,128)}, f32[8,2,1,512]{3,2,1,0:T(1,128)S(1)}, u32[]{:S(2)}, u32[]{:S(2)}) collective-permute-start(f32[8,2,1,512]{3,2,1,0:T(1,128)} %seen_at.1), channel_id=1, source_target_pairs={{0,8},{4,12},{8,0},{12,4},{1,9},{5,13},{9,1},{13,5},{2,10},{6,14},... | collective-permute-start | bytes 98312 | tf_op jit(solution)/shard_map/ppermute | solution.py:744
  4.7 4.6 %collective-permute-start = (f32[8,2,1,512]{3,2,1,0:T(1,128)}, f32[8,2,1,512]{3,2,1,0:T(1,128)S(1)}, u32[]{:S(2)}, u32[]{:S(2)}) collective-permute-start(f32[8,2,1,512]{3,2,1,0:T(1,128)} %seen_at.1), channel_id=1, source_target_pairs={{0,4},{1,13},{4,0},{5,9},{8,12},{9,5},{12,8},{13,1},{2,6},{3,15},{... | collective-permute-start | bytes 98312 | tf_op jit(solution)/shard_map/ppermute | solution.py:770
  6.3 3.6 %collective-permute-start.2 = (f32[8,8,512]{2,1,0:T(8,128)}, f32[8,8,512]{2,1,0:T(8,128)S(1)}, u32[]{:S(2)}, u32[]{:S(2)}) collective-permute-start(f32[8,8,512]{2,1,0:T(8,128)} %own_at.1), channel_id=1, source_target_pairs={{0,1},{1,0},{2,3},{3,2},{4,5},{5,4},{6,7},{7,6},{8,9},{9,8},{10,11... | collective-permute-start | bytes 393224 | tf_op jit(solution)/shard_map/ppermute | solution.py:744
  9.3 1.4 %collective-permute-start.4 = (f32[8,2,1,512]{3,2,1,0:T(1,128)S(1)}, f32[8,2,1,512]{3,2,1,0:T(1,128)S(1)}, u32[]{:S(2)}, u32[]{:S(2)}) collective-permute-start(f32[8,2,1,512]{3,2,1,0:T(1,128)S(1)} %collective-permute-done.s1), channel_id=1, source_target_pairs={{0,1},{1,0},{2,3},{3,2},{4,5},{5,4},{6,7},{7,6},{8,9},{9,8},{10,11... | collective-permute-start | bytes 98312 | tf_op jit(solution)/shard_map/ppermute | solution.py:744
  11.8 3.4 %collective-permute-start.7 = (f32[72,128]{1,0:T(8,128)S(1)}, f32[72,128]{1,0:T(8,128)S(1)}, u32[]{:S(2)}, u32[]{:S(2)}) collective-permute-start(f32[72,128]{1,0:T(8,128)S(1)} %get-tuple-element.39.p0), channel_id=1, source_target_pairs={{0,3},{1,2},{2,1},{3,0},{4,7},{5,6},{6,5},{7,4},{8,11},{9,10},{10,... | collective-permute-start | bytes 110600 | tf_op jit(solution)/shard_map/ppermute | solution.py:744
  13.3 4.0 %collective-permute-start.6 = (f32[72,128]{1,0:T(8,128)S(1)}, f32[72,128]{1,0:T(8,128)S(1)}, u32[]{:S(2)}, u32[]{:S(2)}) collective-permute-start(f32[72,128]{1,0:T(8,128)S(1)} %get-tuple-element.39.p0), channel_id=1, source_target_pairs={{0,2},{2,0},{1,3},{3,1},{4,6},{6,4},{5,7},{7,5},{8,10},{10,8},{9,1... | collective-permute-start | bytes 110600 | tf_op jit(solution)/shard_map/ppermute | solution.py:744
  13.8 3.4 %collective-permute-start.5 = (f32[72,128]{1,0:T(8,128)S(1)}, f32[72,128]{1,0:T(8,128)S(1)}, u32[]{:S(2)}, u32[]{:S(2)}) collective-permute-start(f32[72,128]{1,0:T(8,128)S(1)} %get-tuple-element.39.p0), channel_id=1, source_target_pairs={{0,1},{1,0},{2,3},{3,2},{4,5},{5,4},{6,7},{7,6},{8,9},{9,8},{10,11... | collective-permute-start | bytes 110600 | tf_op jit(solution)/shard_map/ppermute | solution.py:744
  13.8 10.9 %collective-permute-start.1 = (f32[8,128,128]{2,1,0:T(8,128)S(1)}, f32[8,128,128]{2,1,0:T(8,128)S(1)}, u32[]{:S(2)}, u32[]{:S(2)}) collective-permute-start(f32[8,128,128]{2,1,0:T(8,128)S(1)} %get-tuple-element.27.share), channel_id=1, source_target_pairs={{0,1},{1,0},{2,3},{3,2},{4,5},{5,4},{6,7},{7,6},{8,9},{9,8},{10,11... | collective-permute-start | bytes 1572872 | tf_op jit(solution)/shard_map/ppermute | solution.py:744
  19.0 5.7 %collective-permute-start.8 = (f32[200,128]{1,0:T(8,128)S(1)}, f32[200,128]{1,0:T(8,128)S(1)}, u32[]{:S(2)}, u32[]{:S(2)}) collective-permute-start(f32[200,128]{1,0:T(8,128)S(1)} %get-tuple-element.41.p0), channel_id=1, source_target_pairs={{0,1},{1,0},{2,3},{3,2},{4,5},{5,4},{6,7},{7,6},{8,9},{9,8},{10,11... | collective-permute-start | bytes 307208 | tf_op jit(solution)/shard_map/ppermute | solution.py:744
  19.1 5.0 %collective-permute-start.9 = (f32[136,128]{1,0:T(8,128)S(1)}, f32[136,128]{1,0:T(8,128)S(1)}, u32[]{:S(2)}, u32[]{:S(2)}) collective-permute-start(f32[136,128]{1,0:T(8,128)S(1)} %get-tuple-element.42), channel_id=1, source_target_pairs={{0,2},{2,0},{1,3},{3,1},{4,6},{6,4},{5,7},{7,5},{8,10},{10,8},{9,1... | collective-permute-start | bytes 208904 | tf_op jit(solution)/shard_map/ppermute | solution.py:744
  19.8 4.9 %collective-permute-start.10 = (f32[136,128]{1,0:T(8,128)S(1)}, f32[136,128]{1,0:T(8,128)S(1)}, u32[]{:S(2)}, u32[]{:S(2)}) collective-permute-start(f32[136,128]{1,0:T(8,128)S(1)} %get-tuple-element.43), channel_id=1, source_target_pairs={{0,3},{1,2},{2,1},{3,0},{4,7},{5,6},{6,5},{7,4},{8,11},{9,10},{10,... | collective-permute-start | bytes 208904 | tf_op jit(solution)/shard_map/ppermute | solution.py:744

commit v7 on v5

--- a/solution.py
+++ b/solution.py
@@ -369,7 +369,7 @@
     span = there[0] - there[1]
     sources = offsets.shape[1]
     columns = jnp.transpose(jnp.concatenate([offsets[...], jnp.zeros((6, sources))]))
-    step = 16
+    step = 32
     for start in range(0, sources, step):
         rows = slice(start, start + step)
         geometry = columns[rows, 0:1] * span[0:1] + columns[rows, 1:2] * span[1:2]

time: 26.4 us -> 26.4 us (level)
  no operation moved by 1% of the time
where the time goes in v7:
time: 26.4 us; the launch traced here: 26.2 us
  starting transfers between devices  10.4 us (39%)
  Pallas kernels  7.91 us (30%)
  waiting for transfers between devices  7.2 us (27%)
  between operations  0.69 us (3%)
    ppermute x10, starting transfers between devices, swap(): lax.ppermute(x, axis, [(i, i ^ bit) for i in range(lax.axis_size(axis))])  8.82 us
    pallas_call x5, Pallas kernels, call(): pl.pallas_call(kernel, out_shape=out_shape, in_specs=[pl.BlockSpec(memory...  7.91 us
    ppermute x10, waiting for transfers between devices, swap(): lax.ppermute(x, axis, [(i, i ^ bit) for i in range(lax.axis_size(axis))])  7.2 us
    ppermute x1, starting transfers between devices, per_device_owned(): lax.ppermute(visibilities, ('chan', 'dir'), [(2 * chan + core, 2 * (chan...  1.58 us
  transfers between devices with their start and end apart: 11, of which 4 were waited for; matrix products, arithmetic and copies ran while one was open for 0% of the time, Pallas kernels for 25%

profile of v7, /device:TPU:0, one launch (start us, length us, event | category | flops | bytes accessed | tf_op | source)
XLA Modules:
  0.0 26.2 jit_solution(18441706208953514115)
XLA Ops:
  0.6 4.1 %collective-permute-start.3 = (f32[8,2,1,512]{3,2,1,0:T(1,128)}, f32[8,2,1,512]{3,2,1,0:T(1,128)S(1)}, u32[]{:S(2)}, u32[]{:S(2)}) collective-permute-start(f32[8,2,1,512]{3,2,1,0:T(1,128)} %seen_at.1), channel_id=1, source_target_pairs={{0,8},{4,12},{8,0},{12,4},{1,9},{5,13},{9,1},{13,5},{2,10},{6,14},... | collective-permute-start | bytes 98312 | tf_op jit(solution)/shard_map/ppermute | solution.py:744
  4.7 1.6 %collective-permute-start = (f32[8,2,1,512]{3,2,1,0:T(1,128)}, f32[8,2,1,512]{3,2,1,0:T(1,128)S(1)}, u32[]{:S(2)}, u32[]{:S(2)}) collective-permute-start(f32[8,2,1,512]{3,2,1,0:T(1,128)} %seen_at.1), channel_id=1, source_target_pairs={{0,4},{1,13},{4,0},{5,9},{8,12},{9,5},{12,8},{13,1},{2,6},{3,15},{... | collective-permute-start | bytes 98312 | tf_op jit(solution)/shard_map/ppermute | solution.py:770
  6.3 0.0 collective-permute-start.2
  6.3 3.0 %shard_map.95 = (f32[8,192,256]{2,1,0:T(8,128)S(1)}, f32[8,128,128]{2,1,0:T(8,128)S(1)}, f32[128,256]{1,0:T(8,128)S(1)}, bf16[2,256,256]{2,1,0:T(8,128)(2,1)S(1)...) custom-call(s32[2,1,512]{2,1,0:T(1,128)} %pairs_at.1, ...), custom_call_target="tpu_custom_call" | custom-call | flops 4000000000 | bytes 2968576 | tf_op jit(solution)/shard_map/pallas_call | solution.py:718
  9.3 0.0 collective-permute-done.s1
  9.3 0.6 %collective-permute-start.4 = (f32[8,2,1,512]{3,2,1,0:T(1,128)S(1)}, f32[8,2,1,512]{3,2,1,0:T(1,128)S(1)}, u32[]{:S(2)}, u32[]{:S(2)}) collective-permute-start(f32[8,2,1,512]{3,2,1,0:T(1,128)S(1)} %collective-permute-done.s1), channel_id=1, source_target_pairs={{0,1},{1,0},{2,3},{3,2},{4,5},{5,4},{6,7},{7,6},{8,9},{9,8},{10,11... | collective-permute-start | bytes 98312 | tf_op jit(solution)/shard_map/ppermute | solution.py:744
  9.9 0.1 collective-permute-start.1
  10.0 0.0 collective-permute-done.2.other
  10.0 0.8 %shard_map.96 = (f32[128,256]{1,0:T(8,128)S(1)}, f32[2,2,128,128]{3,2,1,0:T(8,128)S(1)}, f32[2,8,8,128]{3,2,1,0:T(8,128)S(1)}) custom-call(f32[8,192,256]{2,1,0:T(8,128)S(1)} %get-tuple-element.29.coherent, bf16[2,256,256]{2,1,0:T(8,128)(2,1)S(1)} %get-tuple-element.31.hots, f32[8,8,512]{2,1,0:T(8,128)S(1)} %get-tuple-element.32.own, ...), custom_call_target="tpu_custom_call" | custom-call | flops 2000000000 | bytes 2555904 | tf_op jit(solution)/shard_map/pallas_call | solution.py:718
  10.8 0.0 collective-permute-done.3.s2
  10.8 0.0 collective-permute-done.4.s3
  10.8 1.0 %shard_map.97 = (f32[72,128]{1,0:T(8,128)S(1)}, f32[144,128]{1,0:T(8,128)S(1)}) custom-call(s32[1,512]{1,0:T(1,128)S(1)} %get-tuple-element.23.mask, f32[8,192,256]{2,1,0:T(8,128)S(1)} %get-tuple-element.29.coherent, f32[128,256]{1,0:T(8,128)S(1)} %get-tuple-element.30.gram, bf16[2,256,256]{2,1,0:T(8,128)(2,1)S(1)} %get-tuple-element.31.hots, ...), custom_call_target="tpu_custom_call" | custom-call | flops 1000000000 | bytes 2537472 | tf_op jit(solution)/shard_map/pallas_call | solution.py:718
  11.8 1.6 %collective-permute-start.7 = (f32[72,128]{1,0:T(8,128)S(1)}, f32[72,128]{1,0:T(8,128)S(1)}, u32[]{:S(2)}, u32[]{:S(2)}) collective-permute-start(f32[72,128]{1,0:T(8,128)S(1)} %get-tuple-element.39.p0), channel_id=1, source_target_pairs={{0,3},{1,2},{2,1},{3,0},{4,7},{5,6},{6,5},{7,4},{8,11},{9,10},{10,... | collective-permute-start | bytes 110600 | tf_op jit(solution)/shard_map/ppermute | solution.py:744
  13.4 0.5 %collective-permute-start.6 = (f32[72,128]{1,0:T(8,128)S(1)}, f32[72,128]{1,0:T(8,128)S(1)}, u32[]{:S(2)}, u32[]{:S(2)}) collective-permute-start(f32[72,128]{1,0:T(8,128)S(1)} %get-tuple-element.39.p0), channel_id=1, source_target_pairs={{0,2},{2,0},{1,3},{3,1},{4,6},{6,4},{5,7},{7,5},{8,10},{10,8},{9,1... | collective-permute-start | bytes 110600 | tf_op jit(solution)/shard_map/ppermute | solution.py:744
  13.9 0.0 collective-permute-start.5
  13.9 1.3 %collective-permute-done.7.p3 = f32[72,128]{1,0:T(8,128)S(1)} collective-permute-done((f32[72,128]{1,0:T(8,128)S(1)}, f32[72,128]{1,0:T(8,128)S(1)}, u32[]{:S(2)}, u32[]{:S(2)}) %collective-permute-start.7) | collective-permute-done | bytes 36896 | tf_op jit(solution)/shard_map/ppermute | solution.py:744
  15.3 2.1 %collective-permute-done.6.p2 = f32[72,128]{1,0:T(8,128)S(1)} collective-permute-done((f32[72,128]{1,0:T(8,128)S(1)}, f32[72,128]{1,0:T(8,128)S(1)}, u32[]{:S(2)}, u32[]{:S(2)}) %collective-permute-start.6) | collective-permute-done | bytes 36896 | tf_op jit(solution)/shard_map/ppermute | solution.py:744
  17.4 0.0 collective-permute-done.5.p1
  17.4 1.7 %shard_map.98 = (f32[200,128]{1,0:T(8,128)S(1)}, f32[136,128]{1,0:T(8,128)S(1)}, f32[136,128]{1,0:T(8,128)S(1)}, f32[128,256]{1,0:T(8,128)S(1)}) custom-call(s32[1,512]{1,0:T(1,128)S(1)} %get-tuple-element.23.mask, f32[8,192,256]{2,1,0:T(8,128)S(1)} %get-tuple-element.29.coherent, f32[128,256]{1,0:T(8,128)S(1)} %get-tuple-element.30.gram, ...), custom_call_target="tpu_custom_call" | custom-call | flops 2000000000 | bytes 2824192 | tf_op jit(solution)/shard_map/pallas_call | solution.py:718
  19.1 0.1 collective-permute-start.8
  19.2 0.6 %collective-permute-start.9 = (f32[136,128]{1,0:T(8,128)S(1)}, f32[136,128]{1,0:T(8,128)S(1)}, u32[]{:S(2)}, u32[]{:S(2)}) collective-permute-start(f32[136,128]{1,0:T(8,128)S(1)} %get-tuple-element.42), channel_id=1, source_target_pairs={{0,2},{2,0},{1,3},{3,1},{4,6},{6,4},{5,7},{7,5},{8,10},{10,8},{9,1... | collective-permute-start | bytes 208904 | tf_op jit(solution)/shard_map/ppermute | solution.py:744
  19.8 1.2 %collective-permute-start.10 = (f32[136,128]{1,0:T(8,128)S(1)}, f32[136,128]{1,0:T(8,128)S(1)}, u32[]{:S(2)}, u32[]{:S(2)}) collective-permute-start(f32[136,128]{1,0:T(8,128)S(1)} %get-tuple-element.43), channel_id=1, source_target_pairs={{0,3},{1,2},{2,1},{3,0},{4,7},{5,6},{6,5},{7,4},{8,11},{9,10},{10,... | collective-permute-start | bytes 208904 | tf_op jit(solution)/shard_map/ppermute | solution.py:744
  21.1 3.2 %collective-permute-done.9.p2 = f32[136,128]{1,0:T(8,128)S(1)} collective-permute-done((f32[136,128]{1,0:T(8,128)S(1)}, f32[136,128]{1,0:T(8,128)S(1)}, u32[]{:S(2)}, u32[]{:S(2)}) %collective-permute-start.9) | collective-permute-done | bytes 69664 | tf_op jit(solution)/shard_map/ppermute | solution.py:744
  24.2 0.6 %collective-permute-done.10.p3 = f32[136,128]{1,0:T(8,128)S(1)} collective-permute-done((f32[136,128]{1,0:T(8,128)S(1)}, f32[136,128]{1,0:T(8,128)S(1)}, u32[]{:S(2)}, u32[]{:S(2)}) %collective-permute-start.10) | collective-permute-done | bytes 69664 | tf_op jit(solution)/shard_map/ppermute | solution.py:744
  24.8 0.0 collective-permute-done.8.p1
  24.8 0.0 collective-permute-done.1.other_share
  24.8 1.4 %shard_map.99 = (f32[8,8,1,128]{3,2,1,0:T(1,128)}, f32[8,8,512]{2,1,0:T(8,128)}) custom-call(s32[1,512]{1,0:T(1,128)S(1)} %get-tuple-element.23.mask, f32[8,128,128]{2,1,0:T(8,128)S(1)} %get-tuple-element.27.share, f32[8,128,128]{2,1,0:T(8,128)S(1)} %collective-permute-done.1.other_share, bf16[2,256,128]{2,1,0:T(8,128)(2,1)S(1)} %get-tuple-element.28.hots, ...), custom_call_target="tpu_custom_call" | custom-call | flops 1000000000 | bytes 1951744 | tf_op jit(solution)/shard_map/pallas_call | solution.py:718
Async XLA Ops:
  0.6 10.1 %collective-permute-start.3 = (f32[8,2,1,512]{3,2,1,0:T(1,128)}, f32[8,2,1,512]{3,2,1,0:T(1,128)S(1)}, u32[]{:S(2)}, u32[]{:S(2)}) collective-permute-start(f32[8,2,1,512]{3,2,1,0:T(1,128)} %seen_at.1), channel_id=1, source_target_pairs={{0,8},{4,12},{8,0},{12,4},{1,9},{5,13},{9,1},{13,5},{2,10},{6,14},... | collective-permute-start | bytes 98312 | tf_op jit(solution)/shard_map/ppermute | solution.py:744
  4.7 4.6 %collective-permute-start = (f32[8,2,1,512]{3,2,1,0:T(1,128)}, f32[8,2,1,512]{3,2,1,0:T(1,128)S(1)}, u32[]{:S(2)}, u32[]{:S(2)}) collective-permute-start(f32[8,2,1,512]{3,2,1,0:T(1,128)} %seen_at.1), channel_id=1, source_target_pairs={{0,4},{1,13},{4,0},{5,9},{8,12},{9,5},{12,8},{13,1},{2,6},{3,15},{... | collective-permute-start | bytes 98312 | tf_op jit(solution)/shard_map/ppermute | solution.py:770
  6.3 3.7 %collective-permute-start.2 = (f32[8,8,512]{2,1,0:T(8,128)}, f32[8,8,512]{2,1,0:T(8,128)S(1)}, u32[]{:S(2)}, u32[]{:S(2)}) collective-permute-start(f32[8,8,512]{2,1,0:T(8,128)} %own_at.1), channel_id=1, source_target_pairs={{0,1},{1,0},{2,3},{3,2},{4,5},{5,4},{6,7},{7,6},{8,9},{9,8},{10,11... | collective-permute-start | bytes 393224 | tf_op jit(solution)/shard_map/ppermute | solution.py:744
  9.3 1.5 %collective-permute-start.4 = (f32[8,2,1,512]{3,2,1,0:T(1,128)S(1)}, f32[8,2,1,512]{3,2,1,0:T(1,128)S(1)}, u32[]{:S(2)}, u32[]{:S(2)}) collective-permute-start(f32[8,2,1,512]{3,2,1,0:T(1,128)S(1)} %collective-permute-done.s1), channel_id=1, source_target_pairs={{0,1},{1,0},{2,3},{3,2},{4,5},{5,4},{6,7},{7,6},{8,9},{9,8},{10,11... | collective-permute-start | bytes 98312 | tf_op jit(solution)/shard_map/ppermute | solution.py:744
  9.9 14.9 %collective-permute-start.1 = (f32[8,128,128]{2,1,0:T(8,128)S(1)}, f32[8,128,128]{2,1,0:T(8,128)S(1)}, u32[]{:S(2)}, u32[]{:S(2)}) collective-permute-start(f32[8,128,128]{2,1,0:T(8,128)S(1)} %get-tuple-element.27.share), channel_id=1, source_target_pairs={{0,1},{1,0},{2,3},{3,2},{4,5},{5,4},{6,7},{7,6},{8,9},{9,8},{10,11... | collective-permute-start | bytes 1572872 | tf_op jit(solution)/shard_map/ppermute | solution.py:744
  11.8 3.4 %collective-permute-start.7 = (f32[72,128]{1,0:T(8,128)S(1)}, f32[72,128]{1,0:T(8,128)S(1)}, u32[]{:S(2)}, u32[]{:S(2)}) collective-permute-start(f32[72,128]{1,0:T(8,128)S(1)} %get-tuple-element.39.p0), channel_id=1, source_target_pairs={{0,3},{1,2},{2,1},{3,0},{4,7},{5,6},{6,5},{7,4},{8,11},{9,10},{10,... | collective-permute-start | bytes 110600 | tf_op jit(solution)/shard_map/ppermute | solution.py:744
  13.4 4.0 %collective-permute-start.6 = (f32[72,128]{1,0:T(8,128)S(1)}, f32[72,128]{1,0:T(8,128)S(1)}, u32[]{:S(2)}, u32[]{:S(2)}) collective-permute-start(f32[72,128]{1,0:T(8,128)S(1)} %get-tuple-element.39.p0), channel_id=1, source_target_pairs={{0,2},{2,0},{1,3},{3,1},{4,6},{6,4},{5,7},{7,5},{8,10},{10,8},{9,1... | collective-permute-start | bytes 110600 | tf_op jit(solution)/shard_map/ppermute | solution.py:744
  13.9 3.4 %collective-permute-start.5 = (f32[72,128]{1,0:T(8,128)S(1)}, f32[72,128]{1,0:T(8,128)S(1)}, u32[]{:S(2)}, u32[]{:S(2)}) collective-permute-start(f32[72,128]{1,0:T(8,128)S(1)} %get-tuple-element.39.p0), channel_id=1, source_target_pairs={{0,1},{1,0},{2,3},{3,2},{4,5},{5,4},{6,7},{7,6},{8,9},{9,8},{10,11... | collective-permute-start | bytes 110600 | tf_op jit(solution)/shard_map/ppermute | solution.py:744
  19.1 5.7 %collective-permute-start.8 = (f32[200,128]{1,0:T(8,128)S(1)}, f32[200,128]{1,0:T(8,128)S(1)}, u32[]{:S(2)}, u32[]{:S(2)}) collective-permute-start(f32[200,128]{1,0:T(8,128)S(1)} %get-tuple-element.41.p0), channel_id=1, source_target_pairs={{0,1},{1,0},{2,3},{3,2},{4,5},{5,4},{6,7},{7,6},{8,9},{9,8},{10,11... | collective-permute-start | bytes 307208 | tf_op jit(solution)/shard_map/ppermute | solution.py:744
  19.2 5.0 %collective-permute-start.9 = (f32[136,128]{1,0:T(8,128)S(1)}, f32[136,128]{1,0:T(8,128)S(1)}, u32[]{:S(2)}, u32[]{:S(2)}) collective-permute-start(f32[136,128]{1,0:T(8,128)S(1)} %get-tuple-element.42), channel_id=1, source_target_pairs={{0,2},{2,0},{1,3},{3,1},{4,6},{6,4},{5,7},{7,5},{8,10},{10,8},{9,1... | collective-permute-start | bytes 208904 | tf_op jit(solution)/shard_map/ppermute | solution.py:744
  19.8 5.0 %collective-permute-start.10 = (f32[136,128]{1,0:T(8,128)S(1)}, f32[136,128]{1,0:T(8,128)S(1)}, u32[]{:S(2)}, u32[]{:S(2)}) collective-permute-start(f32[136,128]{1,0:T(8,128)S(1)} %get-tuple-element.43), channel_id=1, source_target_pairs={{0,3},{1,2},{2,1},{3,0},{4,7},{5,6},{6,5},{7,4},{8,11},{9,10},{10,... | collective-permute-start | bytes 208904 | tf_op jit(solution)/shard_map/ppermute | solution.py:744
